TPU v7x, 256 devices: a whole 4x4x8 slice. The times are simulated.
256 devices in a mesh: grp: 8 (over y, core), dev: 32 (over z, x).
Axes of the slice: x: 4, y: 4, z: 8, core: 2. Of those that a mesh axis runs over, the one named last changes fastest.
Arguments:
- blocks: bfloat16 [8, 32, 12, 64, 1728], P('grp', 'dev'), may hold values from -0.75 to 0.75
- prolong: bfloat16 [8, 32, 12, 64, 256], P('grp', 'dev'), may hold values from -0.75 to 0.75
- block_cols: int32 [8, 32, 12, 27], P('grp', 'dev'), may hold values from -1 to 95, as said below
- fetch_rows: int32 [8, 32, 32, 3], P('grp', 'dev'), may hold values from 0 to 11
- tile_slot: int32 [8, 32, 12, 27], P('grp', 'dev'), may hold values from 0 to 15
- tile_owner: int32 [8, 32, 16], P('grp', 'dev'), may hold values from 0 to 255, as said below
- tile_place: int32 [8, 32, 16], P('grp', 'dev'), may hold values from 0 to 1
Outputs:
- coarse: float32 [8, 32, 2, 256, 256], P('grp', 'dev')
Inputs may be any that keep to these rules, and one draw needn't show every extreme that they name: `block_cols`: -1 marks a padded block slot; at most 243 slots of one device are not padding, exactly 243 on the first device. `tile_owner`: the 16 tiles of one device go to owners of distinct dev indices; at most 4 of them go to owners in one group, exactly 4 to the device's own group.
All inputs are finite; a program needn't handle non-finite values.
Results may differ from a plain program's by a relative error of at most 0.004.
Values may be sent and summed in bfloat16 or wider, within the bound.
No kernel may reach another device: no remote copies, remote signals or barrier semaphores. Data moves between devices by JAX's collectives and lax.ppermute only.
A program may use at most 128 MiB of HBM per device.

v0:
```python
import jax
import jax.numpy as jnp
from jax import lax
from jax.sharding import PartitionSpec as P

BLOCK = 64
W = 256
K = 27
CT = 2
NCAP = 3


def body(blocks, prolong, block_cols, fetch_rows, tile_slot, tile_owner, tile_place):
    dev_count = lax.axis_size("dev")
    grp_count = lax.axis_size("grp")
    panels = prolong[0, 0]
    chosen = fetch_rows[0, 0]
    outgoing = panels[chosen]
    arrived = lax.all_to_all(outgoing, "dev", split_axis=0, concat_axis=0, tiled=True)
    arrived = arrived.reshape(dev_count * NCAP, BLOCK, W)
    owners = tile_owner[0, 0]
    places = tile_place[0, 0]
    local_count = owners.shape[0]
    tile_range = jnp.arange(local_count, dtype=jnp.int32)

    def one_row(running, item):
        block_row, panel_row, column_ids, slot_ids = item
        matrix = block_row.reshape(BLOCK, K, BLOCK)
        near_panels = arrived[jnp.maximum(column_ids, 0)]
        product = jnp.einsum(
            "rkc,kcw->krw", matrix, near_panels, preferred_element_type=jnp.float32
        )
        product = jnp.where((column_ids >= 0)[:, None, None], product, 0.0).astype(jnp.bfloat16)
        outer_tile = jnp.einsum(
            "ra,krb->kab", panel_row, product, preferred_element_type=jnp.float32
        )
        selector = (slot_ids[:, None] == tile_range[None, :]).astype(jnp.float32)
        added = jnp.einsum("kt,kab->tab", selector, outer_tile, precision=lax.Precision.HIGHEST)
        return (running + added, None)

    running = jnp.zeros((local_count, W, W), jnp.float32)
    running, unused = lax.scan(
        one_row, running, (blocks[0, 0], panels, block_cols[0, 0], tile_slot[0, 0])
    )
    partial_value = running.astype(jnp.bfloat16)
    dev_target = owners % dev_count
    grp_target = owners // dev_count
    sending = jnp.zeros((dev_count, W, W), jnp.bfloat16).at[dev_target].set(partial_value)
    labels = jnp.full((dev_count,), -1, jnp.int32).at[dev_target].set(grp_target * CT + places)
    got_tiles, got_labels = (
        lax.all_to_all(sending, "dev", split_axis=0, concat_axis=0, tiled=True),
        lax.all_to_all(labels, "dev", split_axis=0, concat_axis=0, tiled=True),
    )
    spread = grp_count * CT
    keyed = jnp.where(got_labels >= 0, got_labels, spread)
    table = (
        jnp.zeros((spread, W, W), jnp.float32)
        .at[keyed]
        .add(got_tiles.astype(jnp.float32), mode="drop")
    )
    result = lax.psum_scatter(table, "grp", scatter_dimension=0, tiled=True)
    return result.reshape(1, 1, CT, W, W)


def solution(mesh):
    return jax.shard_map(
        body,
        mesh=mesh,
        in_specs=(
            P("grp", "dev", None, None, None),
            P("grp", "dev", None, None, None),
            P("grp", "dev", None, None),
            P("grp", "dev", None, None),
            P("grp", "dev", None, None),
            P("grp", "dev", None),
            P("grp", "dev", None),
        ),
        out_specs=P("grp", "dev", None, None, None),
        check_vma=False,
    )
```

profile of v0, /device:TPU:4, one launch (start us, length us, event | category | flops | bytes accessed | tf_op | source)
XLA Modules:
  0.0 666.7 jit_solution(12411617590211893207)
XLA Ops:
  11.0 11.7 %all-to-all-start.1 = ((bf16[32,3,64,256]{3,2,1,0:T(8,128)(2,1)}), bf16[32,3,64,256]{3,2,1,0:T(8,128)(2,1)S(1)}, u32[]{:S(2)}, u32[]{:S(2)}) async-start(bf16[32,3,64,256]{3,2,1,0:T(8,128)(2,1)} %bitcast.68), calls=%async_computation.1 | async-start | bytes 6291456 | tf_op jit(solution)/shard_map/all_to_all | solution.py:19
  24.1 69.6 %all-to-all-done.1 = bf16[32,3,64,256]{3,2,1,0:T(8,128)(2,1)S(1)} async-done(((bf16[32,3,64,256]{3,2,1,0:T(8,128)(2,1)}), bf16[32,3,64,256]{3,2,1,0:T(8,128)(2,1)S(1)}, u32[]{:S(2)}, u32[]{:S(2)}) %all-to-all-start.1) | async-done | bytes 3145760 | tf_op jit(solution)/shard_map/all_to_all | solution.py:19
  93.8 7.5 %all-to-all-start = ((s32[32,1,1]{2,1,0:T(1,128)}), s32[32,1,1]{2,1,0:T(1,128)S(1)}, u32[]{:S(2)}, u32[]{:S(2)}) async-start(s32[32,1,1]{2,1,0:T(1,128)} %copy.19), calls=%async_computation | async-start | bytes 32768 | tf_op jit(solution)/shard_map/all_to_all | solution.py:52
  101.3 377.6 %while.11 = (s32[]{:T(128)}, f32[16,256,256]{2,0,1:T(8,128)}, s32[12,27]{1,0:T(8,128)S(1)}, s32[12,27]{1,0:T(8,128)S(1)}, bf16[12,64,1728]{2,1,0:T(8,128)(2,1)},...) while((s32[]{:T(128)}, f32[16,256,256]{2,0,1:T(8,128)}, ...), condition=%wide.region_2.3_spmd.clone, body=%wide.region_1.2_spmd.clone.sunk | while | flops 625837568 | bytes 65664576 | solution.py:42
  112.5 10.3 %copy.34 = f32[27,256,256]{2,0,1:T(8,128)} copy(f32[27,256,256]{1,2,0:T(8,128)} %convolution_bitcast_fusion.2) | data formatting | bytes 14155776 | tf_op jit(solution)/shard_map/while/body/eval_jaxpr/ra,krb->kab/transpose | solution.py:34
  122.9 8.8 %select_add_fusion.2 = f32[16,256,256]{2,0,1:T(8,128)} fusion(f32[16,256,256]{2,0,1:T(8,128)} %get-tuple-element.149, f32[27,256,256]{2,0,1:T(8,128)} %copy.34, pred[]{:T(512)S(6)} %compare.12, s32[27]{0:T(128)S(1)} %get-tuple-element.138), kind=kOutput, calls=%fused_computation.6.clone.1 | convolution fusion | flops 341836224 | bytes 15466605 | tf_op jit(solution)/shard_map/while/body/eval_jaxpr/kt,kab->tab/dot_general | solution.py:38
  142.9 10.3 %copy.34 = f32[27,256,256]{2,0,1:T(8,128)} copy(f32[27,256,256]{1,2,0:T(8,128)} %convolution_bitcast_fusion.2) | data formatting | bytes 14155776 | tf_op jit(solution)/shard_map/while/body/eval_jaxpr/ra,krb->kab/transpose | solution.py:34
  153.2 10.0 %select_add_fusion.2 = f32[16,256,256]{2,0,1:T(8,128)} fusion(f32[16,256,256]{2,0,1:T(8,128)} %get-tuple-element.149, f32[27,256,256]{2,0,1:T(8,128)} %copy.34, pred[]{:T(512)S(6)} %compare.12, s32[27]{0:T(128)S(1)} %get-tuple-element.138), kind=kOutput, calls=%fused_computation.6.clone.1 | convolution fusion | flops 341836224 | bytes 15466605 | tf_op jit(solution)/shard_map/while/body/eval_jaxpr/kt,kab->tab/dot_general | solution.py:38
  174.5 10.3 %copy.34 = f32[27,256,256]{2,0,1:T(8,128)} copy(f32[27,256,256]{1,2,0:T(8,128)} %convolution_bitcast_fusion.2) | data formatting | bytes 14155776 | tf_op jit(solution)/shard_map/while/body/eval_jaxpr/ra,krb->kab/transpose | solution.py:34
  184.8 10.0 %select_add_fusion.2 = f32[16,256,256]{2,0,1:T(8,128)} fusion(f32[16,256,256]{2,0,1:T(8,128)} %get-tuple-element.149, f32[27,256,256]{2,0,1:T(8,128)} %copy.34, pred[]{:T(512)S(6)} %compare.12, s32[27]{0:T(128)S(1)} %get-tuple-element.138), kind=kOutput, calls=%fused_computation.6.clone.1 | convolution fusion | flops 341836224 | bytes 15466605 | tf_op jit(solution)/shard_map/while/body/eval_jaxpr/kt,kab->tab/dot_general | solution.py:38
  206.0 10.3 %copy.34 = f32[27,256,256]{2,0,1:T(8,128)} copy(f32[27,256,256]{1,2,0:T(8,128)} %convolution_bitcast_fusion.2) | data formatting | bytes 14155776 | tf_op jit(solution)/shard_map/while/body/eval_jaxpr/ra,krb->kab/transpose | solution.py:34
  216.4 10.0 %select_add_fusion.2 = f32[16,256,256]{2,0,1:T(8,128)} fusion(f32[16,256,256]{2,0,1:T(8,128)} %get-tuple-element.149, f32[27,256,256]{2,0,1:T(8,128)} %copy.34, pred[]{:T(512)S(6)} %compare.12, s32[27]{0:T(128)S(1)} %get-tuple-element.138), kind=kOutput, calls=%fused_computation.6.clone.1 | convolution fusion | flops 341836224 | bytes 15466605 | tf_op jit(solution)/shard_map/while/body/eval_jaxpr/kt,kab->tab/dot_general | solution.py:38
  237.6 10.3 %copy.34 = f32[27,256,256]{2,0,1:T(8,128)} copy(f32[27,256,256]{1,2,0:T(8,128)} %convolution_bitcast_fusion.2) | data formatting | bytes 14155776 | tf_op jit(solution)/shard_map/while/body/eval_jaxpr/ra,krb->kab/transpose | solution.py:34
  247.9 10.0 %select_add_fusion.2 = f32[16,256,256]{2,0,1:T(8,128)} fusion(f32[16,256,256]{2,0,1:T(8,128)} %get-tuple-element.149, f32[27,256,256]{2,0,1:T(8,128)} %copy.34, pred[]{:T(512)S(6)} %compare.12, s32[27]{0:T(128)S(1)} %get-tuple-element.138), kind=kOutput, calls=%fused_computation.6.clone.1 | convolution fusion | flops 341836224 | bytes 15466605 | tf_op jit(solution)/shard_map/while/body/eval_jaxpr/kt,kab->tab/dot_general | solution.py:38
  269.2 10.3 %copy.34 = f32[27,256,256]{2,0,1:T(8,128)} copy(f32[27,256,256]{1,2,0:T(8,128)} %convolution_bitcast_fusion.2) | data formatting | bytes 14155776 | tf_op jit(solution)/shard_map/while/body/eval_jaxpr/ra,krb->kab/transpose | solution.py:34
  279.5 10.0 %select_add_fusion.2 = f32[16,256,256]{2,0,1:T(8,128)} fusion(f32[16,256,256]{2,0,1:T(8,128)} %get-tuple-element.149, f32[27,256,256]{2,0,1:T(8,128)} %copy.34, pred[]{:T(512)S(6)} %compare.12, s32[27]{0:T(128)S(1)} %get-tuple-element.138), kind=kOutput, calls=%fused_computation.6.clone.1 | convolution fusion | flops 341836224 | bytes 15466605 | tf_op jit(solution)/shard_map/while/body/eval_jaxpr/kt,kab->tab/dot_general | solution.py:38
  300.7 10.3 %copy.34 = f32[27,256,256]{2,0,1:T(8,128)} copy(f32[27,256,256]{1,2,0:T(8,128)} %convolution_bitcast_fusion.2) | data formatting | bytes 14155776 | tf_op jit(solution)/shard_map/while/body/eval_jaxpr/ra,krb->kab/transpose | solution.py:34
  311.0 10.0 %select_add_fusion.2 = f32[16,256,256]{2,0,1:T(8,128)} fusion(f32[16,256,256]{2,0,1:T(8,128)} %get-tuple-element.149, f32[27,256,256]{2,0,1:T(8,128)} %copy.34, pred[]{:T(512)S(6)} %compare.12, s32[27]{0:T(128)S(1)} %get-tuple-element.138), kind=kOutput, calls=%fused_computation.6.clone.1 | convolution fusion | flops 341836224 | bytes 15466605 | tf_op jit(solution)/shard_map/while/body/eval_jaxpr/kt,kab->tab/dot_general | solution.py:38
  332.3 10.3 %copy.34 = f32[27,256,256]{2,0,1:T(8,128)} copy(f32[27,256,256]{1,2,0:T(8,128)} %convolution_bitcast_fusion.2) | data formatting | bytes 14155776 | tf_op jit(solution)/shard_map/while/body/eval_jaxpr/ra,krb->kab/transpose | solution.py:34
  342.6 10.0 %select_add_fusion.2 = f32[16,256,256]{2,0,1:T(8,128)} fusion(f32[16,256,256]{2,0,1:T(8,128)} %get-tuple-element.149, f32[27,256,256]{2,0,1:T(8,128)} %copy.34, pred[]{:T(512)S(6)} %compare.12, s32[27]{0:T(128)S(1)} %get-tuple-element.138), kind=kOutput, calls=%fused_computation.6.clone.1 | convolution fusion | flops 341836224 | bytes 15466605 | tf_op jit(solution)/shard_map/while/body/eval_jaxpr/kt,kab->tab/dot_general | solution.py:38
  363.9 10.3 %copy.34 = f32[27,256,256]{2,0,1:T(8,128)} copy(f32[27,256,256]{1,2,0:T(8,128)} %convolution_bitcast_fusion.2) | data formatting | bytes 14155776 | tf_op jit(solution)/shard_map/while/body/eval_jaxpr/ra,krb->kab/transpose | solution.py:34
  374.2 10.0 %select_add_fusion.2 = f32[16,256,256]{2,0,1:T(8,128)} fusion(f32[16,256,256]{2,0,1:T(8,128)} %get-tuple-element.149, f32[27,256,256]{2,0,1:T(8,128)} %copy.34, pred[]{:T(512)S(6)} %compare.12, s32[27]{0:T(128)S(1)} %get-tuple-element.138), kind=kOutput, calls=%fused_computation.6.clone.1 | convolution fusion | flops 341836224 | bytes 15466605 | tf_op jit(solution)/shard_map/while/body/eval_jaxpr/kt,kab->tab/dot_general | solution.py:38
  395.4 10.3 %copy.34 = f32[27,256,256]{2,0,1:T(8,128)} copy(f32[27,256,256]{1,2,0:T(8,128)} %convolution_bitcast_fusion.2) | data formatting | bytes 14155776 | tf_op jit(solution)/shard_map/while/body/eval_jaxpr/ra,krb->kab/transpose | solution.py:34
  405.7 10.0 %select_add_fusion.2 = f32[16,256,256]{2,0,1:T(8,128)} fusion(f32[16,256,256]{2,0,1:T(8,128)} %get-tuple-element.149, f32[27,256,256]{2,0,1:T(8,128)} %copy.34, pred[]{:T(512)S(6)} %compare.12, s32[27]{0:T(128)S(1)} %get-tuple-element.138), kind=kOutput, calls=%fused_computation.6.clone.1 | convolution fusion | flops 341836224 | bytes 15466605 | tf_op jit(solution)/shard_map/while/body/eval_jaxpr/kt,kab->tab/dot_general | solution.py:38
  427.0 10.3 %copy.34 = f32[27,256,256]{2,0,1:T(8,128)} copy(f32[27,256,256]{1,2,0:T(8,128)} %convolution_bitcast_fusion.2) | data formatting | bytes 14155776 | tf_op jit(solution)/shard_map/while/body/eval_jaxpr/ra,krb->kab/transpose | solution.py:34
  437.3 10.0 %select_add_fusion.2 = f32[16,256,256]{2,0,1:T(8,128)} fusion(f32[16,256,256]{2,0,1:T(8,128)} %get-tuple-element.149, f32[27,256,256]{2,0,1:T(8,128)} %copy.34, pred[]{:T(512)S(6)} %compare.12, s32[27]{0:T(128)S(1)} %get-tuple-element.138), kind=kOutput, calls=%fused_computation.6.clone.1 | convolution fusion | flops 341836224 | bytes 15466605 | tf_op jit(solution)/shard_map/while/body/eval_jaxpr/kt,kab->tab/dot_general | solution.py:38
  458.5 10.3 %copy.34 = f32[27,256,256]{2,0,1:T(8,128)} copy(f32[27,256,256]{1,2,0:T(8,128)} %convolution_bitcast_fusion.2) | data formatting | bytes 14155776 | tf_op jit(solution)/shard_map/while/body/eval_jaxpr/ra,krb->kab/transpose | solution.py:34
  468.8 10.0 %select_add_fusion.2 = f32[16,256,256]{2,0,1:T(8,128)} fusion(f32[16,256,256]{2,0,1:T(8,128)} %get-tuple-element.149, f32[27,256,256]{2,0,1:T(8,128)} %copy.34, pred[]{:T(512)S(6)} %compare.12, s32[27]{0:T(128)S(1)} %get-tuple-element.138), kind=kOutput, calls=%fused_computation.6.clone.1 | convolution fusion | flops 341836224 | bytes 15466605 | tf_op jit(solution)/shard_map/while/body/eval_jaxpr/kt,kab->tab/dot_general | solution.py:38
  490.9 9.8 %all-to-all-start.2 = ((bf16[32,256,256]{2,1,0:T(8,128)(2,1)}), bf16[32,256,256]{2,1,0:T(8,128)(2,1)}, u32[]{:S(2)}, u32[]{:S(2)}) async-start(bf16[32,256,256]{2,1,0:T(8,128)(2,1)} %scatter_fusion), calls=%async_computation.2 | async-start | bytes 8388608 | tf_op jit(solution)/shard_map/all_to_all | solution.py:51
  501.5 91.9 %all-to-all-done.2 = bf16[32,256,256]{2,1,0:T(8,128)(2,1)} async-done(((bf16[32,256,256]{2,1,0:T(8,128)(2,1)}), bf16[32,256,256]{2,1,0:T(8,128)(2,1)}, u32[]{:S(2)}, u32[]{:S(2)}) %all-to-all-start.2) | async-done | bytes 4194336 | tf_op jit(solution)/shard_map/all_to_all | solution.py:51
  602.3 17.6 %scatter_fusion.1 = f32[16,256,256]{2,1,0:T(8,128)} fusion(f32[16,256,256]{2,1,0:T(8,128)} %broadcast.139, s32[32]{0:T(128)S(1)} %fusion.16, f32[32,256,256]{2,1,0:T(8,128)} %convert_element_type.11), kind=kCustom, calls=%fused_computation.4 | custom fusion | flops 2097152 | bytes 25165952 | tf_op jit(solution)/shard_map/scatter-add | solution.py:59
  619.9 40.0 %reduce-scatter.2.cloned.1.call-done = f32[2,256,256]{2,1,0:T(8,128)} async-done(((f32[16,256,256]{2,1,0:T(8,128)}), f32[2,256,256]{2,1,0:T(8,128)}) %reduce-scatter.2.cloned.1.call-update) | async-done | bytes 524304 | tf_op jit(solution)/shard_map/reduce_scatter | solution.py:61
  (161 shorter events, 161.6 us)
Async XLA Ops:
  11.0 11.8 %copy-start.4 = (s32[1,1,16]{2,1,0:T(1,128)S(1)}, s32[1,1,16]{2,1,0:T(1,128)}, u32[]{:S(2)}) copy-start(s32[1,1,16]{2,1,0:T(1,128)} %param.14) | copy-start | bytes 196
  11.0 11.8 %copy-start.5 = (s32[1,1,16]{2,1,0:T(1,128)S(1)}, s32[1,1,16]{2,1,0:T(1,128)}, u32[]{:S(2)}) copy-start(s32[1,1,16]{2,1,0:T(1,128)} %param.15) | copy-start | bytes 196
  11.0 13.1 %copy-start.2 = (s32[1,1,12,27]{3,1,2,0:T(1,128)S(1)}, s32[1,1,12,27]{3,1,2,0:T(1,128)}, u32[]{:S(2)}) copy-start(s32[1,1,12,27]{3,1,2,0:T(1,128)} %param.11) | copy-start | bytes 3892
  11.0 13.1 %copy-start.3 = (s32[1,1,12,27]{3,1,2,0:T(1,128)S(1)}, s32[1,1,12,27]{3,1,2,0:T(1,128)}, u32[]{:S(2)}) copy-start(s32[1,1,12,27]{3,1,2,0:T(1,128)} %param.13) | copy-start | bytes 3892
  11.0 82.8 %all-to-all-start.1 = ((bf16[32,3,64,256]{3,2,1,0:T(8,128)(2,1)}), bf16[32,3,64,256]{3,2,1,0:T(8,128)(2,1)S(1)}, u32[]{:S(2)}, u32[]{:S(2)}) async-start(bf16[32,3,64,256]{3,2,1,0:T(8,128)(2,1)} %bitcast.68), calls=%async_computation.1 | async-start | bytes 6291456 | tf_op jit(solution)/shard_map/all_to_all | solution.py:19
  93.8 397.1 %all-to-all-start = ((s32[32,1,1]{2,1,0:T(1,128)}), s32[32,1,1]{2,1,0:T(1,128)S(1)}, u32[]{:S(2)}, u32[]{:S(2)}) async-start(s32[32,1,1]{2,1,0:T(1,128)} %copy.19), calls=%async_computation | async-start | bytes 32768 | tf_op jit(solution)/shard_map/all_to_all | solution.py:52
  101.3 1.7 copy-start
  122.9 8.8 %copy-start.1 = (bf16[96,64,256]{2,1,0:T(8,128)(2,1)S(1)}, bf16[96,64,256]{2,1,0:T(8,128)(2,1)}, u32[]{:S(2)}) copy-start(bf16[96,64,256]{2,1,0:T(8,128)(2,1)} %copy-done) | copy-start | bytes 9437188 | tf_op jit(solution)/shard_map/while
  131.7 1.7 copy-start
  153.2 10.0 %copy-start.1 = (bf16[96,64,256]{2,1,0:T(8,128)(2,1)S(1)}, bf16[96,64,256]{2,1,0:T(8,128)(2,1)}, u32[]{:S(2)}) copy-start(bf16[96,64,256]{2,1,0:T(8,128)(2,1)} %copy-done) | copy-start | bytes 9437188 | tf_op jit(solution)/shard_map/while
  163.3 1.7 copy-start
  184.8 10.0 %copy-start.1 = (bf16[96,64,256]{2,1,0:T(8,128)(2,1)S(1)}, bf16[96,64,256]{2,1,0:T(8,128)(2,1)}, u32[]{:S(2)}) copy-start(bf16[96,64,256]{2,1,0:T(8,128)(2,1)} %copy-done) | copy-start | bytes 9437188 | tf_op jit(solution)/shard_map/while
  194.8 1.7 copy-start
  216.3 10.0 %copy-start.1 = (bf16[96,64,256]{2,1,0:T(8,128)(2,1)S(1)}, bf16[96,64,256]{2,1,0:T(8,128)(2,1)}, u32[]{:S(2)}) copy-start(bf16[96,64,256]{2,1,0:T(8,128)(2,1)} %copy-done) | copy-start | bytes 9437188 | tf_op jit(solution)/shard_map/while
  226.4 1.7 copy-start
  247.9 10.0 %copy-start.1 = (bf16[96,64,256]{2,1,0:T(8,128)(2,1)S(1)}, bf16[96,64,256]{2,1,0:T(8,128)(2,1)}, u32[]{:S(2)}) copy-start(bf16[96,64,256]{2,1,0:T(8,128)(2,1)} %copy-done) | copy-start | bytes 9437188 | tf_op jit(solution)/shard_map/while
  257.9 1.7 copy-start
  279.5 10.0 %copy-start.1 = (bf16[96,64,256]{2,1,0:T(8,128)(2,1)S(1)}, bf16[96,64,256]{2,1,0:T(8,128)(2,1)}, u32[]{:S(2)}) copy-start(bf16[96,64,256]{2,1,0:T(8,128)(2,1)} %copy-done) | copy-start | bytes 9437188 | tf_op jit(solution)/shard_map/while
  289.5 1.7 copy-start
  311.0 10.0 %copy-start.1 = (bf16[96,64,256]{2,1,0:T(8,128)(2,1)S(1)}, bf16[96,64,256]{2,1,0:T(8,128)(2,1)}, u32[]{:S(2)}) copy-start(bf16[96,64,256]{2,1,0:T(8,128)(2,1)} %copy-done) | copy-start | bytes 9437188 | tf_op jit(solution)/shard_map/while
  321.1 1.7 copy-start
  342.6 10.0 %copy-start.1 = (bf16[96,64,256]{2,1,0:T(8,128)(2,1)S(1)}, bf16[96,64,256]{2,1,0:T(8,128)(2,1)}, u32[]{:S(2)}) copy-start(bf16[96,64,256]{2,1,0:T(8,128)(2,1)} %copy-done) | copy-start | bytes 9437188 | tf_op jit(solution)/shard_map/while
  352.6 1.7 copy-start
  374.2 10.0 %copy-start.1 = (bf16[96,64,256]{2,1,0:T(8,128)(2,1)S(1)}, bf16[96,64,256]{2,1,0:T(8,128)(2,1)}, u32[]{:S(2)}) copy-start(bf16[96,64,256]{2,1,0:T(8,128)(2,1)} %copy-done) | copy-start | bytes 9437188 | tf_op jit(solution)/shard_map/while
  384.2 1.7 copy-start
  405.7 10.0 %copy-start.1 = (bf16[96,64,256]{2,1,0:T(8,128)(2,1)S(1)}, bf16[96,64,256]{2,1,0:T(8,128)(2,1)}, u32[]{:S(2)}) copy-start(bf16[96,64,256]{2,1,0:T(8,128)(2,1)} %copy-done) | copy-start | bytes 9437188 | tf_op jit(solution)/shard_map/while
  415.8 1.7 copy-start
  437.3 10.0 %copy-start.1 = (bf16[96,64,256]{2,1,0:T(8,128)(2,1)S(1)}, bf16[96,64,256]{2,1,0:T(8,128)(2,1)}, u32[]{:S(2)}) copy-start(bf16[96,64,256]{2,1,0:T(8,128)(2,1)} %copy-done) | copy-start | bytes 9437188 | tf_op jit(solution)/shard_map/while
  447.3 1.7 copy-start
  468.8 10.0 %copy-start.1 = (bf16[96,64,256]{2,1,0:T(8,128)(2,1)S(1)}, bf16[96,64,256]{2,1,0:T(8,128)(2,1)}, u32[]{:S(2)}) copy-start(bf16[96,64,256]{2,1,0:T(8,128)(2,1)} %copy-done) | copy-start | bytes 9437188 | tf_op jit(solution)/shard_map/while
  490.9 102.5 %all-to-all-start.2 = ((bf16[32,256,256]{2,1,0:T(8,128)(2,1)}), bf16[32,256,256]{2,1,0:T(8,128)(2,1)}, u32[]{:S(2)}, u32[]{:S(2)}) async-start(bf16[32,256,256]{2,1,0:T(8,128)(2,1)} %scatter_fusion), calls=%async_computation.2 | async-start | bytes 8388608 | tf_op jit(solution)/shard_map/all_to_all | solution.py:51
  500.8 159.1 %reduce-scatter.2.cloned.1.call-start = ((), (), s32[]{:S(2)}) async-start(), calls=%async_computation.4 | async-start | bytes 4718592 | tf_op jit(solution)/shard_map/reduce_scatter | solution.py:61
Sparse Core Ops, SparseCore 0:
  620.0 39.7 reduce-scatter.1
where the time goes:
time: 671 us; the launch traced here: 667 us
  local copies, waits for them, and re-layouts  211 us (31%)
  waiting for transfers between devices  202 us (30%)
  matrix products  186 us (28%)
  starting transfers between devices  29.1 us (4%)
  other arithmetic  25.8 us (4%)
  between operations  13.5 us (2%)
    transpose x12, local copies, waits for them, and re-layouts, one_row(): jnp.einsum('ra,krb->kab', panel_row, product, preferred_element_type=jnp....  124 us
    dot_general x12, matrix products, one_row(): jnp.einsum('kt,kab->tab', selector, outer_tile, precision=lax.Precision.H...  119 us
    all_to_all x1, waiting for transfers between devices, body(): lax.all_to_all(sending, 'dev', split_axis=0, concat_axis=0, tiled=True)  91.9 us
    all_to_all x1, waiting for transfers between devices, body(): lax.all_to_all(outgoing, 'dev', split_axis=0, concat_axis=0, tiled=True)  69.6 us
    dot_general x12, matrix products, one_row(): jnp.einsum('ra,krb->kab', panel_row, product, preferred_element_type=jnp....  66.5 us
    reduce_scatter x1, waiting for transfers between devices, body(): result = lax.psum_scatter(table, 'grp', scatter_dimension=0, tiled=True)  40 us
    gather x12, local copies, waits for them, and re-layouts, one_row(): near_panels = arrived[jnp.maximum(column_ids, 0)]  29.9 us
    while x48, local copies, waits for them, and re-layouts  20.2 us
  transfers between devices with their start and end apart: 4, of which 3 were waited for; matrix products, arithmetic and copies ran while one was open for 56% of the time, Pallas kernels for 0%

commit v1 on v0

v1 whole, which is shorter than its diff:
```python
import functools

import jax
import jax.numpy as jnp
from jax import lax
from jax.experimental import pallas as pl
from jax.experimental.pallas import tpu as pltpu
from jax.sharding import PartitionSpec as P

BLOCK = 64
W = 256
R = 12
K = 27
CT = 2
NCAP = 3
LT = 16
PAIR = 2 * BLOCK


def tiles_kernel(cols_ref, slots_ref, places_ref, a_ref, pt_ref, b_ref, out_ref, near_ref):
    row = pl.program_id(0)
    width = b_ref.shape[-1]
    rows_of = pl.ds(row * BLOCK, BLOCK)

    @pl.when(row == 0)
    def _():
        @pl.loop(0, LT)
        def _(t):
            near_ref[t] = jnp.zeros(near_ref.shape[1:], jnp.float32)

    lane = lax.broadcasted_iota(jnp.int32, (BLOCK, PAIR), 1)
    left = jnp.where(lane < BLOCK, 1.0, 0.0).astype(jnp.bfloat16)
    right = jnp.where(lane < BLOCK, 0.0, 1.0).astype(jnp.bfloat16)

    def target(k):
        return jnp.where(cols_ref[row, k] < 0, LT, slots_ref[row, k])

    def panel(k):
        return b_ref[jnp.maximum(cols_ref[row, k], 0)]

    def add(k, product):
        rounded = product.astype(jnp.bfloat16).astype(jnp.float32)
        near_ref[target(k), rows_of, :] += rounded

    for j in range(K // 2):
        pair = a_ref[0, :, j * PAIR : (j + 1) * PAIR]
        both = jnp.concatenate([pair * left, pair * right], axis=0)
        panels = jnp.concatenate([panel(2 * j), panel(2 * j + 1)], axis=0)
        product = jnp.dot(both, panels, preferred_element_type=jnp.float32)
        add(2 * j, product[:BLOCK])
        add(2 * j + 1, product[BLOCK:])
    last = a_ref[0, :, (K - 1) * BLOCK :]
    add(K - 1, jnp.dot(last, panel(K - 1), preferred_element_type=jnp.float32))

    @pl.when(row == R - 1)
    def _():
        @pl.loop(0, LT)
        def _(t):
            near = near_ref[t]
            high = near.astype(jnp.bfloat16)
            low = (near - high.astype(jnp.float32)).astype(jnp.bfloat16)
            tile = jnp.dot(pt_ref[...], high, preferred_element_type=jnp.float32)
            tile += jnp.dot(pt_ref[...], low, preferred_element_type=jnp.float32)
            out_ref[places_ref[t]] = tile.astype(jnp.bfloat16)


def device_tiles(blocks, pt, arrived, cols, slots, places, n_places):
    width = arrived.shape[-1]
    return pl.pallas_call(
        tiles_kernel,
        out_shape=jax.ShapeDtypeStruct((n_places, W, width), jnp.bfloat16),
        grid_spec=pltpu.PrefetchScalarGridSpec(
            num_scalar_prefetch=3,
            grid=(R,),
            in_specs=[
                pl.BlockSpec((1, BLOCK, K * BLOCK), lambda i, *_: (i, 0, 0)),
                pl.BlockSpec((W, R * BLOCK), lambda i, *_: (0, 0)),
                pl.BlockSpec(arrived.shape, lambda i, *_: (0, 0, 0)),
            ],
            out_specs=pl.BlockSpec((n_places, W, width), lambda i, *_: (0, 0, 0)),
            scratch_shapes=[pltpu.VMEM((LT + 1, R * BLOCK, width), jnp.float32)],
        ),
        compiler_params=pltpu.CompilerParams(
            dimension_semantics=("arbitrary",), vmem_limit_bytes=60 << 20
        ),
        cost_estimate=pl.CostEstimate(
            flops=8_000_000_000 * width // W,
            bytes_accessed=10_000_000 * width // W,
            transcendentals=0,
        ),
        name="device_tiles",
    )(cols, slots, places, blocks, pt, arrived)


def table_kernel(labels_ref, got_ref, table_ref, sum_ref):
    spread = table_ref.shape[0]

    @pl.loop(0, spread)
    def _(t):
        sum_ref[t] = jnp.zeros(sum_ref.shape[1:], jnp.float32)

    @pl.loop(0, got_ref.shape[0])
    def _(s):
        label = labels_ref[s]
        at = jnp.where(label < 0, spread, label)
        sum_ref[at] += got_ref[s].astype(jnp.float32)

    @pl.loop(0, spread)
    def _(t):
        table_ref[t] = sum_ref[t].astype(table_ref.dtype)


def table_of(labels, got, spread):
    n, _, width = got.shape
    rows = 64
    return pl.pallas_call(
        table_kernel,
        out_shape=jax.ShapeDtypeStruct((spread, W, width), jnp.bfloat16),
        grid_spec=pltpu.PrefetchScalarGridSpec(
            num_scalar_prefetch=1,
            grid=(W // rows,),
            in_specs=[pl.BlockSpec((n, rows, width), lambda i, *_: (0, i, 0))],
            out_specs=pl.BlockSpec((spread, rows, width), lambda i, *_: (0, i, 0)),
            scratch_shapes=[pltpu.VMEM((spread + 1, rows, width), jnp.float32)],
        ),
        compiler_params=pltpu.CompilerParams(dimension_semantics=("arbitrary",)),
        cost_estimate=pl.CostEstimate(
            flops=n * W * width, bytes_accessed=6_000_000 * width // W, transcendentals=0
        ),
        name="table_of",
    )(labels, got)


def body(blocks, prolong, block_cols, fetch_rows, tile_slot, tile_owner, tile_place):
    dev_count = lax.axis_size("dev")
    grp_count = lax.axis_size("grp")
    panels = prolong[0, 0]
    outgoing = panels[fetch_rows[0, 0]].reshape(dev_count, NCAP * BLOCK, W)
    arrived = lax.all_to_all(outgoing, "dev", split_axis=0, concat_axis=0, tiled=True)
    arrived = arrived.reshape(dev_count * NCAP, BLOCK, W)

    owners = tile_owner[0, 0]
    dev_target = owners % dev_count
    label = (owners // dev_count) * CT + tile_place[0, 0]
    labels = jnp.full((dev_count,), -1, jnp.int32).at[dev_target].set(label)
    got_labels = lax.all_to_all(labels, "dev", split_axis=0, concat_axis=0, tiled=True)

    pt = panels.reshape(R * BLOCK, W).T
    sending = device_tiles(
        blocks[0, 0], pt, arrived, block_cols[0, 0], tile_slot[0, 0], dev_target, dev_count
    )
    got = lax.all_to_all(sending, "dev", split_axis=0, concat_axis=0, tiled=True)
    table = table_of(got_labels, got, grp_count * CT)
    parts = lax.all_to_all(table, "grp", split_axis=0, concat_axis=0, tiled=True)
    parts = parts.reshape(grp_count, CT, W, W).astype(jnp.float32)
    return parts.sum(0).reshape(1, 1, CT, W, W)


def solution(mesh):
    return jax.shard_map(
        body,
        mesh=mesh,
        in_specs=(
            P("grp", "dev", None, None, None),
            P("grp", "dev", None, None, None),
            P("grp", "dev", None, None),
            P("grp", "dev", None, None),
            P("grp", "dev", None, None),
            P("grp", "dev", None),
            P("grp", "dev", None),
        ),
        out_specs=P("grp", "dev", None, None, None),
        check_vma=False,
    )
```

time: 671 us -> 258 us (0.38)
  local copies, waits for them, and re-layouts: 211 us -> 7.81 us
  matrix products: 186 us -> 0 us
  waiting for transfers between devices: 202 us -> 156 us
  blocking collectives: 0 us -> 31.6 us
  Pallas kernels: 0 us -> 25.8 us
  other arithmetic: 25.8 us -> 5.38 us
  between operations: 13.5 us -> 0.05 us
    dot_general x24 -> x0, matrix products: 186 us -> none  [the longest x12 119 us: one_row(): jnp.einsum('kt,kab->tab', selector, outer_tile, precision=lax.Precision.H...]
    transpose x12 -> x0, local copies, waits for them, and re-layouts: 124 us -> none  [one_row(): jnp.einsum('ra,krb->kab', panel_row, product, preferred_element_type=jnp....]
    reduce_scatter x1 -> x0, waiting for transfers between devices: 40 us -> none  [body(): result = lax.psum_scatter(table, 'grp', scatter_dimension=0, tiled=True)]
    all_to_all x0 -> x1, blocking collectives: none -> 31.6 us  [body(): lax.all_to_all(table, 'grp', split_axis=0, concat_axis=0, tiled=True)]
    gather x13 -> x1, local copies, waits for them, and re-layouts: 33.4 us -> 3.54 us  [body(): outgoing = panels[fetch_rows[0, 0]].reshape(dev_count, NCAP * BLOCK, W)]
    pallas_call x0 -> x2, Pallas kernels: none -> 25.8 us  [the longest x1 19.7 us: device_tiles(): pl.pallas_call(tiles_kernel, out_shape=jax.ShapeDtypeStruct((n_places, W,...]
    while x49 -> x0, local copies, waits for them, and re-layouts: 24.6 us -> none
    scatter-add x1 -> x0, other arithmetic: 17.6 us -> none  [body(): table = jnp.zeros((spread, W, W), jnp.float32).at[keyed].add(got_tiles.as...]
  transfers between devices with their start and end apart: 4 -> 3, of which waited for: 3 -> 2; matrix products, arithmetic and copies ran while one was open for 56% -> 3% of each run, Pallas kernels for 0% -> 8%
where the time goes in v1:
time: 258 us; the launch traced here: 256 us
  waiting for transfers between devices  156 us (60%)
  blocking collectives  31.6 us (12%)
  starting transfers between devices  29.1 us (11%)
  Pallas kernels  25.8 us (10%)
  local copies, waits for them, and re-layouts  7.81 us (3%)
  other arithmetic  5.38 us (2%)
    all_to_all x1, waiting for transfers between devices, body(): lax.all_to_all(sending, 'dev', split_axis=0, concat_axis=0, tiled=True)  91.6 us
    all_to_all x1, waiting for transfers between devices, body(): lax.all_to_all(outgoing, 'dev', split_axis=0, concat_axis=0, tiled=True)  64.5 us
    all_to_all x1, blocking collectives, body(): lax.all_to_all(table, 'grp', split_axis=0, concat_axis=0, tiled=True)  31.6 us
    pallas_call x1, Pallas kernels, device_tiles(): pl.pallas_call(tiles_kernel, out_shape=jax.ShapeDtypeStruct((n_places, W,...  19.7 us
    all_to_all x1, starting transfers between devices, body(): lax.all_to_all(outgoing, 'dev', split_axis=0, concat_axis=0, tiled=True)  11.7 us
    all_to_all x1, starting transfers between devices, body(): lax.all_to_all(sending, 'dev', split_axis=0, concat_axis=0, tiled=True)  9.84 us
    all_to_all x1, starting transfers between devices, body(): lax.all_to_all(labels, 'dev', split_axis=0, concat_axis=0, tiled=True)  7.54 us
    pallas_call x1, Pallas kernels, table_of(): pl.pallas_call(table_kernel, out_shape=jax.ShapeDtypeStruct((spread, W, w...  6.09 us
  transfers between devices with their start and end apart: 3, of which 2 were waited for; matrix products, arithmetic and copies ran while one was open for 3% of the time, Pallas kernels for 8%

profile of v1, /device:TPU:4, one launch (start us, length us, event | category | flops | bytes accessed | tf_op | source)
XLA Modules:
  0.0 255.9 jit_solution(12359056464026127915)
XLA Ops:
  0.0 0.7 compare_select_fusion
  0.7 0.1 copy.17
  0.8 0.1 reshape.109
  0.9 3.5 %gather_fusion = bf16[96,64,256]{2,1,0:T(8,128)(2,1)} fusion(bf16[12,64,256]{2,1,0:T(8,128)(2,1)} %bitcast.42, s32[1024]{0:T(1024)S(1)} %pad_clamp_fusion), kind=kCustom, calls=%fused_computation | custom fusion | bytes 6291840 | tf_op jit(solution)/shard_map/gather | solution.py:138
  4.4 0.0 copy-start
  4.4 0.0 copy-start.2
  4.4 0.0 copy-start.3
  4.4 11.7 %all-to-all-start.1 = ((bf16[32,192,256]{2,1,0:T(8,128)(2,1)}), bf16[32,192,256]{2,1,0:T(8,128)(2,1)S(1)}, u32[]{:S(2)}, u32[]{:S(2)}) async-start(bf16[32,192,256]{2,1,0:T(8,128)(2,1)} %bitcast.10), calls=%async_computation.1 | async-start | bytes 6291456 | tf_op jit(solution)/shard_map/all_to_all | solution.py:139
  16.2 1.2 fusion.1
  17.3 1.3 and_select_fusion
  18.6 1.3 scatter_custom_fusion
  19.9 1.3 copy.15
  21.1 0.0 copy-done
  21.1 0.9 copy.16
  22.1 0.0 copy-done.2
  22.1 0.0 copy-done.3
  22.1 0.6 copy_bitcast_fusion
  22.7 64.5 %all-to-all-done.1 = bf16[32,192,256]{2,1,0:T(8,128)(2,1)S(1)} async-done(((bf16[32,192,256]{2,1,0:T(8,128)(2,1)}), bf16[32,192,256]{2,1,0:T(8,128)(2,1)S(1)}, u32[]{:S(2)}, u32[]{:S(2)}) %all-to-all-start.1) | async-done | bytes 3145760 | tf_op jit(solution)/shard_map/all_to_all | solution.py:139
  87.2 0.0 copy-start.1
  87.2 7.5 %all-to-all-start = ((s32[32,1,1]{2,1,0:T(1,128)}), s32[32,1,1]{2,1,0:T(1,128)S(1)}, u32[]{:S(2)}, u32[]{:S(2)}) async-start(s32[32,1,1]{2,1,0:T(1,128)} %copy.15), calls=%async_computation | async-start | bytes 32768 | tf_op jit(solution)/shard_map/all_to_all | solution.py:146
  94.7 0.0 copy-done.1
  94.8 19.7 %device_tiles.1 = bf16[32,256,256]{2,1,0:T(8,128)(2,1)} custom-call(s32[12,27]{1,0:T(8,128)} %get-tuple-element.8.cols_ref, s32[12,27]{1,0:T(8,128)} %get-tuple-element.7.slots_ref, s32[16]{0:T(128)} %get-tuple-element.5.places_ref, bf16[12,64,1728]{2,1,0:T(8,128)(2,1)} %bitcast.48, bf16[256,768]{1,0:T(8,128)(2,1)} %bitcast.46, bf16[96,64,256]{2,1,0:T(8,128)(2,1)} %bitcast.45), custom_call_target="tpu_custom_call" | custom-call | flops 8000000000 | bytes 10000000 | tf_op jit(solution)/shard_map/device_tiles/pallas_call | solution.py:69
  114.5 0.0 all-to-all-done
  114.5 9.8 %all-to-all-start.2 = ((bf16[32,256,256]{2,1,0:T(8,128)(2,1)}), bf16[32,256,256]{2,1,0:T(8,128)(2,1)}, u32[]{:S(2)}, u32[]{:S(2)}) async-start(bf16[32,256,256]{2,1,0:T(8,128)(2,1)} %device_tiles.1), calls=%async_computation.2 | async-start | bytes 8388608 | tf_op jit(solution)/shard_map/all_to_all | solution.py:152
  124.3 1.2 reduce.labels_ref
  125.5 91.6 %all-to-all-done.2.got_ref = bf16[32,256,256]{2,1,0:T(8,128)(2,1)} async-done(((bf16[32,256,256]{2,1,0:T(8,128)(2,1)}), bf16[32,256,256]{2,1,0:T(8,128)(2,1)}, u32[]{:S(2)}, u32[]{:S(2)}) %all-to-all-start.2) | async-done | bytes 4194336 | tf_op jit(solution)/shard_map/all_to_all | solution.py:152
  217.1 6.1 %table_of.1 = bf16[16,256,256]{2,1,0:T(8,128)(2,1)} custom-call(s32[32]{0:T(128)} %reduce.labels_ref, bf16[32,256,256]{2,1,0:T(8,128)(2,1)} %all-to-all-done.2.got_ref), custom_call_target="tpu_custom_call" | custom-call | flops 2097152 | bytes 6000000 | tf_op jit(solution)/shard_map/table_of/pallas_call | solution.py:116
  223.2 31.6 %all_to_all.26 = bf16[16,256,256]{2,1,0:T(8,128)(2,1)S(1)} all-to-all(bf16[16,256,256]{2,1,0:T(8,128)(2,1)} %table_of.1), channel_id=1, replica_groups=mesh['grp'=8,'dev'=32] {'grp'}, dimensions={0} | all-to-all | bytes 4194304 | tf_op jit(solution)/shard_map/all_to_all | solution.py:154
  254.8 1.1 convert_reduce_fusion
  (1 shorter events, 0.0 us)
Async XLA Ops:
  4.4 16.7 %copy-start = (bf16[1,1,12,64,256]{4,3,2,1,0:T(8,128)(2,1)S(1)}, bf16[1,1,12,64,256]{4,3,2,1,0:T(8,128)(2,1)}, u32[]{:S(2)}) copy-start(bf16[1,1,12,64,256]{4,3,2,1,0:T(8,128)(2,1)} %param.8) | copy-start | bytes 1179652
  4.4 17.6 %copy-start.2 = (s32[1,1,12,27]{3,1,2,0:T(1,128)S(1)}, s32[1,1,12,27]{3,1,2,0:T(1,128)}, u32[]{:S(2)}) copy-start(s32[1,1,12,27]{3,1,2,0:T(1,128)} %param.11) | copy-start | bytes 3892
  4.4 17.6 %copy-start.3 = (s32[1,1,12,27]{3,1,2,0:T(1,128)S(1)}, s32[1,1,12,27]{3,1,2,0:T(1,128)}, u32[]{:S(2)}) copy-start(s32[1,1,12,27]{3,1,2,0:T(1,128)} %param.9) | copy-start | bytes 3892
  4.4 82.8 %all-to-all-start.1 = ((bf16[32,192,256]{2,1,0:T(8,128)(2,1)}), bf16[32,192,256]{2,1,0:T(8,128)(2,1)S(1)}, u32[]{:S(2)}, u32[]{:S(2)}) async-start(bf16[32,192,256]{2,1,0:T(8,128)(2,1)} %bitcast.10), calls=%async_computation.1 | async-start | bytes 6291456 | tf_op jit(solution)/shard_map/all_to_all | solution.py:139
  87.2 7.5 %copy-start.1 = (bf16[32,192,256]{2,1,0:T(8,128)(2,1)}, bf16[32,192,256]{2,1,0:T(8,128)(2,1)S(1)}, u32[]{:S(2)}) copy-start(bf16[32,192,256]{2,1,0:T(8,128)(2,1)S(1)} %all-to-all-done.1) | copy-start | bytes 9437188
  87.2 27.3 %all-to-all-start = ((s32[32,1,1]{2,1,0:T(1,128)}), s32[32,1,1]{2,1,0:T(1,128)S(1)}, u32[]{:S(2)}, u32[]{:S(2)}) async-start(s32[32,1,1]{2,1,0:T(1,128)} %copy.15), calls=%async_computation | async-start | bytes 32768 | tf_op jit(solution)/shard_map/all_to_all | solution.py:146
  114.5 102.6 %all-to-all-start.2 = ((bf16[32,256,256]{2,1,0:T(8,128)(2,1)}), bf16[32,256,256]{2,1,0:T(8,128)(2,1)}, u32[]{:S(2)}, u32[]{:S(2)}) async-start(bf16[32,256,256]{2,1,0:T(8,128)(2,1)} %device_tiles.1), calls=%async_computation.2 | async-start | bytes 8388608 | tf_op jit(solution)/shard_map/all_to_all | solution.py:152

commit v2 on v1

--- a/solution.py
+++ b/solution.py
@@ -6,6 +6,7 @@
 from jax.experimental import pallas as pl
 from jax.experimental.pallas import tpu as pltpu
 from jax.sharding import PartitionSpec as P
+
 
 BLOCK = 64
 W = 256
@@ -15,19 +16,135 @@
 NCAP = 3
 LT = 16
 PAIR = 2 * BLOCK
-
-
-def tiles_kernel(cols_ref, slots_ref, places_ref, a_ref, pt_ref, b_ref, out_ref, near_ref):
+HALVES = 1
+STEPS = (1, -1, 2)
+
+
+def pick_kernel(n_x, ups, asks_ref, *refs):
+    block_refs, out_refs = refs[: len(ups)], refs[len(ups) :]
+    z, x = lax.axis_index("dev") // n_x, lax.axis_index("dev") % n_x
+    n_z = asks_ref.shape[0] // n_x
+    for i, (up, block_ref) in enumerate(zip(ups, block_refs)):
+        source = (z + n_z - up) % n_z * n_x + x
+        for step, out_ref in zip(STEPS, out_refs):
+            peer = (x + n_x + step) % n_x
+            for c in range(NCAP):
+                out_ref[i * NCAP + c] = block_ref[asks_ref[source, 1 + peer * NCAP + c]]
+
+
+def pick(asks, n_x, ups, blocks):
+    shape = (len(blocks) * NCAP,) + blocks[0].shape[1:]
+    whole = lambda shape: pl.BlockSpec(shape, lambda i, *_: (0,) * len(shape))
+    return pl.pallas_call(
+        functools.partial(pick_kernel, n_x, ups),
+        out_shape=[jax.ShapeDtypeStruct(shape, blocks[0].dtype)] * len(STEPS),
+        grid_spec=pltpu.PrefetchScalarGridSpec(
+            num_scalar_prefetch=1,
+            grid=(1,),
+            in_specs=[whole(b.shape) for b in blocks],
+            out_specs=[whole(shape)] * len(STEPS),
+        ),
+        cost_estimate=pl.CostEstimate(flops=0, bytes_accessed=1_500_000, transcendentals=0),
+        name="pick",
+    )(asks, *blocks)
+
+
+def fetch(panels, rows_of, labels):
+    n_z, n_x = 8, 4
+    half = n_z // 2
+    me = lax.axis_index("dev")
+    z, x = me // n_x, me % n_x
+
+    def along_z(step):
+        return [(s, (s // n_x + step) % n_z * n_x + s % n_x) for s in range(n_z * n_x)]
+
+    def along_x(step):
+        return [(s, s // n_x * n_x + (s % n_x + step) % n_x) for s in range(n_z * n_x)]
+
+    def forward(asks, ups, blocks):
+        picked = pick(asks, n_x, ups, blocks)
+        return [lax.ppermute(p, "dev", along_x(step)) for p, step in zip(picked, STEPS)]
+
+    fetched = rows_of.reshape(n_z, 1, n_x * NCAP)
+    first = jnp.broadcast_to(fetched, (n_z, n_x, n_x * NCAP)).reshape(n_z * n_x, n_x * NCAP)
+    asked = jnp.concatenate([labels[:, None], first], axis=1)
+
+    up = lax.ppermute(panels, "dev", along_z(1))
+    down = lax.ppermute(panels, "dev", along_z(-1))
+    asks = lax.all_to_all(asked, "dev", split_axis=0, concat_axis=0, tiled=True)
+    blocks = {0: panels}
+    sent = {0: forward(asked, (0,), (panels,))}
+    for k in range(1, half):
+        blocks[n_z - k], blocks[k] = up, down
+        if k + 1 < half:
+            new_up = lax.ppermute(up, "dev", along_z(1))
+            new_down = lax.ppermute(down, "dev", along_z(-1))
+        else:
+            odd = lax.axis_index("grp") % 2 == 1
+            n = n_z * n_x
+            pairs = [
+                (g * n + s, g * n + t)
+                for g in range(lax.axis_size("grp"))
+                for s, t in along_z(-1 if g % 2 else 1)
+            ]
+            far = lax.ppermute(jnp.where(odd, down, up), ("grp", "dev"), pairs)
+        sent[k] = forward(asks, (k, -k), (up, down))
+        up, down = new_up, new_down
+    blocks[half] = far
+    sent[half] = forward(asks, (half,), (far,))
+
+    entry = jnp.arange(n_z * n_x * NCAP, dtype=jnp.int32)
+    s, c = entry // NCAP, entry % NCAP
+    dz, dx = (s // n_x - z) % n_z, (s % n_x - x) % n_x
+    table = asks[:, 1:].reshape(n_z, n_x, n_x, NCAP)
+    column = jnp.arange(n_x)[:, None] == x
+    own = jnp.sum(jnp.where(column[None, :, :, None] & column.T[None, :, :, None], table, 0), (1, 2))
+    own = jnp.broadcast_to(own[:, None, :], (n_z, n_x, NCAP)).reshape(-1)
+    there = n_z * R + (dx - 1) * (n_z * NCAP) + dz * NCAP + c
+    where = jnp.where(dx == 0, dz * R + own, there).astype(jnp.int32)
+
+    pieces, spots = [], []
+    for d in range(n_z):
+        pieces.append(blocks[d])
+        spots.append([(0, R, d * R)])
+    for j, step in enumerate(STEPS):
+        base = n_z * R + ((-step) % n_x - 1) * (n_z * NCAP)
+        for k in range(half + 1):
+            pieces.append(sent[k][j])
+            if k in (0, half):
+                spots.append([(0, NCAP, base + k * NCAP)])
+            else:
+                spots.append([(0, NCAP, base + (n_z - k) * NCAP), (NCAP, NCAP, base + k * NCAP)])
+    return pieces, spots, where, asks[:, 0]
+
+
+def tiles_kernel(spots, first, cols_ref, slots_ref, places_ref, where_ref, a_ref, pt_ref, *refs):
+    piece_refs, (out_ref, b_ref, near_ref, sems) = refs[: len(spots)], refs[len(spots) :]
     row = pl.program_id(0)
     width = b_ref.shape[-1]
     rows_of = pl.ds(row * BLOCK, BLOCK)
 
     @pl.when(row == 0)
     def _():
+        copies = []
+        for piece_ref, parts in zip(piece_refs, spots):
+            for start, n, place in parts:
+                copies.append(
+                    pltpu.make_async_copy(
+                        piece_ref.at[pl.ds(start, n), :, pl.ds(first, width)],
+                        b_ref.at[pl.ds(place, n)],
+                        sems.at[len(copies)],
+                    )
+                )
+                copies[-1].start()
+
         @pl.loop(0, LT)
         def _(t):
             near_ref[t] = jnp.zeros(near_ref.shape[1:], jnp.float32)
 
+        for copy in copies:
+            copy.wait()
+
     lane = lax.broadcasted_iota(jnp.int32, (BLOCK, PAIR), 1)
     left = jnp.where(lane < BLOCK, 1.0, 0.0).astype(jnp.bfloat16)
     right = jnp.where(lane < BLOCK, 0.0, 1.0).astype(jnp.bfloat16)
@@ -36,7 +153,7 @@
         return jnp.where(cols_ref[row, k] < 0, LT, slots_ref[row, k])
 
     def panel(k):
-        return b_ref[jnp.maximum(cols_ref[row, k], 0)]
+        return b_ref[where_ref[jnp.maximum(cols_ref[row, k], 0)]]
 
     def add(k, product):
         rounded = product.astype(jnp.bfloat16).astype(jnp.float32)
@@ -64,32 +181,37 @@
             out_ref[places_ref[t]] = tile.astype(jnp.bfloat16)
 
 
-def device_tiles(blocks, pt, arrived, cols, slots, places, n_places):
-    width = arrived.shape[-1]
+def device_tiles(blocks, pt, pieces, spots, where, cols, slots, places, n_places, first, width):
+    n_copies = sum(len(parts) for parts in spots)
+    n_panels = max(place + n for parts in spots for _, n, place in parts)
     return pl.pallas_call(
-        tiles_kernel,
+        functools.partial(tiles_kernel, spots, first),
         out_shape=jax.ShapeDtypeStruct((n_places, W, width), jnp.bfloat16),
         grid_spec=pltpu.PrefetchScalarGridSpec(
-            num_scalar_prefetch=3,
+            num_scalar_prefetch=4,
             grid=(R,),
             in_specs=[
                 pl.BlockSpec((1, BLOCK, K * BLOCK), lambda i, *_: (i, 0, 0)),
                 pl.BlockSpec((W, R * BLOCK), lambda i, *_: (0, 0)),
-                pl.BlockSpec(arrived.shape, lambda i, *_: (0, 0, 0)),
+            ]
+            + [pl.BlockSpec(memory_space=pltpu.HBM)] * len(pieces),
+            out_specs=pl.BlockSpec((n_places, W, width), lambda i, *_: (0, 0, 0)),
+            scratch_shapes=[
+                pltpu.VMEM((n_panels, BLOCK, width), jnp.bfloat16),
+                pltpu.VMEM((LT + 1, R * BLOCK, width), jnp.float32),
+                pltpu.SemaphoreType.DMA((n_copies,)),
             ],
-            out_specs=pl.BlockSpec((n_places, W, width), lambda i, *_: (0, 0, 0)),
-            scratch_shapes=[pltpu.VMEM((LT + 1, R * BLOCK, width), jnp.float32)],
         ),
         compiler_params=pltpu.CompilerParams(
             dimension_semantics=("arbitrary",), vmem_limit_bytes=60 << 20
         ),
         cost_estimate=pl.CostEstimate(
             flops=8_000_000_000 * width // W,
-            bytes_accessed=10_000_000 * width // W,
+            bytes_accessed=20_000_000 * width // W,
             transcendentals=0,
         ),
         name="device_tiles",
-    )(cols, slots, places, blocks, pt, arrived)
+    )(cols, slots, places, where, blocks, pt, *pieces)
 
 
 def table_kernel(labels_ref, got_ref, table_ref, sum_ref):
@@ -131,34 +253,36 @@
     )(labels, got)
 
 
-def body(blocks, prolong, block_cols, fetch_rows, tile_slot, tile_owner, tile_place):
+def layer(blocks, prolong, block_cols, fetch_rows, tile_slot, tile_owner, tile_place):
     dev_count = lax.axis_size("dev")
     grp_count = lax.axis_size("grp")
     panels = prolong[0, 0]
-    outgoing = panels[fetch_rows[0, 0]].reshape(dev_count, NCAP * BLOCK, W)
-    arrived = lax.all_to_all(outgoing, "dev", split_axis=0, concat_axis=0, tiled=True)
-    arrived = arrived.reshape(dev_count * NCAP, BLOCK, W)
-
     owners = tile_owner[0, 0]
     dev_target = owners % dev_count
     label = (owners // dev_count) * CT + tile_place[0, 0]
-    labels = jnp.full((dev_count,), -1, jnp.int32).at[dev_target].set(label)
-    got_labels = lax.all_to_all(labels, "dev", split_axis=0, concat_axis=0, tiled=True)
+    meant = dev_target[None, :] == jnp.arange(dev_count)[:, None]
+    labels = jnp.max(jnp.where(meant, label[None, :], -1), axis=1)
+    pieces, spots, where, got_labels = fetch(panels, fetch_rows[0, 0], labels)
 
     pt = panels.reshape(R * BLOCK, W).T
-    sending = device_tiles(
-        blocks[0, 0], pt, arrived, block_cols[0, 0], tile_slot[0, 0], dev_target, dev_count
-    )
-    got = lax.all_to_all(sending, "dev", split_axis=0, concat_axis=0, tiled=True)
-    table = table_of(got_labels, got, grp_count * CT)
-    parts = lax.all_to_all(table, "grp", split_axis=0, concat_axis=0, tiled=True)
-    parts = parts.reshape(grp_count, CT, W, W).astype(jnp.float32)
-    return parts.sum(0).reshape(1, 1, CT, W, W)
+    parts = []
+    width = W // HALVES
+    for h in range(HALVES):
+        sending = device_tiles(
+            blocks[0, 0], pt, pieces, spots, where, block_cols[0, 0], tile_slot[0, 0],
+            dev_target, dev_count, h * width, width,
+        )
+        got = lax.all_to_all(sending, "dev", split_axis=0, concat_axis=0, tiled=True)
+        table = table_of(got_labels, got, grp_count * CT)
+        part = lax.all_to_all(table, "grp", split_axis=0, concat_axis=0, tiled=True)
+        part = part.reshape(grp_count, CT, W, width).astype(jnp.float32)
+        parts.append(part.sum(0))
+    return jnp.concatenate(parts, axis=-1).reshape(1, 1, CT, W, W)
 
 
 def solution(mesh):
     return jax.shard_map(
-        body,
+        layer,
         mesh=mesh,
         in_specs=(
             P("grp", "dev", None, None, None),

time: 258 us -> 260 us (level)
  waiting for transfers between devices: 156 us -> 120 us
  starting transfers between devices: 29.1 us -> 53.4 us
  Pallas kernels: 25.8 us -> 40.8 us
    all_to_all x3 -> x2, waiting for transfers between devices: 156 us -> 92.8 us  [the longest x1 89.9 us: layer(): lax.all_to_all(sending, 'dev', split_axis=0, concat_axis=0, tiled=True)]
    ppermute x0 -> x22, starting transfers between devices: none -> 35.9 us  [the longest x15 23.4 us: forward(): lax.ppermute(p, 'dev', along_x(step))]
    ppermute x0 -> x22, waiting for transfers between devices: none -> 27.1 us  [the longest x2 12.9 us: fetch(): new_up = lax.ppermute(up, 'dev', along_z(1))]
    pallas_call x1 -> x6, Pallas kernels: 19.7 us -> 34.8 us  [the longest x1 20.7 us: device_tiles(): pl.pallas_call(functools.partial(tiles_kernel, spots, first), out_shape=j...]
    all_to_all x3 -> x2, starting transfers between devices: 29.1 us -> 17.5 us  [the longest x1 8.85 us: fetch(): asks = lax.all_to_all(asked, 'dev', split_axis=0, concat_axis=0, tiled=True)]
    gather x1 -> x0, local copies, waits for them, and re-layouts: 3.54 us -> none  [body(): outgoing = panels[fetch_rows[0, 0]].reshape(dev_count, NCAP * BLOCK, W)]
    unnamed x9 -> x50, local copies, waits for them, and re-layouts: 0.62 us -> 3.7 us
  transfers between devices with their start and end apart: 3 -> 24, of which waited for: 2 -> 10; matrix products, arithmetic and copies ran while one was open for 3% -> 3% of each run, Pallas kernels for 8% -> 5%
where the time goes in v2:
time: 260 us; the launch traced here: 257 us
  waiting for transfers between devices  120 us (46%)
  starting transfers between devices  53.4 us (21%)
  Pallas kernels  40.8 us (16%)
  blocking collectives  31.7 us (12%)
  local copies, waits for them, and re-layouts  7.87 us (3%)
  other arithmetic  3.37 us (1%)
    all_to_all x1, waiting for transfers between devices, layer(): lax.all_to_all(sending, 'dev', split_axis=0, concat_axis=0, tiled=True)  89.9 us
    all_to_all x1, blocking collectives, layer(): part = lax.all_to_all(table, 'grp', split_axis=0, concat_axis=0, tiled=True)  31.7 us
    ppermute x15, starting transfers between devices, forward(): lax.ppermute(p, 'dev', along_x(step))  23.4 us
    pallas_call x1, Pallas kernels, device_tiles(): pl.pallas_call(functools.partial(tiles_kernel, spots, first), out_shape=j...  20.7 us
    pallas_call x5, Pallas kernels, pick(): pl.pallas_call(functools.partial(pick_kernel, n_x, ups), out_shape=[jax.S...  14.1 us
    ppermute x2, waiting for transfers between devices, fetch(): new_up = lax.ppermute(up, 'dev', along_z(1))  12.9 us
    ppermute x1, waiting for transfers between devices, fetch(): up = lax.ppermute(panels, 'dev', along_z(1))  9.32 us
    all_to_all x1, starting transfers between devices, fetch(): asks = lax.all_to_all(asked, 'dev', split_axis=0, concat_axis=0, tiled=True)  8.85 us
  transfers between devices with their start and end apart: 24, of which 10 were waited for; matrix products, arithmetic and copies ran while one was open for 3% of the time, Pallas kernels for 5%

profile of v2, /device:TPU:4, one launch (start us, length us, event | category | flops | bytes accessed | tf_op | source)
XLA Modules:
  0.0 257.2 jit_solution(12781642489503469054)
XLA Ops:
  0.0 1.9 collective-permute-start.3
  1.9 4.0 %collective-permute-start = (bf16[12,64,256]{2,1,0:T(8,128)(2,1)}, bf16[12,64,256]{2,1,0:T(8,128)(2,1)S(1)}, u32[]{:S(2)}, u32[]{:S(2)}) collective-permute-start(bf16[12,64,256]{2,1,0:T(8,128)(2,1)} %bitcast.42), channel_id=1, source_target_pairs={{0,28},{1,29},{2,30},{3,31},{4,0},{5,1},{6,2},{7,3},{8,4},{9,5},{1... | collective-permute-start | bytes 1179656 | tf_op jit(solution)/shard_map/ppermute | solution.py:73
  5.9 9.3 %collective-permute-done.3.refs_0_.refs_7_ = bf16[12,64,256]{2,1,0:T(8,128)(2,1)S(1)} collective-permute-done((bf16[12,64,256]{2,1,0:T(8,128)(2,1)}, bf16[12,64,256]{2,1,0:T(8,128)(2,1)S(1)}, u32[]{:S(2)}, u32[]{:S(2)}) %collective-permute-start.3) | collective-permute-done | bytes 393248 | tf_op jit(solution)/shard_map/ppermute | solution.py:72
  15.3 3.2 %collective-permute-start.1 = (bf16[12,64,256]{2,1,0:T(8,128)(2,1)S(1)}, bf16[12,64,256]{2,1,0:T(8,128)(2,1)S(1)}, u32[]{:S(2)}, u32[]{:S(2)}) collective-permute-start(bf16[12,64,256]{2,1,0:T(8,128)(2,1)S(1)} %collective-permute-done.refs_1_), channel_id=1, source_target_pairs={{0,28},{1,29},{2,30},{3,31},{4,0},{5,1},{6,2},{7,3},{8,4},{9,5},{1... | collective-permute-start | bytes 1179656 | tf_op jit(solution)/shard_map/ppermute | solution.py:81
  18.5 8.2 %collective-permute-done.4.refs_0_.refs_6_ = bf16[12,64,256]{2,1,0:T(8,128)(2,1)S(1)} collective-permute-done((bf16[12,64,256]{2,1,0:T(8,128)(2,1)S(1)}, bf16[12,64,256]{2,1,0:T(8,128)(2,1)S(1)}, u32[]{:S(2)}, u32[]{:S(2)}) %collective-permute-start.4) | collective-permute-done | bytes 393248 | tf_op jit(solution)/shard_map/ppermute | solution.py:80
  26.8 3.2 %collective-permute-start.2 = (bf16[12,64,256]{2,1,0:T(8,128)(2,1)S(1)}, bf16[12,64,256]{2,1,0:T(8,128)(2,1)S(1)}, u32[]{:S(2)}, u32[]{:S(2)}) collective-permute-start(bf16[12,64,256]{2,1,0:T(8,128)(2,1)S(1)} %collective-permute-done.1.refs_1_.refs_2_), channel_id=1, source_target_pairs={{0,28},{1,29},{2,30},{3,31},{4,0},{5,1},{6,2},{7,3},{8,4},{9,5},{1... | collective-permute-start | bytes 1179656 | tf_op jit(solution)/shard_map/ppermute | solution.py:81
  32.7 4.7 %collective-permute-done.5.refs_0_.refs_5_ = bf16[12,64,256]{2,1,0:T(8,128)(2,1)S(1)} collective-permute-done((bf16[12,64,256]{2,1,0:T(8,128)(2,1)S(1)}, bf16[12,64,256]{2,1,0:T(8,128)(2,1)S(1)}, u32[]{:S(2)}, u32[]{:S(2)}) %collective-permute-start.5) | collective-permute-done | bytes 393248 | tf_op jit(solution)/shard_map/ppermute | solution.py:80
  38.9 8.9 %all-to-all-start = ((s32[32,1,13]{2,1,0:T(1,128)}), s32[32,1,13]{2,1,0:T(1,128)S(1)}, u32[]{:S(2)}, u32[]{:S(2)}) async-start(s32[32,1,13]{2,1,0:T(1,128)} %bitcast.53), calls=%async_computation | async-start | bytes 32768 | tf_op jit(solution)/shard_map/all_to_all | solution.py:74
  47.8 2.7 %pick.5 = (bf16[3,64,256]{2,1,0:T(8,128)(2,1)}, bf16[3,64,256]{2,1,0:T(8,128)(2,1)}, bf16[3,64,256]{2,1,0:T(8,128)(2,1)}) custom-call(s32[32,13]{1,0:T(8,128)} %pad_add_fusion.asks_ref, bf16[12,64,256]{2,1,0:T(8,128)(2,1)} %bitcast.43), custom_call_target="tpu_custom_call" | custom-call | bytes 1500000 | tf_op jit(solution)/shard_map/pick/pallas_call | solution.py:38
  50.5 1.2 collective-permute-start.7
  52.5 2.9 %all-to-all-done = s32[32,1,13]{2,1,0:T(1,128)S(1)} async-done(((s32[32,1,13]{2,1,0:T(1,128)}), s32[32,1,13]{2,1,0:T(1,128)S(1)}, u32[]{:S(2)}, u32[]{:S(2)}) %all-to-all-start) | async-done | bytes 1696 | tf_op jit(solution)/shard_map/all_to_all | solution.py:74
  56.0 2.9 %pick.6 = (bf16[6,64,256]{2,1,0:T(8,128)(2,1)}, bf16[6,64,256]{2,1,0:T(8,128)(2,1)}, bf16[6,64,256]{2,1,0:T(8,128)(2,1)}) custom-call(s32[32,13]{1,0:T(8,128)} %bitcast.46, bf16[12,64,256]{2,1,0:T(8,128)(2,1)} %copy-done.5, bf16[12,64,256]{2,1,0:T(8,128)(2,1)} %copy-done.6), custom_call_target="tpu_custom_call" | custom-call | bytes 1500000 | tf_op jit(solution)/shard_map/pick/pallas_call | solution.py:38
  58.9 1.5 collective-permute-start.8
  60.9 1.3 copy_bitcast_fusion
  62.2 3.5 %collective-permute-start.17 = (bf16[3,64,256]{2,1,0:T(8,128)(2,1)}, bf16[3,64,256]{2,1,0:T(8,128)(2,1)S(1)}, u32[]{:S(2)}, u32[]{:S(2)}) collective-permute-start(bf16[3,64,256]{2,1,0:T(8,128)(2,1)} %get-tuple-element.30), channel_id=1, source_target_pairs={{0,2},{1,3},{2,0},{3,1},{4,6},{5,7},{6,4},{7,5},{8,10},{9,11},{10,... | collective-permute-start | bytes 294920 | tf_op jit(solution)/shard_map/ppermute | solution.py:66
  65.8 2.9 %pick.7 = (bf16[6,64,256]{2,1,0:T(8,128)(2,1)}, bf16[6,64,256]{2,1,0:T(8,128)(2,1)}, bf16[6,64,256]{2,1,0:T(8,128)(2,1)}) custom-call(s32[32,13]{1,0:T(8,128)} %bitcast.47, bf16[12,64,256]{2,1,0:T(8,128)(2,1)} %copy-done.7, bf16[12,64,256]{2,1,0:T(8,128)(2,1)} %copy-done.8), custom_call_target="tpu_custom_call" | custom-call | bytes 1500000 | tf_op jit(solution)/shard_map/pick/pallas_call | solution.py:38
  68.7 2.9 %pick.8 = (bf16[6,64,256]{2,1,0:T(8,128)(2,1)}, bf16[6,64,256]{2,1,0:T(8,128)(2,1)}, bf16[6,64,256]{2,1,0:T(8,128)(2,1)}) custom-call(s32[32,13]{1,0:T(8,128)} %bitcast.48, bf16[12,64,256]{2,1,0:T(8,128)(2,1)} %copy-done.1, bf16[12,64,256]{2,1,0:T(8,128)(2,1)} %copy-done.2), custom_call_target="tpu_custom_call" | custom-call | bytes 1500000 | tf_op jit(solution)/shard_map/pick/pallas_call | solution.py:38
  71.6 1.5 collective-permute-start.9
  73.7 4.7 %collective-permute-start.19 = (bf16[6,64,256]{2,1,0:T(8,128)(2,1)}, bf16[6,64,256]{2,1,0:T(8,128)(2,1)S(1)}, u32[]{:S(2)}, u32[]{:S(2)}) collective-permute-start(bf16[6,64,256]{2,1,0:T(8,128)(2,1)} %get-tuple-element.32), channel_id=1, source_target_pairs={{0,2},{1,3},{2,0},{3,1},{4,6},{5,7},{6,4},{7,5},{8,10},{9,11},{10,... | collective-permute-start | bytes 589832 | tf_op jit(solution)/shard_map/ppermute | solution.py:66
  80.7 2.7 %pick.9 = (bf16[3,64,256]{2,1,0:T(8,128)(2,1)}, bf16[3,64,256]{2,1,0:T(8,128)(2,1)}, bf16[3,64,256]{2,1,0:T(8,128)(2,1)}) custom-call(s32[32,13]{1,0:T(8,128)} %bitcast.50, bf16[12,64,256]{2,1,0:T(8,128)(2,1)} %copy-done.9), custom_call_target="tpu_custom_call" | custom-call | bytes 1500000 | tf_op jit(solution)/shard_map/pick/pallas_call | solution.py:38
  83.4 2.0 collective-permute-start.15
  85.5 3.1 %collective-permute-start.20 = (bf16[6,64,256]{2,1,0:T(8,128)(2,1)}, bf16[6,64,256]{2,1,0:T(8,128)(2,1)S(1)}, u32[]{:S(2)}, u32[]{:S(2)}) collective-permute-start(bf16[6,64,256]{2,1,0:T(8,128)(2,1)} %get-tuple-element.33), channel_id=1, source_target_pairs={{0,2},{1,3},{2,0},{3,1},{4,6},{5,7},{6,4},{7,5},{8,10},{9,11},{10,... | collective-permute-start | bytes 589832 | tf_op jit(solution)/shard_map/ppermute | solution.py:66
  89.6 0.9 collective-permute-start.16
  91.2 2.2 collective-permute-start.21
  93.9 2.0 collective-permute-done.20.refs_21_
  96.1 1.9 collective-permute-done.21.refs_22_
  98.6 20.7 %device_tiles.1 = bf16[32,256,256]{2,1,0:T(8,128)(2,1)} custom-call(s32[12,27]{1,0:T(8,128)} %get-tuple-element.38.cols_ref, s32[12,27]{1,0:T(8,128)} %get-tuple-element.37.slots_ref, s32[16]{0:T(128)} %copy-done.10, s32[96]{0:T(128)} %compare_select_fusion.4.where_ref, bf16[12,64,1728]{2,1,0:T(8,128)(2,1)} %bitcast.56, bf16[256,768]{1,0:T(8,128)(2,1)} %bitcast.52, ...), custom_call_target="tpu_custom_call" | custom-call | flops 8000000000 | bytes 20000000 | tf_op jit(solution)/shard_map/device_tiles/pallas_call | solution.py:187
  119.3 8.7 %all-to-all-start.1 = ((bf16[32,256,256]{2,1,0:T(8,128)(2,1)}), bf16[32,256,256]{2,1,0:T(8,128)(2,1)}, u32[]{:S(2)}, u32[]{:S(2)}) async-start(bf16[32,256,256]{2,1,0:T(8,128)(2,1)} %device_tiles.1), calls=%async_computation.1 | async-start | bytes 8388608 | tf_op jit(solution)/shard_map/all_to_all | solution.py:275
  128.6 89.9 %all-to-all-done.1.got_ref = bf16[32,256,256]{2,1,0:T(8,128)(2,1)} async-done(((bf16[32,256,256]{2,1,0:T(8,128)(2,1)}), bf16[32,256,256]{2,1,0:T(8,128)(2,1)}, u32[]{:S(2)}, u32[]{:S(2)}) %all-to-all-start.1) | async-done | bytes 4194336 | tf_op jit(solution)/shard_map/all_to_all | solution.py:275
  218.4 6.1 %table_of.1 = bf16[16,256,256]{2,1,0:T(8,128)(2,1)} custom-call(s32[32]{0:T(128)} %slice_reduce_fusion.labels_ref, bf16[32,256,256]{2,1,0:T(8,128)(2,1)} %all-to-all-done.1.got_ref), custom_call_target="tpu_custom_call" | custom-call | flops 2097152 | bytes 6000000 | tf_op jit(solution)/shard_map/table_of/pallas_call | solution.py:238
  224.5 31.7 %all_to_all.21 = bf16[16,256,256]{2,1,0:T(8,128)(2,1)S(1)} all-to-all(bf16[16,256,256]{2,1,0:T(8,128)(2,1)} %table_of.1), channel_id=1, replica_groups=mesh['grp'=8,'dev'=32] {'grp'}, dimensions={0} | all-to-all | bytes 4194304 | tf_op jit(solution)/shard_map/all_to_all | solution.py:277
  256.2 1.1 convert_reduce_fusion
  (94 shorter events, 13.0 us)
Async XLA Ops:
  0.0 78.5 %copy-start = (bf16[1,1,12,64,256]{4,3,2,1,0:T(8,128)(2,1)S(1)}, bf16[1,1,12,64,256]{4,3,2,1,0:T(8,128)(2,1)}, u32[]{:S(2)}) copy-start(bf16[1,1,12,64,256]{4,3,2,1,0:T(8,128)(2,1)} %param.8) | copy-start | bytes 1179652
  0.0 15.2 %collective-permute-start.3 = (bf16[12,64,256]{2,1,0:T(8,128)(2,1)}, bf16[12,64,256]{2,1,0:T(8,128)(2,1)S(1)}, u32[]{:S(2)}, u32[]{:S(2)}) collective-permute-start(bf16[12,64,256]{2,1,0:T(8,128)(2,1)} %bitcast.41), channel_id=1, source_target_pairs={{0,4},{1,5},{2,6},{3,7},{4,8},{5,9},{6,10},{7,11},{8,12},{9,13},{1... | collective-permute-start | bytes 1179656 | tf_op jit(solution)/shard_map/ppermute | solution.py:72
  1.9 13.3 %collective-permute-start = (bf16[12,64,256]{2,1,0:T(8,128)(2,1)}, bf16[12,64,256]{2,1,0:T(8,128)(2,1)S(1)}, u32[]{:S(2)}, u32[]{:S(2)}) collective-permute-start(bf16[12,64,256]{2,1,0:T(8,128)(2,1)} %bitcast.42), channel_id=1, source_target_pairs={{0,28},{1,29},{2,30},{3,31},{4,0},{5,1},{6,2},{7,3},{8,4},{9,5},{1... | collective-permute-start | bytes 1179656 | tf_op jit(solution)/shard_map/ppermute | solution.py:73
  15.3 40.2 %copy-start.5 = (bf16[12,64,256]{2,1,0:T(8,128)(2,1)}, bf16[12,64,256]{2,1,0:T(8,128)(2,1)S(1)}, u32[]{:S(2)}) copy-start(bf16[12,64,256]{2,1,0:T(8,128)(2,1)S(1)} %collective-permute-done.3.refs_0_.refs_7_) | copy-start | bytes 1179652
  15.3 11.5 %collective-permute-start.4 = (bf16[12,64,256]{2,1,0:T(8,128)(2,1)S(1)}, bf16[12,64,256]{2,1,0:T(8,128)(2,1)S(1)}, u32[]{:S(2)}, u32[]{:S(2)}) collective-permute-start(bf16[12,64,256]{2,1,0:T(8,128)(2,1)S(1)} %collective-permute-done.3.refs_0_.refs_7_), channel_id=1, source_target_pairs={{0,4},{1,5},{2,6},{3,7},{4,8},{5,9},{6,10},{7,11},{8,12},{9,13},{1... | collective-permute-start | bytes 1179656 | tf_op jit(solution)/shard_map/ppermute | solution.py:80
  15.3 40.1 %copy-start.6 = (bf16[12,64,256]{2,1,0:T(8,128)(2,1)}, bf16[12,64,256]{2,1,0:T(8,128)(2,1)S(1)}, u32[]{:S(2)}) copy-start(bf16[12,64,256]{2,1,0:T(8,128)(2,1)S(1)} %collective-permute-done.refs_1_) | copy-start | bytes 1179652
  15.3 11.5 %collective-permute-start.1 = (bf16[12,64,256]{2,1,0:T(8,128)(2,1)S(1)}, bf16[12,64,256]{2,1,0:T(8,128)(2,1)S(1)}, u32[]{:S(2)}, u32[]{:S(2)}) collective-permute-start(bf16[12,64,256]{2,1,0:T(8,128)(2,1)S(1)} %collective-permute-done.refs_1_), channel_id=1, source_target_pairs={{0,28},{1,29},{2,30},{3,31},{4,0},{5,1},{6,2},{7,3},{8,4},{9,5},{1... | collective-permute-start | bytes 1179656 | tf_op jit(solution)/shard_map/ppermute | solution.py:81
  26.7 39.0 %copy-start.7 = (bf16[12,64,256]{2,1,0:T(8,128)(2,1)}, bf16[12,64,256]{2,1,0:T(8,128)(2,1)S(1)}, u32[]{:S(2)}) copy-start(bf16[12,64,256]{2,1,0:T(8,128)(2,1)S(1)} %collective-permute-done.4.refs_0_.refs_6_) | copy-start | bytes 1179652
  26.7 10.6 %collective-permute-start.5 = (bf16[12,64,256]{2,1,0:T(8,128)(2,1)S(1)}, bf16[12,64,256]{2,1,0:T(8,128)(2,1)S(1)}, u32[]{:S(2)}, u32[]{:S(2)}) collective-permute-start(bf16[12,64,256]{2,1,0:T(8,128)(2,1)S(1)} %collective-permute-done.4.refs_0_.refs_6_), channel_id=1, source_target_pairs={{0,4},{1,5},{2,6},{3,7},{4,8},{5,9},{6,10},{7,11},{8,12},{9,13},{1... | collective-permute-start | bytes 1179656 | tf_op jit(solution)/shard_map/ppermute | solution.py:80
  26.8 39.0 %copy-start.8 = (bf16[12,64,256]{2,1,0:T(8,128)(2,1)}, bf16[12,64,256]{2,1,0:T(8,128)(2,1)S(1)}, u32[]{:S(2)}) copy-start(bf16[12,64,256]{2,1,0:T(8,128)(2,1)S(1)} %collective-permute-done.1.refs_1_.refs_2_) | copy-start | bytes 1179652
  26.8 10.6 %collective-permute-start.2 = (bf16[12,64,256]{2,1,0:T(8,128)(2,1)S(1)}, bf16[12,64,256]{2,1,0:T(8,128)(2,1)S(1)}, u32[]{:S(2)}, u32[]{:S(2)}) collective-permute-start(bf16[12,64,256]{2,1,0:T(8,128)(2,1)S(1)} %collective-permute-done.1.refs_1_.refs_2_), channel_id=1, source_target_pairs={{0,28},{1,29},{2,30},{3,31},{4,0},{5,1},{6,2},{7,3},{8,4},{9,5},{1... | collective-permute-start | bytes 1179656 | tf_op jit(solution)/shard_map/ppermute | solution.py:81
  37.4 31.3 %copy-start.1 = (bf16[12,64,256]{2,1,0:T(8,128)(2,1)}, bf16[12,64,256]{2,1,0:T(8,128)(2,1)S(1)}, u32[]{:S(2)}) copy-start(bf16[12,64,256]{2,1,0:T(8,128)(2,1)S(1)} %collective-permute-done.5.refs_0_.refs_5_) | copy-start | bytes 1179652
  37.4 31.3 %copy-start.2 = (bf16[12,64,256]{2,1,0:T(8,128)(2,1)}, bf16[12,64,256]{2,1,0:T(8,128)(2,1)S(1)}, u32[]{:S(2)}) copy-start(bf16[12,64,256]{2,1,0:T(8,128)(2,1)S(1)} %collective-permute-done.2.refs_1_.refs_3_) | copy-start | bytes 1179652
  37.4 41.0 %collective-permute-start.6 = (bf16[12,64,256]{2,1,0:T(8,128)(2,1)S(1)}, bf16[12,64,256]{2,1,0:T(8,128)(2,1)S(1)}, u32[]{:S(2)}, u32[]{:S(2)}) collective-permute-start(bf16[12,64,256]{2,1,0:T(8,128)(2,1)S(1)} %broadcast_select_fusion), channel_id=1, source_target_pairs={{0,4},{1,5},{2,6},{3,7},{4,8},{5,9},{6,10},{7,11},{8,12},{9,13},{1... | collective-permute-start | bytes 1179656 | tf_op jit(solution)/shard_map/ppermute | solution.py:90
  38.9 16.5 %all-to-all-start = ((s32[32,1,13]{2,1,0:T(1,128)}), s32[32,1,13]{2,1,0:T(1,128)S(1)}, u32[]{:S(2)}, u32[]{:S(2)}) async-start(s32[32,1,13]{2,1,0:T(1,128)} %bitcast.53), calls=%async_computation | async-start | bytes 32768 | tf_op jit(solution)/shard_map/all_to_all | solution.py:74
  50.5 11.8 %collective-permute-start.7 = (bf16[3,64,256]{2,1,0:T(8,128)(2,1)}, bf16[3,64,256]{2,1,0:T(8,128)(2,1)}, u32[]{:S(2)}, u32[]{:S(2)}) collective-permute-start(bf16[3,64,256]{2,1,0:T(8,128)(2,1)} %get-tuple-element.20), channel_id=1, source_target_pairs={{0,1},{1,2},{2,3},{3,0},{4,5},{5,6},{6,7},{7,4},{8,9},{9,10},{10,1... | collective-permute-start | bytes 294920 | tf_op jit(solution)/shard_map/ppermute | solution.py:66
  51.6 20.0 %collective-permute-start.12 = (bf16[3,64,256]{2,1,0:T(8,128)(2,1)}, bf16[3,64,256]{2,1,0:T(8,128)(2,1)}, u32[]{:S(2)}, u32[]{:S(2)}) collective-permute-start(bf16[3,64,256]{2,1,0:T(8,128)(2,1)} %get-tuple-element.25), channel_id=1, source_target_pairs={{0,3},{1,0},{2,1},{3,2},{4,7},{5,4},{6,5},{7,6},{8,11},{9,8},{10,9... | collective-permute-start | bytes 294920 | tf_op jit(solution)/shard_map/ppermute | solution.py:66
  58.9 14.2 %collective-permute-start.8 = (bf16[6,64,256]{2,1,0:T(8,128)(2,1)}, bf16[6,64,256]{2,1,0:T(8,128)(2,1)S(1)}, u32[]{:S(2)}, u32[]{:S(2)}) collective-permute-start(bf16[6,64,256]{2,1,0:T(8,128)(2,1)} %get-tuple-element.21), channel_id=1, source_target_pairs={{0,1},{1,2},{2,3},{3,0},{4,5},{5,6},{6,7},{7,4},{8,9},{9,10},{10,1... | collective-permute-start | bytes 589832 | tf_op jit(solution)/shard_map/ppermute | solution.py:66
  60.4 13.4 %collective-permute-start.13 = (bf16[6,64,256]{2,1,0:T(8,128)(2,1)}, bf16[6,64,256]{2,1,0:T(8,128)(2,1)S(1)}, u32[]{:S(2)}, u32[]{:S(2)}) collective-permute-start(bf16[6,64,256]{2,1,0:T(8,128)(2,1)} %get-tuple-element.26), channel_id=1, source_target_pairs={{0,3},{1,0},{2,1},{3,2},{4,7},{5,4},{6,5},{7,6},{8,11},{9,8},{10,9... | collective-permute-start | bytes 589832 | tf_op jit(solution)/shard_map/ppermute | solution.py:66
  62.2 9.4 %collective-permute-start.17 = (bf16[3,64,256]{2,1,0:T(8,128)(2,1)}, bf16[3,64,256]{2,1,0:T(8,128)(2,1)S(1)}, u32[]{:S(2)}, u32[]{:S(2)}) collective-permute-start(bf16[3,64,256]{2,1,0:T(8,128)(2,1)} %get-tuple-element.30), channel_id=1, source_target_pairs={{0,2},{1,3},{2,0},{3,1},{4,6},{5,7},{6,4},{7,5},{8,10},{9,11},{10,... | collective-permute-start | bytes 294920 | tf_op jit(solution)/shard_map/ppermute | solution.py:66
  71.6 11.8 %collective-permute-start.18 = (bf16[6,64,256]{2,1,0:T(8,128)(2,1)}, bf16[6,64,256]{2,1,0:T(8,128)(2,1)S(1)}, u32[]{:S(2)}, u32[]{:S(2)}) collective-permute-start(bf16[6,64,256]{2,1,0:T(8,128)(2,1)} %get-tuple-element.31), channel_id=1, source_target_pairs={{0,2},{1,3},{2,0},{3,1},{4,6},{5,7},{6,4},{7,5},{8,10},{9,11},{10,... | collective-permute-start | bytes 589832 | tf_op jit(solution)/shard_map/ppermute | solution.py:66
  71.6 26.3 %copy-start.20 = (bf16[3,64,256]{2,1,0:T(8,128)(2,1)}, bf16[3,64,256]{2,1,0:T(8,128)(2,1)S(1)}, u32[]{:S(2)}) copy-start(bf16[3,64,256]{2,1,0:T(8,128)(2,1)S(1)} %collective-permute-done.17.refs_18_) | copy-start | bytes 294916
  71.6 13.8 %collective-permute-start.9 = (bf16[6,64,256]{2,1,0:T(8,128)(2,1)}, bf16[6,64,256]{2,1,0:T(8,128)(2,1)S(1)}, u32[]{:S(2)}, u32[]{:S(2)}) collective-permute-start(bf16[6,64,256]{2,1,0:T(8,128)(2,1)} %get-tuple-element.22), channel_id=1, source_target_pairs={{0,1},{1,2},{2,3},{3,0},{4,5},{5,6},{6,7},{7,4},{8,9},{9,10},{10,1... | collective-permute-start | bytes 589832 | tf_op jit(solution)/shard_map/ppermute | solution.py:66
  73.1 15.4 %collective-permute-start.14 = (bf16[6,64,256]{2,1,0:T(8,128)(2,1)}, bf16[6,64,256]{2,1,0:T(8,128)(2,1)S(1)}, u32[]{:S(2)}, u32[]{:S(2)}) collective-permute-start(bf16[6,64,256]{2,1,0:T(8,128)(2,1)} %get-tuple-element.27), channel_id=1, source_target_pairs={{0,3},{1,0},{2,1},{3,2},{4,7},{5,4},{6,5},{7,6},{8,11},{9,8},{10,9... | collective-permute-start | bytes 589832 | tf_op jit(solution)/shard_map/ppermute | solution.py:66
  73.7 15.9 %collective-permute-start.19 = (bf16[6,64,256]{2,1,0:T(8,128)(2,1)}, bf16[6,64,256]{2,1,0:T(8,128)(2,1)S(1)}, u32[]{:S(2)}, u32[]{:S(2)}) collective-permute-start(bf16[6,64,256]{2,1,0:T(8,128)(2,1)} %get-tuple-element.32), channel_id=1, source_target_pairs={{0,2},{1,3},{2,0},{3,1},{4,6},{5,7},{6,4},{7,5},{8,10},{9,11},{10,... | collective-permute-start | bytes 589832 | tf_op jit(solution)/shard_map/ppermute | solution.py:66
  78.4 12.8 %collective-permute-start.10 = (bf16[6,64,256]{2,1,0:T(8,128)(2,1)}, bf16[6,64,256]{2,1,0:T(8,128)(2,1)S(1)}, u32[]{:S(2)}, u32[]{:S(2)}) collective-permute-start(bf16[6,64,256]{2,1,0:T(8,128)(2,1)} %get-tuple-element.23), channel_id=1, source_target_pairs={{0,1},{1,2},{2,3},{3,0},{4,5},{5,6},{6,7},{7,4},{8,9},{9,10},{10,1... | collective-permute-start | bytes 589832 | tf_op jit(solution)/shard_map/ppermute | solution.py:66
  83.4 10.5 %collective-permute-start.15 = (bf16[6,64,256]{2,1,0:T(8,128)(2,1)}, bf16[6,64,256]{2,1,0:T(8,128)(2,1)S(1)}, u32[]{:S(2)}, u32[]{:S(2)}) collective-permute-start(bf16[6,64,256]{2,1,0:T(8,128)(2,1)} %get-tuple-element.28), channel_id=1, source_target_pairs={{0,3},{1,0},{2,1},{3,2},{4,7},{5,4},{6,5},{7,6},{8,11},{9,8},{10,9... | collective-permute-start | bytes 589832 | tf_op jit(solution)/shard_map/ppermute | solution.py:66
  85.5 10.4 %collective-permute-start.20 = (bf16[6,64,256]{2,1,0:T(8,128)(2,1)}, bf16[6,64,256]{2,1,0:T(8,128)(2,1)S(1)}, u32[]{:S(2)}, u32[]{:S(2)}) collective-permute-start(bf16[6,64,256]{2,1,0:T(8,128)(2,1)} %get-tuple-element.33), channel_id=1, source_target_pairs={{0,2},{1,3},{2,0},{3,1},{4,6},{5,7},{6,4},{7,5},{8,10},{9,11},{10,... | collective-permute-start | bytes 589832 | tf_op jit(solution)/shard_map/ppermute | solution.py:66
  88.5 7.5 %collective-permute-start.11 = (bf16[3,64,256]{2,1,0:T(8,128)(2,1)}, bf16[3,64,256]{2,1,0:T(8,128)(2,1)S(1)}, u32[]{:S(2)}, u32[]{:S(2)}) collective-permute-start(bf16[3,64,256]{2,1,0:T(8,128)(2,1)} %get-tuple-element.24), channel_id=1, source_target_pairs={{0,1},{1,2},{2,3},{3,0},{4,5},{5,6},{6,7},{7,4},{8,9},{9,10},{10,1... | collective-permute-start | bytes 294920 | tf_op jit(solution)/shard_map/ppermute | solution.py:66
  89.6 6.4 %collective-permute-start.16 = (bf16[3,64,256]{2,1,0:T(8,128)(2,1)}, bf16[3,64,256]{2,1,0:T(8,128)(2,1)S(1)}, u32[]{:S(2)}, u32[]{:S(2)}) collective-permute-start(bf16[3,64,256]{2,1,0:T(8,128)(2,1)} %get-tuple-element.29), channel_id=1, source_target_pairs={{0,3},{1,0},{2,1},{3,2},{4,7},{5,4},{6,5},{7,6},{8,11},{9,8},{10,9... | collective-permute-start | bytes 294920 | tf_op jit(solution)/shard_map/ppermute | solution.py:66
  91.2 6.7 %collective-permute-start.21 = (bf16[3,64,256]{2,1,0:T(8,128)(2,1)}, bf16[3,64,256]{2,1,0:T(8,128)(2,1)S(1)}, u32[]{:S(2)}, u32[]{:S(2)}) collective-permute-start(bf16[3,64,256]{2,1,0:T(8,128)(2,1)} %get-tuple-element.34), channel_id=1, source_target_pairs={{0,2},{1,3},{2,0},{3,1},{4,6},{5,7},{6,4},{7,5},{8,10},{9,11},{10,... | collective-permute-start | bytes 294920 | tf_op jit(solution)/shard_map/ppermute | solution.py:66
  119.3 99.2 %all-to-all-start.1 = ((bf16[32,256,256]{2,1,0:T(8,128)(2,1)}), bf16[32,256,256]{2,1,0:T(8,128)(2,1)}, u32[]{:S(2)}, u32[]{:S(2)}) async-start(bf16[32,256,256]{2,1,0:T(8,128)(2,1)} %device_tiles.1), calls=%async_computation.1 | async-start | bytes 8388608 | tf_op jit(solution)/shard_map/all_to_all | solution.py:275
  (16 other events, 123.5 us)

commit v3 on v2

--- a/solution.py
+++ b/solution.py
@@ -16,7 +16,7 @@
 NCAP = 3
 LT = 16
 PAIR = 2 * BLOCK
-HALVES = 1
+HALVES = 2
 STEPS = (1, -1, 2)
 
 
@@ -34,16 +34,13 @@
 
 def pick(asks, n_x, ups, blocks):
     shape = (len(blocks) * NCAP,) + blocks[0].shape[1:]
-    whole = lambda shape: pl.BlockSpec(shape, lambda i, *_: (0,) * len(shape))
+    vmem = pl.BlockSpec(memory_space=pltpu.VMEM)
     return pl.pallas_call(
         functools.partial(pick_kernel, n_x, ups),
         out_shape=[jax.ShapeDtypeStruct(shape, blocks[0].dtype)] * len(STEPS),
-        grid_spec=pltpu.PrefetchScalarGridSpec(
-            num_scalar_prefetch=1,
-            grid=(1,),
-            in_specs=[whole(b.shape) for b in blocks],
-            out_specs=[whole(shape)] * len(STEPS),
-        ),
+        in_specs=[pl.BlockSpec(memory_space=pltpu.SMEM)] + [vmem] * len(blocks),
+        out_specs=[vmem] * len(STEPS),
+        compiler_params=pltpu.CompilerParams(vmem_limit_bytes=16 << 20),
         cost_estimate=pl.CostEstimate(flops=0, bytes_accessed=1_500_000, transcendentals=0),
         name="pick",
     )(asks, *blocks)
@@ -171,14 +168,18 @@
 
     @pl.when(row == R - 1)
     def _():
-        @pl.loop(0, LT)
-        def _(t):
-            near = near_ref[t]
+        beside = W // width
+
+        @pl.loop(0, LT // beside)
+        def _(u):
+            near = jnp.concatenate([near_ref[u * beside + i] for i in range(beside)], axis=1)
             high = near.astype(jnp.bfloat16)
             low = (near - high.astype(jnp.float32)).astype(jnp.bfloat16)
             tile = jnp.dot(pt_ref[...], high, preferred_element_type=jnp.float32)
             tile += jnp.dot(pt_ref[...], low, preferred_element_type=jnp.float32)
-            out_ref[places_ref[t]] = tile.astype(jnp.bfloat16)
+            tile = tile.astype(jnp.bfloat16)
+            for i in range(beside):
+                out_ref[places_ref[u * beside + i]] = tile[:, i * width : (i + 1) * width]
 
 
 def device_tiles(blocks, pt, pieces, spots, where, cols, slots, places, n_places, first, width):
@@ -214,8 +215,10 @@
     )(cols, slots, places, where, blocks, pt, *pieces)
 
 
-def table_kernel(labels_ref, got_ref, table_ref, sum_ref):
-    spread = table_ref.shape[0]
+def table_kernel(labels_ref, got_ref, *refs):
+    out_refs, sum_ref = refs[:-1], refs[-1]
+    spread = sum_ref.shape[0] - 1
+    each = spread // len(out_refs)
 
     @pl.loop(0, spread)
     def _(t):
@@ -227,22 +230,24 @@
         at = jnp.where(label < 0, spread, label)
         sum_ref[at] += got_ref[s].astype(jnp.float32)
 
-    @pl.loop(0, spread)
-    def _(t):
-        table_ref[t] = sum_ref[t].astype(table_ref.dtype)
-
-
-def table_of(labels, got, spread):
+    for i, out_ref in enumerate(out_refs):
+
+        @pl.loop(0, each)
+        def _(t):
+            out_ref[t] = sum_ref[i * each + t].astype(out_ref.dtype)
+
+
+def table_of(labels, got, spread, pieces):
     n, _, width = got.shape
-    rows = 64
+    rows, each = 64, spread // pieces
     return pl.pallas_call(
         table_kernel,
-        out_shape=jax.ShapeDtypeStruct((spread, W, width), jnp.bfloat16),
+        out_shape=[jax.ShapeDtypeStruct((each, W, width), jnp.bfloat16)] * pieces,
         grid_spec=pltpu.PrefetchScalarGridSpec(
             num_scalar_prefetch=1,
             grid=(W // rows,),
             in_specs=[pl.BlockSpec((n, rows, width), lambda i, *_: (0, i, 0))],
-            out_specs=pl.BlockSpec((spread, rows, width), lambda i, *_: (0, i, 0)),
+            out_specs=[pl.BlockSpec((each, rows, width), lambda i, *_: (0, i, 0))] * pieces,
             scratch_shapes=[pltpu.VMEM((spread + 1, rows, width), jnp.float32)],
         ),
         compiler_params=pltpu.CompilerParams(dimension_semantics=("arbitrary",)),
@@ -251,6 +256,22 @@
         ),
         name="table_of",
     )(labels, got)
+
+
+def sum_over_groups(labels, got, spread, spread_out):
+    groups = lax.axis_size("grp")
+    if not spread_out:
+        (table,) = table_of(labels, got, spread, 1)
+        parts = lax.all_to_all(table, "grp", split_axis=0, concat_axis=0, tiled=True)
+        parts = parts.reshape(groups, CT, W, got.shape[-1])
+        return parts.astype(jnp.float32).sum(0)
+    from_here = (labels - lax.axis_index("grp") * CT) % spread
+    pieces = table_of(jnp.where(labels < 0, -1, from_here), got, spread, groups)
+    total = pieces[0].astype(jnp.float32)
+    for i in range(1, groups):
+        pairs = [(g, (g + i) % groups) for g in range(groups)]
+        total += lax.ppermute(pieces[i], "grp", pairs).astype(jnp.float32)
+    return total
 
 
 def layer(blocks, prolong, block_cols, fetch_rows, tile_slot, tile_owner, tile_place):
@@ -273,10 +294,8 @@
             dev_target, dev_count, h * width, width,
         )
         got = lax.all_to_all(sending, "dev", split_axis=0, concat_axis=0, tiled=True)
-        table = table_of(got_labels, got, grp_count * CT)
-        part = lax.all_to_all(table, "grp", split_axis=0, concat_axis=0, tiled=True)
-        part = part.reshape(grp_count, CT, W, width).astype(jnp.float32)
-        parts.append(part.sum(0))
+        last = h == HALVES - 1
+        parts.append(sum_over_groups(got_labels, got, grp_count * CT, not last))
     return jnp.concatenate(parts, axis=-1).reshape(1, 1, CT, W, W)
 
 

time: 260 us -> 255 us (0.981)
  blocking collectives: 31.7 us -> 0 us
  starting transfers between devices: 53.4 us -> 75.4 us
  Pallas kernels: 40.8 us -> 49.5 us
  waiting for transfers between devices: 120 us -> 113 us
    all_to_all x1 -> x0, blocking collectives: 31.7 us -> none  [layer(): part = lax.all_to_all(table, 'grp', split_axis=0, concat_axis=0, tiled=True)]
    all_to_all x1 -> x2, waiting for transfers between devices: 89.9 us -> 73.3 us  [layer(): lax.all_to_all(sending, 'dev', split_axis=0, concat_axis=0, tiled=True)]
    ppermute x0 -> x7, starting transfers between devices: none -> 11 us  [sum_over_groups(): total += lax.ppermute(pieces[i], 'grp', pairs).astype(jnp.float32)]
    pallas_call x1 -> x2, Pallas kernels: 20.7 us -> 31.5 us  [device_tiles(): pl.pallas_call(functools.partial(tiles_kernel, spots, first), out_shape=j...]
    ppermute x0 -> x7, waiting for transfers between devices: none -> 8.28 us  [sum_over_groups(): total += lax.ppermute(pieces[i], 'grp', pairs).astype(jnp.float32)]
    pallas_call x5, Pallas kernels: 14.1 us -> 7.41 us  [pick(): pl.pallas_call(functools.partial(pick_kernel, n_x, ups), out_shape=[jax.S...]
    pallas_call x1 -> x2, Pallas kernels: 6.06 us -> 10.6 us  [table_of(): pl.pallas_call(table_kernel, out_shape=[jax.ShapeDtypeStruct((each, W, wi...]
    all_to_all x0 -> x1, starting transfers between devices: none -> 4.46 us  [sum_over_groups(): lax.all_to_all(table, 'grp', split_axis=0, concat_axis=0, tiled=True)]
  transfers between devices with their start and end apart: 24 -> 33, of which waited for: 10 -> 13; matrix products, arithmetic and copies ran while one was open for 3% -> 3% of each run, Pallas kernels for 5% -> 13%
where the time goes in v3:
time: 255 us; the launch traced here: 251 us
  waiting for transfers between devices  113 us (44%)
  starting transfers between devices  75.4 us (30%)
  Pallas kernels  49.5 us (19%)
  local copies, waits for them, and re-layouts  7.16 us (3%)
  other arithmetic  5.73 us (2%)
    all_to_all x2, waiting for transfers between devices, layer(): lax.all_to_all(sending, 'dev', split_axis=0, concat_axis=0, tiled=True)  73.3 us
    pallas_call x2, Pallas kernels, device_tiles(): pl.pallas_call(functools.partial(tiles_kernel, spots, first), out_shape=j...  31.5 us
    ppermute x15, starting transfers between devices, forward(): lax.ppermute(p, 'dev', along_x(step))  25.6 us
    ppermute x2, waiting for transfers between devices, fetch(): new_up = lax.ppermute(up, 'dev', along_z(1))  13.9 us
    all_to_all x2, starting transfers between devices, layer(): lax.all_to_all(sending, 'dev', split_axis=0, concat_axis=0, tiled=True)  13.1 us
    ppermute x7, starting transfers between devices, sum_over_groups(): total += lax.ppermute(pieces[i], 'grp', pairs).astype(jnp.float32)  11 us
    pallas_call x2, Pallas kernels, table_of(): pl.pallas_call(table_kernel, out_shape=[jax.ShapeDtypeStruct((each, W, wi...  10.6 us
    ppermute x1, waiting for transfers between devices, fetch(): up = lax.ppermute(panels, 'dev', along_z(1))  9.23 us
  transfers between devices with their start and end apart: 33, of which 13 were waited for; matrix products, arithmetic and copies ran while one was open for 3% of the time, Pallas kernels for 13%

profile of v3, /device:TPU:4, one launch (start us, length us, event | category | flops | bytes accessed | tf_op | source)
XLA Modules:
  0.0 250.8 jit_solution(13931086239862527682)
XLA Ops:
  0.0 1.9 collective-permute-start.3
  1.9 4.0 %collective-permute-start = (bf16[12,64,256]{2,1,0:T(8,128)(2,1)}, bf16[12,64,256]{2,1,0:T(8,128)(2,1)S(1)}, u32[]{:S(2)}, u32[]{:S(2)}) collective-permute-start(bf16[12,64,256]{2,1,0:T(8,128)(2,1)} %bitcast.42), channel_id=1, source_target_pairs={{0,28},{1,29},{2,30},{3,31},{4,0},{5,1},{6,2},{7,3},{8,4},{9,5},{1... | collective-permute-start | bytes 1179656 | tf_op jit(solution)/shard_map/ppermute | solution.py:70
  5.9 9.2 %collective-permute-done.3.refs_0_.refs_7_ = bf16[12,64,256]{2,1,0:T(8,128)(2,1)S(1)} collective-permute-done((bf16[12,64,256]{2,1,0:T(8,128)(2,1)}, bf16[12,64,256]{2,1,0:T(8,128)(2,1)S(1)}, u32[]{:S(2)}, u32[]{:S(2)}) %collective-permute-start.3) | collective-permute-done | bytes 393248 | tf_op jit(solution)/shard_map/ppermute | solution.py:69
  15.2 3.2 %collective-permute-start.1 = (bf16[12,64,256]{2,1,0:T(8,128)(2,1)S(1)}, bf16[12,64,256]{2,1,0:T(8,128)(2,1)S(1)}, u32[]{:S(2)}, u32[]{:S(2)}) collective-permute-start(bf16[12,64,256]{2,1,0:T(8,128)(2,1)S(1)} %collective-permute-done.refs_1_), channel_id=1, source_target_pairs={{0,28},{1,29},{2,30},{3,31},{4,0},{5,1},{6,2},{7,3},{8,4},{9,5},{1... | collective-permute-start | bytes 1179656 | tf_op jit(solution)/shard_map/ppermute | solution.py:78
  18.4 8.2 %collective-permute-done.4.refs_0_.refs_6_ = bf16[12,64,256]{2,1,0:T(8,128)(2,1)S(1)} collective-permute-done((bf16[12,64,256]{2,1,0:T(8,128)(2,1)S(1)}, bf16[12,64,256]{2,1,0:T(8,128)(2,1)S(1)}, u32[]{:S(2)}, u32[]{:S(2)}) %collective-permute-start.4) | collective-permute-done | bytes 393248 | tf_op jit(solution)/shard_map/ppermute | solution.py:77
  26.7 3.2 %collective-permute-start.2 = (bf16[12,64,256]{2,1,0:T(8,128)(2,1)S(1)}, bf16[12,64,256]{2,1,0:T(8,128)(2,1)S(1)}, u32[]{:S(2)}, u32[]{:S(2)}) collective-permute-start(bf16[12,64,256]{2,1,0:T(8,128)(2,1)S(1)} %collective-permute-done.1.refs_1_.refs_2_), channel_id=1, source_target_pairs={{0,28},{1,29},{2,30},{3,31},{4,0},{5,1},{6,2},{7,3},{8,4},{9,5},{1... | collective-permute-start | bytes 1179656 | tf_op jit(solution)/shard_map/ppermute | solution.py:78
  31.6 5.7 %collective-permute-done.5.refs_0_.refs_5_ = bf16[12,64,256]{2,1,0:T(8,128)(2,1)S(1)} collective-permute-done((bf16[12,64,256]{2,1,0:T(8,128)(2,1)S(1)}, bf16[12,64,256]{2,1,0:T(8,128)(2,1)S(1)}, u32[]{:S(2)}, u32[]{:S(2)}) %collective-permute-start.5) | collective-permute-done | bytes 393248 | tf_op jit(solution)/shard_map/ppermute | solution.py:77
  38.9 9.0 %all-to-all-start = ((s32[32,1,13]{2,1,0:T(1,128)}), s32[32,1,13]{2,1,0:T(1,128)S(1)}, u32[]{:S(2)}, u32[]{:S(2)}) async-start(s32[32,1,13]{2,1,0:T(1,128)} %bitcast.5), calls=%async_computation | async-start | bytes 32768 | tf_op jit(solution)/shard_map/all_to_all | solution.py:71
  48.8 1.7 pick.5
  52.5 3.0 %all-to-all-done = s32[32,1,13]{2,1,0:T(1,128)S(1)} async-done(((s32[32,1,13]{2,1,0:T(1,128)}), s32[32,1,13]{2,1,0:T(1,128)S(1)}, u32[]{:S(2)}, u32[]{:S(2)}) %all-to-all-start) | async-done | bytes 1696 | tf_op jit(solution)/shard_map/all_to_all | solution.py:71
  59.8 3.5 %collective-permute-start.17 = (bf16[3,64,256]{2,1,0:T(8,128)(2,1)}, bf16[3,64,256]{2,1,0:T(8,128)(2,1)S(1)}, u32[]{:S(2)}, u32[]{:S(2)}) collective-permute-start(bf16[3,64,256]{2,1,0:T(8,128)(2,1)} %get-tuple-element.38), channel_id=1, source_target_pairs={{0,2},{1,3},{2,0},{3,1},{4,6},{5,7},{6,4},{7,5},{8,10},{9,11},{10,... | collective-permute-start | bytes 294920 | tf_op jit(solution)/shard_map/ppermute | solution.py:63
  63.3 1.7 pick.7
  69.4 4.7 %collective-permute-start.19 = (bf16[6,64,256]{2,1,0:T(8,128)(2,1)}, bf16[6,64,256]{2,1,0:T(8,128)(2,1)S(1)}, u32[]{:S(2)}, u32[]{:S(2)}) collective-permute-start(bf16[6,64,256]{2,1,0:T(8,128)(2,1)} %get-tuple-element.40), channel_id=1, source_target_pairs={{0,2},{1,3},{2,0},{3,1},{4,6},{5,7},{6,4},{7,5},{8,10},{9,11},{10,... | collective-permute-start | bytes 589832 | tf_op jit(solution)/shard_map/ppermute | solution.py:63
  76.6 2.1 collective-permute-start.15
  78.7 4.3 %collective-permute-start.20 = (bf16[6,64,256]{2,1,0:T(8,128)(2,1)S(1)}, bf16[6,64,256]{2,1,0:T(8,128)(2,1)S(1)}, u32[]{:S(2)}, u32[]{:S(2)}) collective-permute-start(bf16[6,64,256]{2,1,0:T(8,128)(2,1)S(1)} %get-tuple-element.41), channel_id=1, source_target_pairs={{0,2},{1,3},{2,0},{3,1},{4,6},{5,7},{6,4},{7,5},{8,10},{9,11},{10,... | collective-permute-start | bytes 589832 | tf_op jit(solution)/shard_map/ppermute | solution.py:63
  83.0 2.3 collective-permute-start.11
  86.9 2.4 collective-permute-start.21
  91.3 2.1 collective-permute-done.21.refs_22_
  94.0 15.7 %device_tiles.3 = bf16[32,256,128]{2,1,0:T(8,128)(2,1)} custom-call(s32[12,27]{1,0:T(8,128)} %get-tuple-element.54.cols_ref, s32[12,27]{1,0:T(8,128)} %get-tuple-element.53.slots_ref, s32[16]{0:T(128)} %copy-done.14, s32[96]{0:T(128)} %compare_select_fusion.6.where_ref, bf16[12,64,1728]{2,1,0:T(8,128)(2,1)} %bitcast.58, bf16[256,768]{1,0:T(8,128)(2,1)} %bitcast.54, ...), custom_call_target="tpu_custom_call" | custom-call | flops 4000000000 | bytes 10000000 | tf_op jit(solution)/shard_map/device_tiles/pallas_call | solution.py:188
  109.7 6.8 %all-to-all-start.2 = ((bf16[32,256,128]{2,1,0:T(8,128)(2,1)}), bf16[32,256,128]{2,1,0:T(8,128)(2,1)S(1)}, u32[]{:S(2)}, u32[]{:S(2)}) async-start(bf16[32,256,128]{2,1,0:T(8,128)(2,1)} %device_tiles.3), calls=%async_computation.2 | async-start | bytes 4194304 | tf_op jit(solution)/shard_map/all_to_all | solution.py:296
  116.6 15.8 %device_tiles.2 = bf16[32,256,128]{2,1,0:T(8,128)(2,1)} custom-call(s32[12,27]{1,0:T(8,128)} %get-tuple-element.54.cols_ref, s32[12,27]{1,0:T(8,128)} %get-tuple-element.53.slots_ref, s32[16]{0:T(128)} %copy-done.14, s32[96]{0:T(128)} %compare_select_fusion.6.where_ref, bf16[12,64,1728]{2,1,0:T(8,128)(2,1)} %bitcast.59, bf16[256,768]{1,0:T(8,128)(2,1)} %bitcast.55, ...), custom_call_target="tpu_custom_call" | custom-call | flops 4000000000 | bytes 10000000 | tf_op jit(solution)/shard_map/device_tiles/pallas_call | solution.py:188
  132.4 32.0 %all-to-all-done.2.got_ref = bf16[32,256,128]{2,1,0:T(8,128)(2,1)S(1)} async-done(((bf16[32,256,128]{2,1,0:T(8,128)(2,1)}), bf16[32,256,128]{2,1,0:T(8,128)(2,1)S(1)}, u32[]{:S(2)}, u32[]{:S(2)}) %all-to-all-start.2) | async-done | bytes 2097184 | tf_op jit(solution)/shard_map/all_to_all | solution.py:296
  165.7 6.3 %all-to-all-start.1 = ((bf16[32,256,128]{2,1,0:T(8,128)(2,1)}), bf16[32,256,128]{2,1,0:T(8,128)(2,1)}, u32[]{:S(2)}, u32[]{:S(2)}) async-start(bf16[32,256,128]{2,1,0:T(8,128)(2,1)} %device_tiles.2), calls=%async_computation.1 | async-start | bytes 4194304 | tf_op jit(solution)/shard_map/all_to_all | solution.py:296
  172.6 5.4 %table_of.3 = bf16[16,256,128]{2,1,0:T(8,128)(2,1)} custom-call(s32[32]{0:T(128)} %slice_reduce_fusion.labels_ref, bf16[32,256,128]{2,1,0:T(8,128)(2,1)} %copy-done.10), custom_call_target="tpu_custom_call" | custom-call | flops 1048576 | bytes 3000000 | tf_op jit(solution)/shard_map/table_of/pallas_call | solution.py:243
  178.0 41.3 %all-to-all-done.1.got_ref = bf16[32,256,128]{2,1,0:T(8,128)(2,1)} async-done(((bf16[32,256,128]{2,1,0:T(8,128)(2,1)}), bf16[32,256,128]{2,1,0:T(8,128)(2,1)}, u32[]{:S(2)}, u32[]{:S(2)}) %all-to-all-start.1) | async-done | bytes 2097184 | tf_op jit(solution)/shard_map/all_to_all | solution.py:296
  219.3 4.5 %all-to-all-start.3 = ((bf16[16,256,128]{2,1,0:T(8,128)(2,1)}), bf16[16,256,128]{2,1,0:T(8,128)(2,1)S(1)}, u32[]{:S(2)}, u32[]{:S(2)}) async-start(bf16[16,256,128]{2,1,0:T(8,128)(2,1)} %table_of.3), calls=%async_computation.3 | async-start | bytes 2097152 | tf_op jit(solution)/shard_map/all_to_all | solution.py:265
  224.4 5.1 %table_of.2 = (bf16[2,256,128]{2,1,0:T(8,128)(2,1)}, bf16[2,256,128]{2,1,0:T(8,128)(2,1)}, bf16[2,256,128]{2,1,0:T(8,128)(2,1)}, bf16[2,256,128]{2,1,0:T(8,128)(...) custom-call(s32[32]{0:T(128)} %compare_select_fusion.7.labels_ref, ...), custom_call_target="tpu_custom_call" | custom-call | flops 1048576 | bytes 3000000 | tf_op jit(solution)/shard_map/table_of/pallas_call | solution.py:243
  231.7 2.0 collective-permute-start.24
  233.6 2.1 collective-permute-start.25
  237.3 4.5 %collective-permute-done.22 = bf16[2,256,128]{2,1,0:T(8,128)(2,1)S(1)} collective-permute-done((bf16[2,256,128]{2,1,0:T(8,128)(2,1)}, bf16[2,256,128]{2,1,0:T(8,128)(2,1)S(1)}, u32[]{:S(2)}, u32[]{:S(2)}) %collective-permute-start.22) | collective-permute-done | bytes 131104 | tf_op jit(solution)/shard_map/ppermute | solution.py:273
  242.6 2.5 collective-permute-start.28
  245.1 2.5 %collective-permute-done.24 = bf16[2,256,128]{2,1,0:T(8,128)(2,1)S(1)} collective-permute-done((bf16[2,256,128]{2,1,0:T(8,128)(2,1)}, bf16[2,256,128]{2,1,0:T(8,128)(2,1)S(1)}, u32[]{:S(2)}, u32[]{:S(2)}) %collective-permute-start.24) | collective-permute-done | bytes 131104 | tf_op jit(solution)/shard_map/ppermute | solution.py:273
  (120 shorter events, 31.8 us)
Async XLA Ops:
  0.0 15.2 %collective-permute-start.3 = (bf16[12,64,256]{2,1,0:T(8,128)(2,1)}, bf16[12,64,256]{2,1,0:T(8,128)(2,1)S(1)}, u32[]{:S(2)}, u32[]{:S(2)}) collective-permute-start(bf16[12,64,256]{2,1,0:T(8,128)(2,1)} %bitcast.41), channel_id=1, source_target_pairs={{0,4},{1,5},{2,6},{3,7},{4,8},{5,9},{6,10},{7,11},{8,12},{9,13},{1... | collective-permute-start | bytes 1179656 | tf_op jit(solution)/shard_map/ppermute | solution.py:69
  1.9 13.3 %collective-permute-start = (bf16[12,64,256]{2,1,0:T(8,128)(2,1)}, bf16[12,64,256]{2,1,0:T(8,128)(2,1)S(1)}, u32[]{:S(2)}, u32[]{:S(2)}) collective-permute-start(bf16[12,64,256]{2,1,0:T(8,128)(2,1)} %bitcast.42), channel_id=1, source_target_pairs={{0,28},{1,29},{2,30},{3,31},{4,0},{5,1},{6,2},{7,3},{8,4},{9,5},{1... | collective-permute-start | bytes 1179656 | tf_op jit(solution)/shard_map/ppermute | solution.py:70
  15.2 11.5 %collective-permute-start.4 = (bf16[12,64,256]{2,1,0:T(8,128)(2,1)S(1)}, bf16[12,64,256]{2,1,0:T(8,128)(2,1)S(1)}, u32[]{:S(2)}, u32[]{:S(2)}) collective-permute-start(bf16[12,64,256]{2,1,0:T(8,128)(2,1)S(1)} %collective-permute-done.3.refs_0_.refs_7_), channel_id=1, source_target_pairs={{0,4},{1,5},{2,6},{3,7},{4,8},{5,9},{6,10},{7,11},{8,12},{9,13},{1... | collective-permute-start | bytes 1179656 | tf_op jit(solution)/shard_map/ppermute | solution.py:77
  15.2 11.5 %collective-permute-start.1 = (bf16[12,64,256]{2,1,0:T(8,128)(2,1)S(1)}, bf16[12,64,256]{2,1,0:T(8,128)(2,1)S(1)}, u32[]{:S(2)}, u32[]{:S(2)}) collective-permute-start(bf16[12,64,256]{2,1,0:T(8,128)(2,1)S(1)} %collective-permute-done.refs_1_), channel_id=1, source_target_pairs={{0,28},{1,29},{2,30},{3,31},{4,0},{5,1},{6,2},{7,3},{8,4},{9,5},{1... | collective-permute-start | bytes 1179656 | tf_op jit(solution)/shard_map/ppermute | solution.py:78
  26.7 10.6 %collective-permute-start.5 = (bf16[12,64,256]{2,1,0:T(8,128)(2,1)S(1)}, bf16[12,64,256]{2,1,0:T(8,128)(2,1)S(1)}, u32[]{:S(2)}, u32[]{:S(2)}) collective-permute-start(bf16[12,64,256]{2,1,0:T(8,128)(2,1)S(1)} %collective-permute-done.4.refs_0_.refs_6_), channel_id=1, source_target_pairs={{0,4},{1,5},{2,6},{3,7},{4,8},{5,9},{6,10},{7,11},{8,12},{9,13},{1... | collective-permute-start | bytes 1179656 | tf_op jit(solution)/shard_map/ppermute | solution.py:77
  26.7 10.6 %collective-permute-start.2 = (bf16[12,64,256]{2,1,0:T(8,128)(2,1)S(1)}, bf16[12,64,256]{2,1,0:T(8,128)(2,1)S(1)}, u32[]{:S(2)}, u32[]{:S(2)}) collective-permute-start(bf16[12,64,256]{2,1,0:T(8,128)(2,1)S(1)} %collective-permute-done.1.refs_1_.refs_2_), channel_id=1, source_target_pairs={{0,28},{1,29},{2,30},{3,31},{4,0},{5,1},{6,2},{7,3},{8,4},{9,5},{1... | collective-permute-start | bytes 1179656 | tf_op jit(solution)/shard_map/ppermute | solution.py:78
  38.2 35.9 %collective-permute-start.6 = (bf16[12,64,256]{2,1,0:T(8,128)(2,1)}, bf16[12,64,256]{2,1,0:T(8,128)(2,1)S(1)}, u32[]{:S(2)}, u32[]{:S(2)}) collective-permute-start(bf16[12,64,256]{2,1,0:T(8,128)(2,1)} %broadcast_select_fusion), channel_id=1, source_target_pairs={{0,4},{1,5},{2,6},{3,7},{4,8},{5,9},{6,10},{7,11},{8,12},{9,13},{1... | collective-permute-start | bytes 1179656 | tf_op jit(solution)/shard_map/ppermute | solution.py:87
  38.9 16.7 %all-to-all-start = ((s32[32,1,13]{2,1,0:T(1,128)}), s32[32,1,13]{2,1,0:T(1,128)S(1)}, u32[]{:S(2)}, u32[]{:S(2)}) async-start(s32[32,1,13]{2,1,0:T(1,128)} %bitcast.5), calls=%async_computation | async-start | bytes 32768 | tf_op jit(solution)/shard_map/all_to_all | solution.py:71
  50.5 9.3 %collective-permute-start.7 = (bf16[3,64,256]{2,1,0:T(8,128)(2,1)S(1)}, bf16[3,64,256]{2,1,0:T(8,128)(2,1)}, u32[]{:S(2)}, u32[]{:S(2)}) collective-permute-start(bf16[3,64,256]{2,1,0:T(8,128)(2,1)S(1)} %get-tuple-element.28), channel_id=1, source_target_pairs={{0,1},{1,2},{2,3},{3,0},{4,5},{5,6},{6,7},{7,4},{8,9},{9,10},{10,1... | collective-permute-start | bytes 294920 | tf_op jit(solution)/shard_map/ppermute | solution.py:63
  51.7 15.6 %collective-permute-start.12 = (bf16[3,64,256]{2,1,0:T(8,128)(2,1)}, bf16[3,64,256]{2,1,0:T(8,128)(2,1)}, u32[]{:S(2)}, u32[]{:S(2)}) collective-permute-start(bf16[3,64,256]{2,1,0:T(8,128)(2,1)} %get-tuple-element.33), channel_id=1, source_target_pairs={{0,3},{1,0},{2,1},{3,2},{4,7},{5,4},{6,5},{7,6},{8,11},{9,8},{10,9... | collective-permute-start | bytes 294920 | tf_op jit(solution)/shard_map/ppermute | solution.py:63
  57.1 11.6 %collective-permute-start.8 = (bf16[6,64,256]{2,1,0:T(8,128)(2,1)}, bf16[6,64,256]{2,1,0:T(8,128)(2,1)}, u32[]{:S(2)}, u32[]{:S(2)}) collective-permute-start(bf16[6,64,256]{2,1,0:T(8,128)(2,1)} %get-tuple-element.29), channel_id=1, source_target_pairs={{0,1},{1,2},{2,3},{3,0},{4,5},{5,6},{6,7},{7,4},{8,9},{9,10},{10,1... | collective-permute-start | bytes 589832 | tf_op jit(solution)/shard_map/ppermute | solution.py:63
  58.6 10.8 %collective-permute-start.13 = (bf16[6,64,256]{2,1,0:T(8,128)(2,1)}, bf16[6,64,256]{2,1,0:T(8,128)(2,1)}, u32[]{:S(2)}, u32[]{:S(2)}) collective-permute-start(bf16[6,64,256]{2,1,0:T(8,128)(2,1)} %get-tuple-element.34), channel_id=1, source_target_pairs={{0,3},{1,0},{2,1},{3,2},{4,7},{5,4},{6,5},{7,6},{8,11},{9,8},{10,9... | collective-permute-start | bytes 589832 | tf_op jit(solution)/shard_map/ppermute | solution.py:63
  59.8 7.5 %collective-permute-start.17 = (bf16[3,64,256]{2,1,0:T(8,128)(2,1)}, bf16[3,64,256]{2,1,0:T(8,128)(2,1)S(1)}, u32[]{:S(2)}, u32[]{:S(2)}) collective-permute-start(bf16[3,64,256]{2,1,0:T(8,128)(2,1)} %get-tuple-element.38), channel_id=1, source_target_pairs={{0,2},{1,3},{2,0},{3,1},{4,6},{5,7},{6,4},{7,5},{8,10},{9,11},{10,... | collective-permute-start | bytes 294920 | tf_op jit(solution)/shard_map/ppermute | solution.py:63
  67.3 9.4 %collective-permute-start.18 = (bf16[6,64,256]{2,1,0:T(8,128)(2,1)S(1)}, bf16[6,64,256]{2,1,0:T(8,128)(2,1)S(1)}, u32[]{:S(2)}, u32[]{:S(2)}) collective-permute-start(bf16[6,64,256]{2,1,0:T(8,128)(2,1)S(1)} %get-tuple-element.39), channel_id=1, source_target_pairs={{0,2},{1,3},{2,0},{3,1},{4,6},{5,7},{6,4},{7,5},{8,10},{9,11},{10,... | collective-permute-start | bytes 589832 | tf_op jit(solution)/shard_map/ppermute | solution.py:63
  67.3 11.4 %collective-permute-start.9 = (bf16[6,64,256]{2,1,0:T(8,128)(2,1)}, bf16[6,64,256]{2,1,0:T(8,128)(2,1)S(1)}, u32[]{:S(2)}, u32[]{:S(2)}) collective-permute-start(bf16[6,64,256]{2,1,0:T(8,128)(2,1)} %get-tuple-element.30), channel_id=1, source_target_pairs={{0,1},{1,2},{2,3},{3,0},{4,5},{5,6},{6,7},{7,4},{8,9},{9,10},{10,1... | collective-permute-start | bytes 589832 | tf_op jit(solution)/shard_map/ppermute | solution.py:63
  68.8 14.3 %collective-permute-start.14 = (bf16[6,64,256]{2,1,0:T(8,128)(2,1)}, bf16[6,64,256]{2,1,0:T(8,128)(2,1)S(1)}, u32[]{:S(2)}, u32[]{:S(2)}) collective-permute-start(bf16[6,64,256]{2,1,0:T(8,128)(2,1)} %get-tuple-element.35), channel_id=1, source_target_pairs={{0,3},{1,0},{2,1},{3,2},{4,7},{5,4},{6,5},{7,6},{8,11},{9,8},{10,9... | collective-permute-start | bytes 589832 | tf_op jit(solution)/shard_map/ppermute | solution.py:63
  69.4 15.9 %collective-permute-start.19 = (bf16[6,64,256]{2,1,0:T(8,128)(2,1)}, bf16[6,64,256]{2,1,0:T(8,128)(2,1)S(1)}, u32[]{:S(2)}, u32[]{:S(2)}) collective-permute-start(bf16[6,64,256]{2,1,0:T(8,128)(2,1)} %get-tuple-element.40), channel_id=1, source_target_pairs={{0,2},{1,3},{2,0},{3,1},{4,6},{5,7},{6,4},{7,5},{8,10},{9,11},{10,... | collective-permute-start | bytes 589832 | tf_op jit(solution)/shard_map/ppermute | solution.py:63
  74.1 12.8 %collective-permute-start.10 = (bf16[6,64,256]{2,1,0:T(8,128)(2,1)}, bf16[6,64,256]{2,1,0:T(8,128)(2,1)S(1)}, u32[]{:S(2)}, u32[]{:S(2)}) collective-permute-start(bf16[6,64,256]{2,1,0:T(8,128)(2,1)} %get-tuple-element.31), channel_id=1, source_target_pairs={{0,1},{1,2},{2,3},{3,0},{4,5},{5,6},{6,7},{7,4},{8,9},{9,10},{10,1... | collective-permute-start | bytes 589832 | tf_op jit(solution)/shard_map/ppermute | solution.py:63
  76.6 13.2 %collective-permute-start.15 = (bf16[6,64,256]{2,1,0:T(8,128)(2,1)}, bf16[6,64,256]{2,1,0:T(8,128)(2,1)S(1)}, u32[]{:S(2)}, u32[]{:S(2)}) collective-permute-start(bf16[6,64,256]{2,1,0:T(8,128)(2,1)} %copy-done.9), channel_id=1, source_target_pairs={{0,3},{1,0},{2,1},{3,2},{4,7},{5,4},{6,5},{7,6},{8,11},{9,8},{10,9... | collective-permute-start | bytes 589832 | tf_op jit(solution)/shard_map/ppermute | solution.py:63
  78.7 12.5 %collective-permute-start.20 = (bf16[6,64,256]{2,1,0:T(8,128)(2,1)S(1)}, bf16[6,64,256]{2,1,0:T(8,128)(2,1)S(1)}, u32[]{:S(2)}, u32[]{:S(2)}) collective-permute-start(bf16[6,64,256]{2,1,0:T(8,128)(2,1)S(1)} %get-tuple-element.41), channel_id=1, source_target_pairs={{0,2},{1,3},{2,0},{3,1},{4,6},{5,7},{6,4},{7,5},{8,10},{9,11},{10,... | collective-permute-start | bytes 589832 | tf_op jit(solution)/shard_map/ppermute | solution.py:63
  83.0 8.2 %collective-permute-start.11 = (bf16[3,64,256]{2,1,0:T(8,128)(2,1)S(1)}, bf16[3,64,256]{2,1,0:T(8,128)(2,1)S(1)}, u32[]{:S(2)}, u32[]{:S(2)}) collective-permute-start(bf16[3,64,256]{2,1,0:T(8,128)(2,1)S(1)} %get-tuple-element.32), channel_id=1, source_target_pairs={{0,1},{1,2},{2,3},{3,0},{4,5},{5,6},{6,7},{7,4},{8,9},{9,10},{10,1... | collective-permute-start | bytes 294920 | tf_op jit(solution)/shard_map/ppermute | solution.py:63
  86.9 6.5 %collective-permute-start.21 = (bf16[3,64,256]{2,1,0:T(8,128)(2,1)S(1)}, bf16[3,64,256]{2,1,0:T(8,128)(2,1)S(1)}, u32[]{:S(2)}, u32[]{:S(2)}) collective-permute-start(bf16[3,64,256]{2,1,0:T(8,128)(2,1)S(1)} %get-tuple-element.42), channel_id=1, source_target_pairs={{0,2},{1,3},{2,0},{3,1},{4,6},{5,7},{6,4},{7,5},{8,10},{9,11},{10,... | collective-permute-start | bytes 294920 | tf_op jit(solution)/shard_map/ppermute | solution.py:63
  109.7 54.6 %all-to-all-start.2 = ((bf16[32,256,128]{2,1,0:T(8,128)(2,1)}), bf16[32,256,128]{2,1,0:T(8,128)(2,1)S(1)}, u32[]{:S(2)}, u32[]{:S(2)}) async-start(bf16[32,256,128]{2,1,0:T(8,128)(2,1)} %device_tiles.3), calls=%async_computation.2 | async-start | bytes 4194304 | tf_op jit(solution)/shard_map/all_to_all | solution.py:296
  165.7 53.6 %all-to-all-start.1 = ((bf16[32,256,128]{2,1,0:T(8,128)(2,1)}), bf16[32,256,128]{2,1,0:T(8,128)(2,1)}, u32[]{:S(2)}, u32[]{:S(2)}) async-start(bf16[32,256,128]{2,1,0:T(8,128)(2,1)} %device_tiles.2), calls=%async_computation.1 | async-start | bytes 4194304 | tf_op jit(solution)/shard_map/all_to_all | solution.py:296
  219.3 30.5 %all-to-all-start.3 = ((bf16[16,256,128]{2,1,0:T(8,128)(2,1)}), bf16[16,256,128]{2,1,0:T(8,128)(2,1)S(1)}, u32[]{:S(2)}, u32[]{:S(2)}) async-start(bf16[16,256,128]{2,1,0:T(8,128)(2,1)} %table_of.3), calls=%async_computation.3 | async-start | bytes 2097152 | tf_op jit(solution)/shard_map/all_to_all | solution.py:265
  229.5 12.3 %collective-permute-start.22 = (bf16[2,256,128]{2,1,0:T(8,128)(2,1)}, bf16[2,256,128]{2,1,0:T(8,128)(2,1)S(1)}, u32[]{:S(2)}, u32[]{:S(2)}) collective-permute-start(bf16[2,256,128]{2,1,0:T(8,128)(2,1)} %get-tuple-element.44), channel_id=1, source_target_pairs={{0,32},{32,64},{64,96},{96,128},{128,160},{160,192},{192,224},{224... | collective-permute-start | bytes 393224 | tf_op jit(solution)/shard_map/ppermute | solution.py:273
  230.0 12.6 %collective-permute-start.23 = (bf16[2,256,128]{2,1,0:T(8,128)(2,1)}, bf16[2,256,128]{2,1,0:T(8,128)(2,1)S(1)}, u32[]{:S(2)}, u32[]{:S(2)}) collective-permute-start(bf16[2,256,128]{2,1,0:T(8,128)(2,1)} %get-tuple-element.45), channel_id=1, source_target_pairs={{0,64},{32,96},{64,128},{96,160},{128,192},{160,224},{192,0},{224,... | collective-permute-start | bytes 393224 | tf_op jit(solution)/shard_map/ppermute | solution.py:273
  231.7 16.0 %collective-permute-start.24 = (bf16[2,256,128]{2,1,0:T(8,128)(2,1)}, bf16[2,256,128]{2,1,0:T(8,128)(2,1)S(1)}, u32[]{:S(2)}, u32[]{:S(2)}) collective-permute-start(bf16[2,256,128]{2,1,0:T(8,128)(2,1)} %get-tuple-element.46), channel_id=1, source_target_pairs={{0,96},{32,128},{64,160},{96,192},{128,224},{160,0},{192,32},{224,... | collective-permute-start | bytes 393224 | tf_op jit(solution)/shard_map/ppermute | solution.py:273
  233.6 15.1 %collective-permute-start.25 = (bf16[2,256,128]{2,1,0:T(8,128)(2,1)}, bf16[2,256,128]{2,1,0:T(8,128)(2,1)S(1)}, u32[]{:S(2)}, u32[]{:S(2)}) collective-permute-start(bf16[2,256,128]{2,1,0:T(8,128)(2,1)} %get-tuple-element.47), channel_id=1, source_target_pairs={{0,128},{32,160},{64,192},{96,224},{128,0},{160,32},{192,64},{224,... | collective-permute-start | bytes 393224 | tf_op jit(solution)/shard_map/ppermute | solution.py:273
  235.7 13.1 %collective-permute-start.26 = (bf16[2,256,128]{2,1,0:T(8,128)(2,1)}, bf16[2,256,128]{2,1,0:T(8,128)(2,1)S(1)}, u32[]{:S(2)}, u32[]{:S(2)}) collective-permute-start(bf16[2,256,128]{2,1,0:T(8,128)(2,1)} %get-tuple-element.48), channel_id=1, source_target_pairs={{0,160},{32,192},{64,224},{96,0},{128,32},{160,64},{192,96},{224,1... | collective-permute-start | bytes 393224 | tf_op jit(solution)/shard_map/ppermute | solution.py:273
  241.8 6.9 %collective-permute-start.27 = (bf16[2,256,128]{2,1,0:T(8,128)(2,1)}, bf16[2,256,128]{2,1,0:T(8,128)(2,1)S(1)}, u32[]{:S(2)}, u32[]{:S(2)}) collective-permute-start(bf16[2,256,128]{2,1,0:T(8,128)(2,1)} %get-tuple-element.49), channel_id=1, source_target_pairs={{0,192},{32,224},{64,0},{96,32},{128,64},{160,96},{192,128},{224,1... | collective-permute-start | bytes 393224 | tf_op jit(solution)/shard_map/ppermute | solution.py:273
  242.6 6.1 %collective-permute-start.28 = (bf16[2,256,128]{2,1,0:T(8,128)(2,1)}, bf16[2,256,128]{2,1,0:T(8,128)(2,1)S(1)}, u32[]{:S(2)}, u32[]{:S(2)}) collective-permute-start(bf16[2,256,128]{2,1,0:T(8,128)(2,1)} %get-tuple-element.50), channel_id=1, source_target_pairs={{0,224},{32,0},{64,32},{96,64},{128,96},{160,128},{192,160},{224,1... | collective-permute-start | bytes 393224 | tf_op jit(solution)/shard_map/ppermute | solution.py:273
  (27 other events, 578.6 us)

commit v4 on v0

v4 whole, which is shorter than its diff:
```python
import functools

import jax
import jax.numpy as jnp
from jax import lax
from jax.experimental import pallas as pl
from jax.experimental.pallas import tpu as pltpu
from jax.sharding import PartitionSpec as P


BLOCK = 64
W = 256
R = 12
K = 27
CT = 2
NCAP = 3
LT = 16
PAIR = 2 * BLOCK
STEPS = (1, -1, 2, 0)


def pick_kernel(n_x, ups, asks_ref, *refs):
    block_refs, out_refs = refs[: len(ups)], refs[len(ups) :]
    z, x = lax.axis_index("dev") // n_x, lax.axis_index("dev") % n_x
    n_z = asks_ref.shape[0] // n_x
    for i, (up, block_ref) in enumerate(zip(ups, block_refs)):
        source = (z + n_z - up) % n_z * n_x + x
        for step, out_ref in zip(STEPS, out_refs):
            peer = (x + n_x + step) % n_x
            for c in range(NCAP):
                out_ref[i * NCAP + c] = block_ref[asks_ref[source, 1 + peer * NCAP + c]]


def pick(asks, n_x, ups, blocks):
    shape = (len(blocks) * NCAP,) + blocks[0].shape[1:]
    vmem = pl.BlockSpec(memory_space=pltpu.VMEM)
    return pl.pallas_call(
        functools.partial(pick_kernel, n_x, ups),
        out_shape=[jax.ShapeDtypeStruct(shape, blocks[0].dtype)] * len(STEPS),
        in_specs=[pl.BlockSpec(memory_space=pltpu.SMEM)] + [vmem] * len(blocks),
        out_specs=[vmem] * len(STEPS),
        compiler_params=pltpu.CompilerParams(vmem_limit_bytes=16 << 20),
        cost_estimate=pl.CostEstimate(flops=0, bytes_accessed=1_500_000, transcendentals=0),
        name="pick",
    )(asks, *blocks)


def fetch(panels, rows_of, labels):
    n_z, n_x = 8, 4
    half = n_z // 2
    me = lax.axis_index("dev")
    z, x = me // n_x, me % n_x

    def along_z(step):
        return [(s, (s // n_x + step) % n_z * n_x + s % n_x) for s in range(n_z * n_x)]

    def along_x(step):
        return [(s, s // n_x * n_x + (s % n_x + step) % n_x) for s in range(n_z * n_x)]

    pieces, spots = [], []

    def forward(ups, blocks):
        picked = pick(asks, n_x, ups, blocks)
        for step, block in zip(STEPS, picked):
            if step:
                block = lax.ppermute(block, "dev", along_x(step))
            pieces.append(block)
            base = (-step) % n_x * n_z
            spots.append([(i * NCAP, NCAP, (base + -up % n_z) * NCAP) for i, up in enumerate(ups)])

    fetched = rows_of.reshape(n_z, 1, n_x * NCAP)
    asked = jnp.broadcast_to(fetched, (n_z, n_x, n_x * NCAP)).reshape(n_z * n_x, n_x * NCAP)
    asked = jnp.concatenate([labels[:, None], asked], axis=1)

    up = lax.ppermute(panels, "dev", along_z(1))
    down = lax.ppermute(panels, "dev", along_z(-1))
    asks = lax.all_to_all(asked, "dev", split_axis=0, concat_axis=0, tiled=True)
    for k in range(1, half):
        if k + 1 < half:
            new_up = lax.ppermute(up, "dev", along_z(1))
            new_down = lax.ppermute(down, "dev", along_z(-1))
        else:
            odd = lax.axis_index("grp") % 2 == 1
            n = n_z * n_x
            pairs = [
                (g * n + s, g * n + t)
                for g in range(lax.axis_size("grp"))
                for s, t in along_z(-1 if g % 2 else 1)
            ]
            far = lax.ppermute(jnp.where(odd, down, up), ("grp", "dev"), pairs)
        if k == 1:
            forward((0, k, -k), (panels, up, down))
        else:
            forward((k, -k), (up, down))
        up, down = new_up, new_down
    forward((half,), (far,))

    entry = jnp.arange(n_z * n_x * NCAP, dtype=jnp.int32)
    s, c = entry // NCAP, entry % NCAP
    dz, dx = (s // n_x - z) % n_z, (s % n_x - x) % n_x
    where = ((dx * n_z + dz) * NCAP + c).astype(jnp.int32)
    return pieces, spots, where, asks[:, 0]


def tiles_kernel(spots, cols_ref, slots_ref, places_ref, where_ref, a_hbm, pt_ref, *refs):
    piece_refs, (out_ref, a_ref, b_ref, near_ref, a_sems) = refs[: len(spots)], refs[len(spots) :]

    def load(row):
        return pltpu.make_async_copy(a_hbm.at[row], a_ref.at[row], a_sems.at[row])

    for row in range(R):
        load(row).start()
    for piece_ref, parts in zip(piece_refs, spots):
        for start, n, place in parts:
            for i in range(n):
                b_ref[place + i] = piece_ref[start + i]

    @pl.loop(0, LT)
    def _(t):
        near_ref[t] = jnp.zeros(near_ref.shape[1:], jnp.float32)

    lane = lax.broadcasted_iota(jnp.int32, (BLOCK, PAIR), 1)
    left = jnp.where(lane < BLOCK, 1.0, 0.0).astype(jnp.bfloat16)
    right = jnp.where(lane < BLOCK, 0.0, 1.0).astype(jnp.bfloat16)

    @pl.loop(0, R)
    def _(row):
        load(row).wait()
        rows_of = pl.ds(row * BLOCK, BLOCK)

        def target(k):
            return jnp.where(cols_ref[row, k] < 0, LT, slots_ref[row, k])

        def panel(k):
            return b_ref[where_ref[jnp.maximum(cols_ref[row, k], 0)]]

        def add(k, product):
            rounded = product.astype(jnp.bfloat16).astype(jnp.float32)
            near_ref[target(k), rows_of, :] += rounded

        for j in range(K // 2):
            pair = a_ref[row, :, j * PAIR : (j + 1) * PAIR]
            both = jnp.concatenate([pair * left, pair * right], axis=0)
            panels = jnp.concatenate([panel(2 * j), panel(2 * j + 1)], axis=0)
            product = jnp.dot(both, panels, preferred_element_type=jnp.float32)
            add(2 * j, product[:BLOCK])
            add(2 * j + 1, product[BLOCK:])
        last = a_ref[row, :, (K - 1) * BLOCK :]
        add(K - 1, jnp.dot(last, panel(K - 1), preferred_element_type=jnp.float32))

    @pl.loop(0, LT)
    def _(t):
        near = near_ref[t]
        high = near.astype(jnp.bfloat16)
        low = (near - high.astype(jnp.float32)).astype(jnp.bfloat16)
        tile = jnp.dot(pt_ref[...], high, preferred_element_type=jnp.float32)
        tile += jnp.dot(pt_ref[...], low, preferred_element_type=jnp.float32)
        out_ref[places_ref[t]] = tile.astype(jnp.bfloat16)


def device_tiles(blocks, pt, pieces, spots, where, cols, slots, places, n_places):
    n_panels = max(place + n for parts in spots for _, n, place in parts)
    smem, vmem = pl.BlockSpec(memory_space=pltpu.SMEM), pl.BlockSpec(memory_space=pltpu.VMEM)
    hbm = pl.BlockSpec(memory_space=pltpu.HBM)
    return pl.pallas_call(
        functools.partial(tiles_kernel, spots),
        out_shape=jax.ShapeDtypeStruct((n_places, W, W), jnp.bfloat16),
        in_specs=[smem] * 4 + [hbm, vmem] + [vmem] * len(pieces),
        out_specs=vmem,
        scratch_shapes=[
            pltpu.VMEM((R, BLOCK, K * BLOCK), jnp.bfloat16),
            pltpu.VMEM((n_panels, BLOCK, W), jnp.bfloat16),
            pltpu.VMEM((LT + 1, R * BLOCK, W), jnp.float32),
            pltpu.SemaphoreType.DMA((R,)),
        ],
        compiler_params=pltpu.CompilerParams(vmem_limit_bytes=50 << 20),
        cost_estimate=pl.CostEstimate(
            flops=8_000_000_000, bytes_accessed=12_000_000, transcendentals=0
        ),
        name="device_tiles",
    )(cols, slots, places, where, blocks, pt, *pieces)


def table_kernel(labels_ref, got_ref, here_ref, there_ref, sum_ref):
    n_here, n_there = here_ref.shape[0], there_ref.shape[0]

    @pl.loop(0, n_here + n_there)
    def _(t):
        sum_ref[t] = jnp.zeros(sum_ref.shape[1:], jnp.float32)

    @pl.loop(0, got_ref.shape[0])
    def _(s):
        label = labels_ref[s]
        at = jnp.where(label < 0, n_here + n_there, label)
        sum_ref[at] += got_ref[s].astype(jnp.float32)

    @pl.loop(0, n_here)
    def _(t):
        here_ref[t] = sum_ref[t]

    @pl.loop(0, n_there)
    def _(t):
        there_ref[t] = sum_ref[n_here + t].astype(there_ref.dtype)


def table_of(labels, got, n_here, n_there):
    rows = 64
    block = lambda n: pl.BlockSpec((n, rows, W), lambda i, *_: (0, i, 0))
    return pl.pallas_call(
        table_kernel,
        out_shape=[
            jax.ShapeDtypeStruct((n_here, W, W), jnp.float32),
            jax.ShapeDtypeStruct((n_there, W, W), jnp.bfloat16),
        ],
        grid_spec=pltpu.PrefetchScalarGridSpec(
            num_scalar_prefetch=1,
            grid=(W // rows,),
            in_specs=[block(got.shape[0])],
            out_specs=[block(n_here), block(n_there)],
            scratch_shapes=[pltpu.VMEM((n_here + n_there + 1, rows, W), jnp.float32)],
        ),
        compiler_params=pltpu.CompilerParams(dimension_semantics=("arbitrary",)),
        cost_estimate=pl.CostEstimate(flops=2_000_000, bytes_accessed=7_000_000, transcendentals=0),
        name="table_of",
    )(labels, got)


def sum_over_groups(labels, got):
    groups, cores = lax.axis_size("grp"), 2
    n_y = groups // cores
    y, core = lax.axis_index("grp") // cores, lax.axis_index("grp") % cores
    to, place = labels // CT, labels % CT
    dy = (to // cores - y) % n_y
    other = (to % cores - core) % cores
    at = jnp.where(labels < 0, -1, (other * n_y + dy) * CT + place)
    here, there = table_of(at, got, n_y * CT, n_y * CT)
    swap = [(g, g // cores * cores + (g + 1) % cores) for g in range(groups)]
    here += lax.ppermute(there, "grp", swap).astype(jnp.float32)
    total = here[:CT]
    for step in (2, 1, 3):
        pairs = [(g, (g + step * cores) % groups) for g in range(groups)]
        part = here[step * CT : (step + 1) * CT].astype(jnp.bfloat16)
        total += lax.ppermute(part, "grp", pairs).astype(jnp.float32)
    return total


def layer(blocks, prolong, block_cols, fetch_rows, tile_slot, tile_owner, tile_place):
    dev_count = lax.axis_size("dev")
    panels = prolong[0, 0]
    owners = tile_owner[0, 0]
    dev_target = owners % dev_count
    label = (owners // dev_count) * CT + tile_place[0, 0]
    meant = dev_target[None, :] == jnp.arange(dev_count)[:, None]
    labels = jnp.max(jnp.where(meant, label[None, :], -1), axis=1)
    pieces, spots, where, got_labels = fetch(panels, fetch_rows[0, 0], labels)

    pt = panels.reshape(R * BLOCK, W).T
    sending = device_tiles(
        blocks[0, 0], pt, pieces, spots, where, block_cols[0, 0], tile_slot[0, 0], dev_target, dev_count
    )
    got = lax.all_to_all(sending, "dev", split_axis=0, concat_axis=0, tiled=True)
    return sum_over_groups(got_labels, got).reshape(1, 1, CT, W, W)


def solution(mesh):
    return jax.shard_map(
        layer,
        mesh=mesh,
        in_specs=(
            P("grp", "dev", None, None, None),
            P("grp", "dev", None, None, None),
            P("grp", "dev", None, None),
            P("grp", "dev", None, None),
            P("grp", "dev", None, None),
            P("grp", "dev", None),
            P("grp", "dev", None),
        ),
        out_specs=P("grp", "dev", None, None, None),
        check_vma=False,
    )
```

time: 671 us -> 232 us (0.35)
  local copies, waits for them, and re-layouts: 211 us -> 3.95 us
  matrix products: 186 us -> 0 us
  waiting for transfers between devices: 202 us -> 132 us
  Pallas kernels: 0 us -> 26.6 us
  other arithmetic: 25.8 us -> 4.35 us
  starting transfers between devices: 29.1 us -> 48.2 us
  blocking collectives: 0 us -> 15.1 us
  between operations: 13.5 us -> 0.19 us
    dot_general x24 -> x0, matrix products: 186 us -> none  [the longest x12 119 us: one_row(): jnp.einsum('kt,kab->tab', selector, outer_tile, precision=lax.Precision.H...]
    transpose x12 -> x0, local copies, waits for them, and re-layouts: 124 us -> none  [one_row(): jnp.einsum('ra,krb->kab', panel_row, product, preferred_element_type=jnp....]
    all_to_all x3 -> x1, waiting for transfers between devices: 162 us -> 87.2 us  [layer(): lax.all_to_all(sending, 'dev', split_axis=0, concat_axis=0, tiled=True)]
    ppermute x0 -> x23, waiting for transfers between devices: none -> 45.1 us  [the longest x2 12.4 us: fetch(): new_down = lax.ppermute(down, 'dev', along_z(-1))]
    ppermute x0 -> x23, starting transfers between devices: none -> 41.7 us  [the longest x12 23.2 us: forward(): block = lax.ppermute(block, 'dev', along_x(step))]
    reduce_scatter x1 -> x0, waiting for transfers between devices: 40 us -> none  [body(): result = lax.psum_scatter(table, 'grp', scatter_dimension=0, tiled=True)]
    gather x13 -> x0, local copies, waits for them, and re-layouts: 33.4 us -> none  [the longest x12 29.9 us: one_row(): near_panels = arrived[jnp.maximum(column_ids, 0)]]
    pallas_call x0 -> x6, Pallas kernels: none -> 26.6 us  [the longest x1 15.2 us: device_tiles(): pl.pallas_call(functools.partial(tiles_kernel, spots), out_shape=jax.Shap...]
  transfers between devices with their start and end apart: 4 -> 24, of which waited for: 3 -> 13; matrix products, arithmetic and copies ran while one was open for 56% -> 1% of each run, Pallas kernels for 0% -> 2%
where the time goes in v4:
time: 232 us; the launch traced here: 231 us
  waiting for transfers between devices  132 us (57%)
  starting transfers between devices  48.2 us (21%)
  Pallas kernels  26.6 us (11%)
  blocking collectives  15.1 us (7%)
  other arithmetic  4.35 us (2%)
  local copies, waits for them, and re-layouts  3.95 us (2%)
    all_to_all x1, waiting for transfers between devices, layer(): lax.all_to_all(sending, 'dev', split_axis=0, concat_axis=0, tiled=True)  87.2 us
    ppermute x12, starting transfers between devices, forward(): block = lax.ppermute(block, 'dev', along_x(step))  23.2 us
    pallas_call x1, Pallas kernels, device_tiles(): pl.pallas_call(functools.partial(tiles_kernel, spots), out_shape=jax.Shap...  15.2 us
    all_to_all x1, blocking collectives, fetch(): asks = lax.all_to_all(asked, 'dev', split_axis=0, concat_axis=0, tiled=True)  15.1 us
    ppermute x2, waiting for transfers between devices, fetch(): new_down = lax.ppermute(down, 'dev', along_z(-1))  12.4 us
    ppermute x3, waiting for transfers between devices, sum_over_groups(): total += lax.ppermute(part, 'grp', pairs).astype(jnp.float32)  10.6 us
    ppermute x1, waiting for transfers between devices, fetch(): down = lax.ppermute(panels, 'dev', along_z(-1))  8.69 us
    ppermute x2, starting transfers between devices, fetch(): new_down = lax.ppermute(down, 'dev', along_z(-1))  7.28 us
  transfers between devices with their start and end apart: 24, of which 13 were waited for; matrix products, arithmetic and copies ran while one was open for 1% of the time, Pallas kernels for 2%

profile of v4, /device:TPU:4, one launch (start us, length us, event | category | flops | bytes accessed | tf_op | source)
XLA Modules:
  0.0 230.7 jit_solution(5504349645161070194)
XLA Ops:
  0.0 5.9 %collective-permute-start.1 = (bf16[12,64,256]{2,1,0:T(8,128)(2,1)}, bf16[12,64,256]{2,1,0:T(8,128)(2,1)S(1)}, u32[]{:S(2)}, u32[]{:S(2)}) collective-permute-start(bf16[12,64,256]{2,1,0:T(8,128)(2,1)} %bitcast.35), channel_id=1, source_target_pairs={{0,28},{1,29},{2,30},{3,31},{4,0},{5,1},{6,2},{7,3},{8,4},{9,5},{1... | collective-permute-start | bytes 1179656 | tf_op jit(solution)/shard_map/ppermute | solution.py:76
  5.9 8.7 %collective-permute-done.1.refs_2_ = bf16[12,64,256]{2,1,0:T(8,128)(2,1)S(1)} collective-permute-done((bf16[12,64,256]{2,1,0:T(8,128)(2,1)}, bf16[12,64,256]{2,1,0:T(8,128)(2,1)S(1)}, u32[]{:S(2)}, u32[]{:S(2)}) %collective-permute-start.1) | collective-permute-done | bytes 393248 | tf_op jit(solution)/shard_map/ppermute | solution.py:76
  14.5 3.6 %collective-permute-start.6 = (bf16[12,64,256]{2,1,0:T(8,128)(2,1)S(1)}, bf16[12,64,256]{2,1,0:T(8,128)(2,1)S(1)}, u32[]{:S(2)}, u32[]{:S(2)}) collective-permute-start(bf16[12,64,256]{2,1,0:T(8,128)(2,1)S(1)} %collective-permute-done.1.refs_2_), channel_id=1, source_target_pairs={{0,28},{1,29},{2,30},{3,31},{4,0},{5,1},{6,2},{7,3},{8,4},{9,5},{1... | collective-permute-start | bytes 1179656 | tf_op jit(solution)/shard_map/ppermute | solution.py:81
  18.1 7.5 %collective-permute-done.6.refs_1_ = bf16[12,64,256]{2,1,0:T(8,128)(2,1)S(1)} collective-permute-done((bf16[12,64,256]{2,1,0:T(8,128)(2,1)S(1)}, bf16[12,64,256]{2,1,0:T(8,128)(2,1)S(1)}, u32[]{:S(2)}, u32[]{:S(2)}) %collective-permute-start.6) | collective-permute-done | bytes 393248 | tf_op jit(solution)/shard_map/ppermute | solution.py:81
  25.7 3.7 %collective-permute-start.11 = (bf16[12,64,256]{2,1,0:T(8,128)(2,1)S(1)}, bf16[12,64,256]{2,1,0:T(8,128)(2,1)S(1)}, u32[]{:S(2)}, u32[]{:S(2)}) collective-permute-start(bf16[12,64,256]{2,1,0:T(8,128)(2,1)S(1)} %collective-permute-done.6.refs_1_), channel_id=1, source_target_pairs={{0,28},{1,29},{2,30},{3,31},{4,0},{5,1},{6,2},{7,3},{8,4},{9,5},{1... | collective-permute-start | bytes 1179656 | tf_op jit(solution)/shard_map/ppermute | solution.py:81
  31.1 4.9 %collective-permute-done.11.refs_1_ = bf16[12,64,256]{2,1,0:T(8,128)(2,1)S(1)} collective-permute-done((bf16[12,64,256]{2,1,0:T(8,128)(2,1)S(1)}, bf16[12,64,256]{2,1,0:T(8,128)(2,1)S(1)}, u32[]{:S(2)}, u32[]{:S(2)}) %collective-permute-start.11) | collective-permute-done | bytes 393248 | tf_op jit(solution)/shard_map/ppermute | solution.py:81
  36.0 3.4 %collective-permute-done.10.refs_0_ = bf16[12,64,256]{2,1,0:T(8,128)(2,1)S(1)} collective-permute-done((bf16[12,64,256]{2,1,0:T(8,128)(2,1)S(1)}, bf16[12,64,256]{2,1,0:T(8,128)(2,1)S(1)}, u32[]{:S(2)}, u32[]{:S(2)}) %collective-permute-start.10) | collective-permute-done | bytes 393248 | tf_op jit(solution)/shard_map/ppermute | solution.py:80
  39.6 15.1 %all_to_all.16 = s32[32,1,13]{2,1,0:T(1,128)S(1)} all-to-all(s32[32,1,13]{2,1,0:T(1,128)S(1)} %bitcast.46), channel_id=1, replica_groups=mesh['grp'=8,'dev'=32] {'dev'}, dimensions={0} | all-to-all | bytes 3328 | tf_op jit(solution)/shard_map/all_to_all | solution.py:77
  54.7 1.0 copy-done
  56.7 1.5 collective-permute-start.2
  58.8 3.5 %collective-permute-start.4 = (bf16[9,64,256]{2,1,0:T(8,128)(2,1)S(1)}, bf16[9,64,256]{2,1,0:T(8,128)(2,1)S(1)}, u32[]{:S(2)}, u32[]{:S(2)}) collective-permute-start(bf16[9,64,256]{2,1,0:T(8,128)(2,1)S(1)} %get-tuple-element.25), channel_id=1, source_target_pairs={{0,2},{1,3},{2,0},{3,1},{4,6},{5,7},{6,4},{7,5},{8,10},{9,11},{10,... | collective-permute-start | bytes 884744 | tf_op jit(solution)/shard_map/ppermute | solution.py:66
  62.3 1.7 pick.5
  64.0 1.7 pick.6
  65.7 1.8 collective-permute-done.2.refs_0_
  68.1 6.3 %collective-permute-start.9 = (bf16[6,64,256]{2,1,0:T(8,128)(2,1)}, bf16[6,64,256]{2,1,0:T(8,128)(2,1)S(1)}, u32[]{:S(2)}, u32[]{:S(2)}) collective-permute-start(bf16[6,64,256]{2,1,0:T(8,128)(2,1)} %get-tuple-element.29), channel_id=1, source_target_pairs={{0,2},{1,3},{2,0},{3,1},{4,6},{5,7},{6,4},{7,5},{8,10},{9,11},{10,... | collective-permute-start | bytes 589832 | tf_op jit(solution)/shard_map/ppermute | solution.py:66
  75.1 1.8 collective-permute-start.12
  76.9 1.1 collective-permute-done.7.refs_4_
  78.7 3.3 %collective-permute-start.14 = (bf16[6,64,256]{2,1,0:T(8,128)(2,1)}, bf16[6,64,256]{2,1,0:T(8,128)(2,1)}, u32[]{:S(2)}, u32[]{:S(2)}) collective-permute-start(bf16[6,64,256]{2,1,0:T(8,128)(2,1)} %get-tuple-element.33), channel_id=1, source_target_pairs={{0,2},{1,3},{2,0},{3,1},{4,6},{5,7},{6,4},{7,5},{8,10},{9,11},{10,... | collective-permute-start | bytes 589832 | tf_op jit(solution)/shard_map/ppermute | solution.py:66
  83.1 2.9 %collective-permute-start.16 = (bf16[3,64,256]{2,1,0:T(8,128)(2,1)S(1)}, bf16[3,64,256]{2,1,0:T(8,128)(2,1)S(1)}, u32[]{:S(2)}, u32[]{:S(2)}) collective-permute-start(bf16[3,64,256]{2,1,0:T(8,128)(2,1)S(1)} %get-tuple-element.35), channel_id=1, source_target_pairs={{0,1},{1,2},{2,3},{3,0},{4,5},{5,6},{6,7},{7,4},{8,9},{9,10},{10,1... | collective-permute-start | bytes 294920 | tf_op jit(solution)/shard_map/ppermute | solution.py:66
  85.9 2.1 collective-permute-start.18
  88.1 2.4 %collective-permute-done.17.refs_13_ = bf16[3,64,256]{2,1,0:T(8,128)(2,1)S(1)} collective-permute-done((bf16[3,64,256]{2,1,0:T(8,128)(2,1)S(1)}, bf16[3,64,256]{2,1,0:T(8,128)(2,1)S(1)}, u32[]{:S(2)}, u32[]{:S(2)}) %collective-permute-start.17) | collective-permute-done | bytes 98336 | tf_op jit(solution)/shard_map/ppermute | solution.py:66
  90.6 1.6 collective-permute-done.18.refs_14_
  93.1 15.2 %device_tiles.1 = bf16[32,256,256]{2,1,0:T(8,128)(2,1)} custom-call(s32[12,27]{1,0:T(8,128)S(1)} %get-tuple-element.49.cols_ref, s32[12,27]{1,0:T(8,128)S(1)} %get-tuple-element.48.slots_ref, s32[16]{0:T(128)S(1)} %get-tuple-element.46.places_ref, s32[96]{0:T(128)S(1)} %fusion.3.where_ref, bf16[12,64,1728]{2,1,0:T(8,128)(2,1)} %bitcast.48, ...), custom_call_target="tpu_custom_call" | custom-call | flops 8000000000 | bytes 12000000 | tf_op jit(solution)/shard_map/device_tiles/pallas_call | solution.py:165
  108.3 6.4 %all-to-all-start.1 = ((bf16[32,256,256]{2,1,0:T(8,128)(2,1)}), bf16[32,256,256]{2,1,0:T(8,128)(2,1)}, u32[]{:S(2)}, u32[]{:S(2)}) async-start(bf16[32,256,256]{2,1,0:T(8,128)(2,1)} %device_tiles.1), calls=%async_computation.1 | async-start | bytes 8388608 | tf_op jit(solution)/shard_map/all_to_all | solution.py:261
  115.4 87.2 %all-to-all-done.1.got_ref = bf16[32,256,256]{2,1,0:T(8,128)(2,1)} async-done(((bf16[32,256,256]{2,1,0:T(8,128)(2,1)}), bf16[32,256,256]{2,1,0:T(8,128)(2,1)}, u32[]{:S(2)}, u32[]{:S(2)}) %all-to-all-start.1) | async-done | bytes 4194336 | tf_op jit(solution)/shard_map/all_to_all | solution.py:261
  202.6 6.3 %table_of.1 = (f32[8,256,256]{2,1,0:T(8,128)}, bf16[8,256,256]{2,1,0:T(8,128)(2,1)}) custom-call(s32[32]{0:T(128)} %fusion.7.labels_ref, bf16[32,256,256]{2,1,0:T(8,128)(2,1)} %all-to-all-done.1.got_ref), custom_call_target="tpu_custom_call" | custom-call | flops 2000000 | bytes 7000000 | tf_op jit(solution)/shard_map/table_of/pallas_call | solution.py:209
  208.9 2.9 %collective-permute-done.19 = bf16[8,256,256]{2,1,0:T(8,128)(2,1)S(1)} collective-permute-done((bf16[8,256,256]{2,1,0:T(8,128)(2,1)}, bf16[8,256,256]{2,1,0:T(8,128)(2,1)S(1)}, u32[]{:S(2)}, u32[]{:S(2)}) %collective-permute-start.19) | collective-permute-done | bytes 1048608 | tf_op jit(solution)/shard_map/ppermute | solution.py:238
  211.8 1.9 fusion.16
  213.8 3.3 %collective-permute-start.20 = (bf16[2,256,256]{2,1,0:T(8,128)(2,1)S(1)}, bf16[2,256,256]{2,1,0:T(8,128)(2,1)S(1)}, u32[]{:S(2)}, u32[]{:S(2)}) collective-permute-start(bf16[2,256,256]{2,1,0:T(8,128)(2,1)S(1)} %get-tuple-element.43), channel_id=1, source_target_pairs={{0,128},{32,160},{64,192},{96,224},{128,0},{160,32},{192,64},{224,... | collective-permute-start | bytes 786440 | tf_op jit(solution)/shard_map/ppermute | solution.py:243
  217.1 1.1 collective-permute-start.22
  219.1 5.5 %collective-permute-done.20 = bf16[2,256,256]{2,1,0:T(8,128)(2,1)S(1)} collective-permute-done((bf16[2,256,256]{2,1,0:T(8,128)(2,1)S(1)}, bf16[2,256,256]{2,1,0:T(8,128)(2,1)S(1)}, u32[]{:S(2)}, u32[]{:S(2)}) %collective-permute-start.20) | collective-permute-done | bytes 262176 | tf_op jit(solution)/shard_map/ppermute | solution.py:243
  224.5 5.2 %collective-permute-done.22 = bf16[2,256,256]{2,1,0:T(8,128)(2,1)S(1)} collective-permute-done((bf16[2,256,256]{2,1,0:T(8,128)(2,1)S(1)}, bf16[2,256,256]{2,1,0:T(8,128)(2,1)S(1)}, u32[]{:S(2)}, u32[]{:S(2)}) %collective-permute-start.22) | collective-permute-done | bytes 262176 | tf_op jit(solution)/shard_map/ppermute | solution.py:243
  (51 shorter events, 10.1 us)
Async XLA Ops:
  0.0 14.5 %collective-permute-start.1 = (bf16[12,64,256]{2,1,0:T(8,128)(2,1)}, bf16[12,64,256]{2,1,0:T(8,128)(2,1)S(1)}, u32[]{:S(2)}, u32[]{:S(2)}) collective-permute-start(bf16[12,64,256]{2,1,0:T(8,128)(2,1)} %bitcast.35), channel_id=1, source_target_pairs={{0,28},{1,29},{2,30},{3,31},{4,0},{5,1},{6,2},{7,3},{8,4},{9,5},{1... | collective-permute-start | bytes 1179656 | tf_op jit(solution)/shard_map/ppermute | solution.py:76
  5.9 12.3 %collective-permute-start = (bf16[12,64,256]{2,1,0:T(8,128)(2,1)}, bf16[12,64,256]{2,1,0:T(8,128)(2,1)S(1)}, u32[]{:S(2)}, u32[]{:S(2)}) collective-permute-start(bf16[12,64,256]{2,1,0:T(8,128)(2,1)} %bitcast.36), channel_id=1, source_target_pairs={{0,4},{1,5},{2,6},{3,7},{4,8},{5,9},{6,10},{7,11},{8,12},{9,13},{1... | collective-permute-start | bytes 1179656 | tf_op jit(solution)/shard_map/ppermute | solution.py:75
  14.5 11.1 %collective-permute-start.6 = (bf16[12,64,256]{2,1,0:T(8,128)(2,1)S(1)}, bf16[12,64,256]{2,1,0:T(8,128)(2,1)S(1)}, u32[]{:S(2)}, u32[]{:S(2)}) collective-permute-start(bf16[12,64,256]{2,1,0:T(8,128)(2,1)S(1)} %collective-permute-done.1.refs_2_), channel_id=1, source_target_pairs={{0,28},{1,29},{2,30},{3,31},{4,0},{5,1},{6,2},{7,3},{8,4},{9,5},{1... | collective-permute-start | bytes 1179656 | tf_op jit(solution)/shard_map/ppermute | solution.py:81
  18.1 11.2 %collective-permute-start.5 = (bf16[12,64,256]{2,1,0:T(8,128)(2,1)S(1)}, bf16[12,64,256]{2,1,0:T(8,128)(2,1)S(1)}, u32[]{:S(2)}, u32[]{:S(2)}) collective-permute-start(bf16[12,64,256]{2,1,0:T(8,128)(2,1)S(1)} %collective-permute-done.refs_1_), channel_id=1, source_target_pairs={{0,4},{1,5},{2,6},{3,7},{4,8},{5,9},{6,10},{7,11},{8,12},{9,13},{1... | collective-permute-start | bytes 1179656 | tf_op jit(solution)/shard_map/ppermute | solution.py:80
  25.7 10.4 %collective-permute-start.11 = (bf16[12,64,256]{2,1,0:T(8,128)(2,1)S(1)}, bf16[12,64,256]{2,1,0:T(8,128)(2,1)S(1)}, u32[]{:S(2)}, u32[]{:S(2)}) collective-permute-start(bf16[12,64,256]{2,1,0:T(8,128)(2,1)S(1)} %collective-permute-done.6.refs_1_), channel_id=1, source_target_pairs={{0,28},{1,29},{2,30},{3,31},{4,0},{5,1},{6,2},{7,3},{8,4},{9,5},{1... | collective-permute-start | bytes 1179656 | tf_op jit(solution)/shard_map/ppermute | solution.py:81
  29.3 10.1 %collective-permute-start.10 = (bf16[12,64,256]{2,1,0:T(8,128)(2,1)S(1)}, bf16[12,64,256]{2,1,0:T(8,128)(2,1)S(1)}, u32[]{:S(2)}, u32[]{:S(2)}) collective-permute-start(bf16[12,64,256]{2,1,0:T(8,128)(2,1)S(1)} %collective-permute-done.5.refs_0_), channel_id=1, source_target_pairs={{0,4},{1,5},{2,6},{3,7},{4,8},{5,9},{6,10},{7,11},{8,12},{9,13},{1... | collective-permute-start | bytes 1179656 | tf_op jit(solution)/shard_map/ppermute | solution.py:80
  29.4 52.6 %copy-start.4 = (s32[1,1,12,27]{3,1,2,0:T(1,128)S(1)}, s32[1,1,12,27]{3,1,2,0:T(1,128)}, u32[]{:S(2)}) copy-start(s32[1,1,12,27]{3,1,2,0:T(1,128)} %param.11) | copy-start | bytes 3892
  29.4 52.6 %copy-start.5 = (s32[1,1,12,27]{3,1,2,0:T(1,128)S(1)}, s32[1,1,12,27]{3,1,2,0:T(1,128)}, u32[]{:S(2)}) copy-start(s32[1,1,12,27]{3,1,2,0:T(1,128)} %param.9) | copy-start | bytes 3892
  31.0 51.0 %copy-start.1 = (bf16[1,1,12,64,256]{4,3,2,1,0:T(8,128)(2,1)S(1)}, bf16[1,1,12,64,256]{4,3,2,1,0:T(8,128)(2,1)}, u32[]{:S(2)}) copy-start(bf16[1,1,12,64,256]{4,3,2,1,0:T(8,128)(2,1)} %param.8) | copy-start | bytes 1179652
  39.5 39.2 %collective-permute-start.15 = (bf16[12,64,256]{2,1,0:T(8,128)(2,1)S(1)}, bf16[12,64,256]{2,1,0:T(8,128)(2,1)S(1)}, u32[]{:S(2)}, u32[]{:S(2)}) collective-permute-start(bf16[12,64,256]{2,1,0:T(8,128)(2,1)S(1)} %broadcast_select_fusion), channel_id=1, source_target_pairs={{0,4},{1,5},{2,6},{3,7},{4,8},{5,9},{6,10},{7,11},{8,12},{9,13},{1... | collective-permute-start | bytes 1179656 | tf_op jit(solution)/shard_map/ppermute | solution.py:90
  54.7 1.0 copy-start
  56.7 10.8 %collective-permute-start.2 = (bf16[9,64,256]{2,1,0:T(8,128)(2,1)S(1)}, bf16[9,64,256]{2,1,0:T(8,128)(2,1)S(1)}, u32[]{:S(2)}, u32[]{:S(2)}) collective-permute-start(bf16[9,64,256]{2,1,0:T(8,128)(2,1)S(1)} %get-tuple-element.23), channel_id=1, source_target_pairs={{0,1},{1,2},{2,3},{3,0},{4,5},{5,6},{6,7},{7,4},{8,9},{9,10},{10,1... | collective-permute-start | bytes 884744 | tf_op jit(solution)/shard_map/ppermute | solution.py:66
  58.2 9.8 %collective-permute-start.3 = (bf16[9,64,256]{2,1,0:T(8,128)(2,1)S(1)}, bf16[9,64,256]{2,1,0:T(8,128)(2,1)S(1)}, u32[]{:S(2)}, u32[]{:S(2)}) collective-permute-start(bf16[9,64,256]{2,1,0:T(8,128)(2,1)S(1)} %get-tuple-element.24), channel_id=1, source_target_pairs={{0,3},{1,0},{2,1},{3,2},{4,7},{5,4},{6,5},{7,6},{8,11},{9,8},{10,9... | collective-permute-start | bytes 884744 | tf_op jit(solution)/shard_map/ppermute | solution.py:66
  58.8 15.6 %collective-permute-start.4 = (bf16[9,64,256]{2,1,0:T(8,128)(2,1)S(1)}, bf16[9,64,256]{2,1,0:T(8,128)(2,1)S(1)}, u32[]{:S(2)}, u32[]{:S(2)}) collective-permute-start(bf16[9,64,256]{2,1,0:T(8,128)(2,1)S(1)} %get-tuple-element.25), channel_id=1, source_target_pairs={{0,2},{1,3},{2,0},{3,1},{4,6},{5,7},{6,4},{7,5},{8,10},{9,11},{10,... | collective-permute-start | bytes 884744 | tf_op jit(solution)/shard_map/ppermute | solution.py:66
  64.0 14.0 %collective-permute-start.7 = (bf16[6,64,256]{2,1,0:T(8,128)(2,1)S(1)}, bf16[6,64,256]{2,1,0:T(8,128)(2,1)S(1)}, u32[]{:S(2)}, u32[]{:S(2)}) collective-permute-start(bf16[6,64,256]{2,1,0:T(8,128)(2,1)S(1)} %get-tuple-element.27), channel_id=1, source_target_pairs={{0,1},{1,2},{2,3},{3,0},{4,5},{5,6},{6,7},{7,4},{8,9},{9,10},{10,1... | collective-permute-start | bytes 589832 | tf_op jit(solution)/shard_map/ppermute | solution.py:66
  67.5 15.5 %collective-permute-start.8 = (bf16[6,64,256]{2,1,0:T(8,128)(2,1)}, bf16[6,64,256]{2,1,0:T(8,128)(2,1)S(1)}, u32[]{:S(2)}, u32[]{:S(2)}) collective-permute-start(bf16[6,64,256]{2,1,0:T(8,128)(2,1)} %get-tuple-element.28), channel_id=1, source_target_pairs={{0,3},{1,0},{2,1},{3,2},{4,7},{5,4},{6,5},{7,6},{8,11},{9,8},{10,9... | collective-permute-start | bytes 589832 | tf_op jit(solution)/shard_map/ppermute | solution.py:66
  68.1 17.9 %collective-permute-start.9 = (bf16[6,64,256]{2,1,0:T(8,128)(2,1)}, bf16[6,64,256]{2,1,0:T(8,128)(2,1)S(1)}, u32[]{:S(2)}, u32[]{:S(2)}) collective-permute-start(bf16[6,64,256]{2,1,0:T(8,128)(2,1)} %get-tuple-element.29), channel_id=1, source_target_pairs={{0,2},{1,3},{2,0},{3,1},{4,6},{5,7},{6,4},{7,5},{8,10},{9,11},{10,... | collective-permute-start | bytes 589832 | tf_op jit(solution)/shard_map/ppermute | solution.py:66
  74.4 0.7 copy-start.2
  75.1 10.9 %collective-permute-start.12 = (bf16[6,64,256]{2,1,0:T(8,128)(2,1)}, bf16[6,64,256]{2,1,0:T(8,128)(2,1)S(1)}, u32[]{:S(2)}, u32[]{:S(2)}) collective-permute-start(bf16[6,64,256]{2,1,0:T(8,128)(2,1)} %get-tuple-element.31), channel_id=1, source_target_pairs={{0,1},{1,2},{2,3},{3,0},{4,5},{5,6},{6,7},{7,4},{8,9},{9,10},{10,1... | collective-permute-start | bytes 589832 | tf_op jit(solution)/shard_map/ppermute | solution.py:66
  78.0 10.1 %collective-permute-start.13 = (bf16[6,64,256]{2,1,0:T(8,128)(2,1)}, bf16[6,64,256]{2,1,0:T(8,128)(2,1)}, u32[]{:S(2)}, u32[]{:S(2)}) collective-permute-start(bf16[6,64,256]{2,1,0:T(8,128)(2,1)} %get-tuple-element.32), channel_id=1, source_target_pairs={{0,3},{1,0},{2,1},{3,2},{4,7},{5,4},{6,5},{7,6},{8,11},{9,8},{10,9... | collective-permute-start | bytes 589832 | tf_op jit(solution)/shard_map/ppermute | solution.py:66
  78.7 9.4 %collective-permute-start.14 = (bf16[6,64,256]{2,1,0:T(8,128)(2,1)}, bf16[6,64,256]{2,1,0:T(8,128)(2,1)}, u32[]{:S(2)}, u32[]{:S(2)}) collective-permute-start(bf16[6,64,256]{2,1,0:T(8,128)(2,1)} %get-tuple-element.33), channel_id=1, source_target_pairs={{0,2},{1,3},{2,0},{3,1},{4,6},{5,7},{6,4},{7,5},{8,10},{9,11},{10,... | collective-permute-start | bytes 589832 | tf_op jit(solution)/shard_map/ppermute | solution.py:66
  83.1 5.1 %collective-permute-start.16 = (bf16[3,64,256]{2,1,0:T(8,128)(2,1)S(1)}, bf16[3,64,256]{2,1,0:T(8,128)(2,1)S(1)}, u32[]{:S(2)}, u32[]{:S(2)}) collective-permute-start(bf16[3,64,256]{2,1,0:T(8,128)(2,1)S(1)} %get-tuple-element.35), channel_id=1, source_target_pairs={{0,1},{1,2},{2,3},{3,0},{4,5},{5,6},{6,7},{7,4},{8,9},{9,10},{10,1... | collective-permute-start | bytes 294920 | tf_op jit(solution)/shard_map/ppermute | solution.py:66
  85.9 4.6 %collective-permute-start.17 = (bf16[3,64,256]{2,1,0:T(8,128)(2,1)S(1)}, bf16[3,64,256]{2,1,0:T(8,128)(2,1)S(1)}, u32[]{:S(2)}, u32[]{:S(2)}) collective-permute-start(bf16[3,64,256]{2,1,0:T(8,128)(2,1)S(1)} %get-tuple-element.36), channel_id=1, source_target_pairs={{0,3},{1,0},{2,1},{3,2},{4,7},{5,4},{6,5},{7,6},{8,11},{9,8},{10,9... | collective-permute-start | bytes 294920 | tf_op jit(solution)/shard_map/ppermute | solution.py:66
  85.9 6.2 %collective-permute-start.18 = (bf16[3,64,256]{2,1,0:T(8,128)(2,1)S(1)}, bf16[3,64,256]{2,1,0:T(8,128)(2,1)S(1)}, u32[]{:S(2)}, u32[]{:S(2)}) collective-permute-start(bf16[3,64,256]{2,1,0:T(8,128)(2,1)S(1)} %get-tuple-element.37), channel_id=1, source_target_pairs={{0,2},{1,3},{2,0},{3,1},{4,6},{5,7},{6,4},{7,5},{8,10},{9,11},{10,... | collective-permute-start | bytes 294920 | tf_op jit(solution)/shard_map/ppermute | solution.py:66
  92.2 1.0 copy-start.3
  108.3 94.4 %all-to-all-start.1 = ((bf16[32,256,256]{2,1,0:T(8,128)(2,1)}), bf16[32,256,256]{2,1,0:T(8,128)(2,1)}, u32[]{:S(2)}, u32[]{:S(2)}) async-start(bf16[32,256,256]{2,1,0:T(8,128)(2,1)} %device_tiles.1), calls=%async_computation.1 | async-start | bytes 8388608 | tf_op jit(solution)/shard_map/all_to_all | solution.py:261
  208.9 2.9 %collective-permute-start.19 = (bf16[8,256,256]{2,1,0:T(8,128)(2,1)}, bf16[8,256,256]{2,1,0:T(8,128)(2,1)S(1)}, u32[]{:S(2)}, u32[]{:S(2)}) collective-permute-start(bf16[8,256,256]{2,1,0:T(8,128)(2,1)} %get-tuple-element.40), channel_id=1, source_target_pairs={{0,32},{32,0},{64,96},{96,64},{128,160},{160,128},{192,224},{224,1... | collective-permute-start | bytes 3145736 | tf_op jit(solution)/shard_map/ppermute | solution.py:238
  213.8 10.8 %collective-permute-start.20 = (bf16[2,256,256]{2,1,0:T(8,128)(2,1)S(1)}, bf16[2,256,256]{2,1,0:T(8,128)(2,1)S(1)}, u32[]{:S(2)}, u32[]{:S(2)}) collective-permute-start(bf16[2,256,256]{2,1,0:T(8,128)(2,1)S(1)} %get-tuple-element.43), channel_id=1, source_target_pairs={{0,128},{32,160},{64,192},{96,224},{128,0},{160,32},{192,64},{224,... | collective-permute-start | bytes 786440 | tf_op jit(solution)/shard_map/ppermute | solution.py:243
  217.1 12.7 %collective-permute-start.22 = (bf16[2,256,256]{2,1,0:T(8,128)(2,1)S(1)}, bf16[2,256,256]{2,1,0:T(8,128)(2,1)S(1)}, u32[]{:S(2)}, u32[]{:S(2)}) collective-permute-start(bf16[2,256,256]{2,1,0:T(8,128)(2,1)S(1)} %get-tuple-element.44), channel_id=1, source_target_pairs={{0,192},{32,224},{64,0},{96,32},{128,64},{160,96},{192,128},{224,1... | collective-permute-start | bytes 786440 | tf_op jit(solution)/shard_map/ppermute | solution.py:243
  218.1 11.6 %collective-permute-start.21 = (bf16[2,256,256]{2,1,0:T(8,128)(2,1)S(1)}, bf16[2,256,256]{2,1,0:T(8,128)(2,1)S(1)}, u32[]{:S(2)}, u32[]{:S(2)}) collective-permute-start(bf16[2,256,256]{2,1,0:T(8,128)(2,1)S(1)} %get-tuple-element.45), channel_id=1, source_target_pairs={{0,64},{32,96},{64,128},{96,160},{128,192},{160,224},{192,0},{224,... | collective-permute-start | bytes 786440 | tf_op jit(solution)/shard_map/ppermute | solution.py:243

commit v5 on v4

--- a/solution.py
+++ b/solution.py
@@ -72,9 +72,10 @@
     asked = jnp.broadcast_to(fetched, (n_z, n_x, n_x * NCAP)).reshape(n_z * n_x, n_x * NCAP)
     asked = jnp.concatenate([labels[:, None], asked], axis=1)
 
+    asks = lax.all_to_all(asked, "dev", split_axis=0, concat_axis=0, tiled=True)
     up = lax.ppermute(panels, "dev", along_z(1))
     down = lax.ppermute(panels, "dev", along_z(-1))
-    asks = lax.all_to_all(asked, "dev", split_axis=0, concat_axis=0, tiled=True)
+    forward((0,), (panels,))
     for k in range(1, half):
         if k + 1 < half:
             new_up = lax.ppermute(up, "dev", along_z(1))
@@ -88,10 +89,7 @@
                 for s, t in along_z(-1 if g % 2 else 1)
             ]
             far = lax.ppermute(jnp.where(odd, down, up), ("grp", "dev"), pairs)
-        if k == 1:
-            forward((0, k, -k), (panels, up, down))
-        else:
-            forward((k, -k), (up, down))
+        forward((k, -k), (up, down))
         up, down = new_up, new_down
     forward((half,), (far,))
 
@@ -103,21 +101,26 @@
 
 
 def tiles_kernel(spots, cols_ref, slots_ref, places_ref, where_ref, a_hbm, pt_ref, *refs):
-    piece_refs, (out_ref, a_ref, b_ref, near_ref, a_sems) = refs[: len(spots)], refs[len(spots) :]
+    piece_refs, (out_ref, a_ref, b_ref, near_ref, a_sems, b_sems) = refs[: len(spots)], refs[len(spots) :]
 
     def load(row):
         return pltpu.make_async_copy(a_hbm.at[row], a_ref.at[row], a_sems.at[row])
 
     for row in range(R):
         load(row).start()
+    copies = []
     for piece_ref, parts in zip(piece_refs, spots):
         for start, n, place in parts:
-            for i in range(n):
-                b_ref[place + i] = piece_ref[start + i]
+            from_ref, to_ref = piece_ref.at[pl.ds(start, n)], b_ref.at[pl.ds(place, n)]
+            copies.append(pltpu.make_async_copy(from_ref, to_ref, b_sems.at[len(copies)]))
+            copies[-1].start()
 
     @pl.loop(0, LT)
     def _(t):
         near_ref[t] = jnp.zeros(near_ref.shape[1:], jnp.float32)
+
+    for copy in copies:
+        copy.wait()
 
     lane = lax.broadcasted_iota(jnp.int32, (BLOCK, PAIR), 1)
     left = jnp.where(lane < BLOCK, 1.0, 0.0).astype(jnp.bfloat16)
@@ -165,15 +168,16 @@
     return pl.pallas_call(
         functools.partial(tiles_kernel, spots),
         out_shape=jax.ShapeDtypeStruct((n_places, W, W), jnp.bfloat16),
-        in_specs=[smem] * 4 + [hbm, vmem] + [vmem] * len(pieces),
+        in_specs=[smem] * 4 + [hbm, vmem] + [pl.BlockSpec(memory_space=pl.ANY)] * len(pieces),
         out_specs=vmem,
         scratch_shapes=[
             pltpu.VMEM((R, BLOCK, K * BLOCK), jnp.bfloat16),
             pltpu.VMEM((n_panels, BLOCK, W), jnp.bfloat16),
             pltpu.VMEM((LT + 1, R * BLOCK, W), jnp.float32),
             pltpu.SemaphoreType.DMA((R,)),
+            pltpu.SemaphoreType.DMA((sum(len(parts) for parts in spots),)),
         ],
-        compiler_params=pltpu.CompilerParams(vmem_limit_bytes=50 << 20),
+        compiler_params=pltpu.CompilerParams(vmem_limit_bytes=51 << 20),
         cost_estimate=pl.CostEstimate(
             flops=8_000_000_000, bytes_accessed=12_000_000, transcendentals=0
         ),
@@ -181,8 +185,9 @@
     )(cols, slots, places, where, blocks, pt, *pieces)
 
 
-def table_kernel(labels_ref, got_ref, here_ref, there_ref, sum_ref):
-    n_here, n_there = here_ref.shape[0], there_ref.shape[0]
+def table_kernel(labels_ref, got_ref, *refs):
+    here_refs, (there_ref, sum_ref) = refs[:-2], refs[-2:]
+    n_here, n_there = len(here_refs) * CT, there_ref.shape[0]
 
     @pl.loop(0, n_here + n_there)
     def _(t):
@@ -191,12 +196,14 @@
     @pl.loop(0, got_ref.shape[0])
     def _(s):
         label = labels_ref[s]
-        at = jnp.where(label < 0, n_here + n_there, label)
-        sum_ref[at] += got_ref[s].astype(jnp.float32)
-
-    @pl.loop(0, n_here)
-    def _(t):
-        here_ref[t] = sum_ref[t]
+
+        @pl.when(label >= 0)
+        def _():
+            sum_ref[label] += got_ref[s].astype(jnp.float32)
+
+    for i, here_ref in enumerate(here_refs):
+        for t in range(CT):
+            here_ref[t] = sum_ref[i * CT + t]
 
     @pl.loop(0, n_there)
     def _(t):
@@ -209,15 +216,15 @@
     return pl.pallas_call(
         table_kernel,
         out_shape=[
-            jax.ShapeDtypeStruct((n_here, W, W), jnp.float32),
+            *[jax.ShapeDtypeStruct((CT, W, W), jnp.float32)] * (n_here // CT),
             jax.ShapeDtypeStruct((n_there, W, W), jnp.bfloat16),
         ],
         grid_spec=pltpu.PrefetchScalarGridSpec(
             num_scalar_prefetch=1,
             grid=(W // rows,),
             in_specs=[block(got.shape[0])],
-            out_specs=[block(n_here), block(n_there)],
-            scratch_shapes=[pltpu.VMEM((n_here + n_there + 1, rows, W), jnp.float32)],
+            out_specs=[block(CT)] * (n_here // CT) + [block(n_there)],
+            scratch_shapes=[pltpu.VMEM((n_here + n_there, rows, W), jnp.float32)],
         ),
         compiler_params=pltpu.CompilerParams(dimension_semantics=("arbitrary",)),
         cost_estimate=pl.CostEstimate(flops=2_000_000, bytes_accessed=7_000_000, transcendentals=0),
@@ -233,14 +240,17 @@
     dy = (to // cores - y) % n_y
     other = (to % cores - core) % cores
     at = jnp.where(labels < 0, -1, (other * n_y + dy) * CT + place)
-    here, there = table_of(at, got, n_y * CT, n_y * CT)
+    *here, there = table_of(at, got, n_y * CT, n_y * CT)
     swap = [(g, g // cores * cores + (g + 1) % cores) for g in range(groups)]
-    here += lax.ppermute(there, "grp", swap).astype(jnp.float32)
-    total = here[:CT]
+    there = lax.ppermute(there, "grp", swap)
+
+    def of_chip(step):
+        return here[step] + there[step * CT : (step + 1) * CT].astype(jnp.float32)
+
+    total = of_chip(0)
     for step in (2, 1, 3):
         pairs = [(g, (g + step * cores) % groups) for g in range(groups)]
-        part = here[step * CT : (step + 1) * CT].astype(jnp.bfloat16)
-        total += lax.ppermute(part, "grp", pairs).astype(jnp.float32)
+        total += lax.ppermute(of_chip(step).astype(jnp.bfloat16), "grp", pairs).astype(jnp.float32)
     return total
 
 

time: 232 us -> 244 us (1.052)
  Pallas kernels: 26.6 us -> 31.9 us
  local copies, waits for them, and re-layouts: 3.95 us -> 6.95 us
    pallas_call x1, Pallas kernels: 15.2 us -> 19.3 us  [device_tiles(): pl.pallas_call(functools.partial(tiles_kernel, spots), out_shape=jax.Shap...]
    unnamed x14 -> x24, local copies, waits for them, and re-layouts: 3.45 us -> 5.75 us
    ppermute x12 -> x15, starting transfers between devices: 23.2 us -> 24.5 us  [forward(): block = lax.ppermute(block, 'dev', along_x(step))]
    pallas_call x4 -> x5, Pallas kernels: 5.16 us -> 6.01 us  [pick(): pl.pallas_call(functools.partial(pick_kernel, n_x, ups), out_shape=[jax.S...]
    ppermute x12 -> x15, waiting for transfers between devices: 7.05 us -> 6.38 us  [forward(): block = lax.ppermute(block, 'dev', along_x(step))]
  transfers between devices with their start and end apart: 24 -> 27, of which waited for: 13 -> 13; matrix products, arithmetic and copies ran while one was open for 1% -> 1% of each run, Pallas kernels for 2% -> 2%
where the time goes in v5:
time: 244 us; the launch traced here: 243 us
  waiting for transfers between devices  134 us (55%)
  starting transfers between devices  50 us (20%)
  Pallas kernels  31.9 us (13%)
  blocking collectives  15.1 us (6%)
  local copies, waits for them, and re-layouts  6.95 us (3%)
  other arithmetic  5.08 us (2%)
    all_to_all x1, waiting for transfers between devices, layer(): lax.all_to_all(sending, 'dev', split_axis=0, concat_axis=0, tiled=True)  89 us
    ppermute x15, starting transfers between devices, forward(): block = lax.ppermute(block, 'dev', along_x(step))  24.5 us
    pallas_call x1, Pallas kernels, device_tiles(): pl.pallas_call(functools.partial(tiles_kernel, spots), out_shape=jax.Shap...  19.3 us
    all_to_all x1, blocking collectives, fetch(): asks = lax.all_to_all(asked, 'dev', split_axis=0, concat_axis=0, tiled=True)  15.1 us
    ppermute x2, waiting for transfers between devices, fetch(): new_down = lax.ppermute(down, 'dev', along_z(-1))  12.5 us
    ppermute x3, waiting for transfers between devices, sum_over_groups(): lax.ppermute(of_chip(step).astype(jnp.bfloat16), 'grp', pairs)  10.7 us
    ppermute x1, waiting for transfers between devices, fetch(): down = lax.ppermute(panels, 'dev', along_z(-1))  8.69 us
    ppermute x2, starting transfers between devices, fetch(): new_down = lax.ppermute(down, 'dev', along_z(-1))  7.28 us
  transfers between devices with their start and end apart: 27, of which 13 were waited for; matrix products, arithmetic and copies ran while one was open for 1% of the time, Pallas kernels for 2%

profile of v5, /device:TPU:4, one launch (start us, length us, event | category | flops | bytes accessed | tf_op | source)
XLA Modules:
  0.0 242.8 jit_solution(17965271138063897606)
XLA Ops:
  0.0 5.9 %collective-permute-start.4 = (bf16[12,64,256]{2,1,0:T(8,128)(2,1)}, bf16[12,64,256]{2,1,0:T(8,128)(2,1)S(1)}, u32[]{:S(2)}, u32[]{:S(2)}) collective-permute-start(bf16[12,64,256]{2,1,0:T(8,128)(2,1)} %bitcast.35), channel_id=1, source_target_pairs={{0,28},{1,29},{2,30},{3,31},{4,0},{5,1},{6,2},{7,3},{8,4},{9,5},{1... | collective-permute-start | bytes 1179656 | tf_op jit(solution)/shard_map/ppermute | solution.py:77
  5.9 8.7 %collective-permute-done.4.refs_1_ = bf16[12,64,256]{2,1,0:T(8,128)(2,1)S(1)} collective-permute-done((bf16[12,64,256]{2,1,0:T(8,128)(2,1)}, bf16[12,64,256]{2,1,0:T(8,128)(2,1)S(1)}, u32[]{:S(2)}, u32[]{:S(2)}) %collective-permute-start.4) | collective-permute-done | bytes 393248 | tf_op jit(solution)/shard_map/ppermute | solution.py:77
  14.6 3.6 %collective-permute-start.9 = (bf16[12,64,256]{2,1,0:T(8,128)(2,1)S(1)}, bf16[12,64,256]{2,1,0:T(8,128)(2,1)S(1)}, u32[]{:S(2)}, u32[]{:S(2)}) collective-permute-start(bf16[12,64,256]{2,1,0:T(8,128)(2,1)S(1)} %collective-permute-done.4.refs_1_), channel_id=1, source_target_pairs={{0,28},{1,29},{2,30},{3,31},{4,0},{5,1},{6,2},{7,3},{8,4},{9,5},{1... | collective-permute-start | bytes 1179656 | tf_op jit(solution)/shard_map/ppermute | solution.py:82
  18.2 7.5 %collective-permute-done.9.refs_1_ = bf16[12,64,256]{2,1,0:T(8,128)(2,1)S(1)} collective-permute-done((bf16[12,64,256]{2,1,0:T(8,128)(2,1)S(1)}, bf16[12,64,256]{2,1,0:T(8,128)(2,1)S(1)}, u32[]{:S(2)}, u32[]{:S(2)}) %collective-permute-start.9) | collective-permute-done | bytes 393248 | tf_op jit(solution)/shard_map/ppermute | solution.py:82
  25.7 3.7 %collective-permute-start.14 = (bf16[12,64,256]{2,1,0:T(8,128)(2,1)S(1)}, bf16[12,64,256]{2,1,0:T(8,128)(2,1)S(1)}, u32[]{:S(2)}, u32[]{:S(2)}) collective-permute-start(bf16[12,64,256]{2,1,0:T(8,128)(2,1)S(1)} %collective-permute-done.9.refs_1_), channel_id=1, source_target_pairs={{0,28},{1,29},{2,30},{3,31},{4,0},{5,1},{6,2},{7,3},{8,4},{9,5},{1... | collective-permute-start | bytes 1179656 | tf_op jit(solution)/shard_map/ppermute | solution.py:82
  31.1 5.0 %collective-permute-done.14.refs_1_ = bf16[12,64,256]{2,1,0:T(8,128)(2,1)S(1)} collective-permute-done((bf16[12,64,256]{2,1,0:T(8,128)(2,1)S(1)}, bf16[12,64,256]{2,1,0:T(8,128)(2,1)S(1)}, u32[]{:S(2)}, u32[]{:S(2)}) %collective-permute-start.14) | collective-permute-done | bytes 393248 | tf_op jit(solution)/shard_map/ppermute | solution.py:82
  36.1 3.4 %collective-permute-done.13.refs_0_ = bf16[12,64,256]{2,1,0:T(8,128)(2,1)S(1)} collective-permute-done((bf16[12,64,256]{2,1,0:T(8,128)(2,1)S(1)}, bf16[12,64,256]{2,1,0:T(8,128)(2,1)S(1)}, u32[]{:S(2)}, u32[]{:S(2)}) %collective-permute-start.13) | collective-permute-done | bytes 393248 | tf_op jit(solution)/shard_map/ppermute | solution.py:81
  39.7 15.1 %all_to_all.16 = s32[32,1,13]{2,1,0:T(1,128)S(1)} all-to-all(s32[32,1,13]{2,1,0:T(1,128)S(1)} %bitcast.47), channel_id=1, replica_groups=mesh['grp'=8,'dev'=32] {'dev'}, dimensions={0} | all-to-all | bytes 3328 | tf_op jit(solution)/shard_map/all_to_all | solution.py:75
  56.7 1.5 collective-permute-start
  58.8 3.5 %collective-permute-start.2 = (bf16[3,64,256]{2,1,0:T(8,128)(2,1)S(1)}, bf16[3,64,256]{2,1,0:T(8,128)(2,1)S(1)}, u32[]{:S(2)}, u32[]{:S(2)}) collective-permute-start(bf16[3,64,256]{2,1,0:T(8,128)(2,1)S(1)} %get-tuple-element.32), channel_id=1, source_target_pairs={{0,2},{1,3},{2,0},{3,1},{4,6},{5,7},{6,4},{7,5},{8,10},{9,11},{10,... | collective-permute-start | bytes 294920 | tf_op jit(solution)/shard_map/ppermute | solution.py:66
  63.3 1.7 pick.7
  65.6 2.0 collective-permute-start.6
  68.3 1.2 collective-permute-start.7
  69.5 1.5 collective-permute-start.10
  71.0 1.7 pick.8
  72.8 1.4 collective-permute-start.11
  74.2 3.8 %collective-permute-start.12 = (bf16[6,64,256]{2,1,0:T(8,128)(2,1)}, bf16[6,64,256]{2,1,0:T(8,128)(2,1)S(1)}, u32[]{:S(2)}, u32[]{:S(2)}) collective-permute-start(bf16[6,64,256]{2,1,0:T(8,128)(2,1)} %get-tuple-element.40), channel_id=1, source_target_pairs={{0,2},{1,3},{2,0},{3,1},{4,6},{5,7},{6,4},{7,5},{8,10},{9,11},{10,... | collective-permute-start | bytes 589832 | tf_op jit(solution)/shard_map/ppermute | solution.py:66
  78.0 2.3 collective-permute-start.15
  80.2 1.7 collective-permute-done.10.refs_8_
  85.4 2.3 collective-permute-start.19
  88.9 2.6 %collective-permute-start.21 = (bf16[3,64,256]{2,1,0:T(8,128)(2,1)S(1)}, bf16[3,64,256]{2,1,0:T(8,128)(2,1)S(1)}, u32[]{:S(2)}, u32[]{:S(2)}) collective-permute-start(bf16[3,64,256]{2,1,0:T(8,128)(2,1)S(1)} %get-tuple-element.48), channel_id=1, source_target_pairs={{0,2},{1,3},{2,0},{3,1},{4,6},{5,7},{6,4},{7,5},{8,10},{9,11},{10,... | collective-permute-start | bytes 294920 | tf_op jit(solution)/shard_map/ppermute | solution.py:66
  92.9 2.1 collective-permute-done.21.refs_18_
  97.7 19.3 %device_tiles.1 = bf16[32,256,256]{2,1,0:T(8,128)(2,1)} custom-call(s32[12,27]{1,0:T(8,128)S(1)} %get-tuple-element.61.cols_ref, s32[12,27]{1,0:T(8,128)S(1)} %get-tuple-element.60.slots_ref, s32[16]{0:T(128)S(1)} %get-tuple-element.58.places_ref, s32[96]{0:T(128)S(1)} %fusion.where_ref, bf16[12,64,1728]{2,1,0:T(8,128)(2,1)} %bitcast.49, ...), custom_call_target="tpu_custom_call" | custom-call | flops 8000000000 | bytes 12000000 | tf_op jit(solution)/shard_map/device_tiles/pallas_call | solution.py:168
  117.0 7.0 %all-to-all-start.1 = ((bf16[32,256,256]{2,1,0:T(8,128)(2,1)}), bf16[32,256,256]{2,1,0:T(8,128)(2,1)}, u32[]{:S(2)}, u32[]{:S(2)}) async-start(bf16[32,256,256]{2,1,0:T(8,128)(2,1)} %device_tiles.1), calls=%async_computation.1 | async-start | bytes 8388608 | tf_op jit(solution)/shard_map/all_to_all | solution.py:271
  124.8 89.0 %all-to-all-done.1.got_ref = bf16[32,256,256]{2,1,0:T(8,128)(2,1)} async-done(((bf16[32,256,256]{2,1,0:T(8,128)(2,1)}), bf16[32,256,256]{2,1,0:T(8,128)(2,1)}, u32[]{:S(2)}, u32[]{:S(2)}) %all-to-all-start.1) | async-done | bytes 4194336 | tf_op jit(solution)/shard_map/all_to_all | solution.py:271
  213.8 6.6 %table_of.1 = (f32[2,256,256]{2,1,0:T(8,128)}, f32[2,256,256]{2,1,0:T(8,128)}, f32[2,256,256]{2,1,0:T(8,128)}, f32[2,256,256]{2,1,0:T(8,128)}, bf16[8,256,256]{2,1,0:T(8,128)(2,1)}) custom-call(s32[32]{0:T(128)} %fusion.4.labels_ref, bf16[32,256,256]{2,1,0:T(8,128)(2,1)} %all-to-all-done.1.got_ref), custom_call_target="tpu_custom_call" | custom-call | flops 2000000 | bytes 7000000 | tf_op jit(solution)/shard_map/table_of/pallas_call | solution.py:216
  220.4 2.9 %collective-permute-done.22 = bf16[8,256,256]{2,1,0:T(8,128)(2,1)S(1)} collective-permute-done((bf16[8,256,256]{2,1,0:T(8,128)(2,1)}, bf16[8,256,256]{2,1,0:T(8,128)(2,1)S(1)}, u32[]{:S(2)}, u32[]{:S(2)}) %collective-permute-start.22) | collective-permute-done | bytes 1048608 | tf_op jit(solution)/shard_map/ppermute | solution.py:245
  223.3 1.5 add_convert_fusion.2
  224.8 3.2 %collective-permute-start.23 = (bf16[2,256,256]{2,1,0:T(8,128)(2,1)S(1)}, bf16[2,256,256]{2,1,0:T(8,128)(2,1)S(1)}, u32[]{:S(2)}, u32[]{:S(2)}) collective-permute-start(bf16[2,256,256]{2,1,0:T(8,128)(2,1)S(1)} %get-tuple-element.55), channel_id=1, source_target_pairs={{0,128},{32,160},{64,192},{96,224},{128,0},{160,32},{192,64},{224,... | collective-permute-start | bytes 786440 | tf_op jit(solution)/shard_map/ppermute | solution.py:253
  230.1 5.5 %collective-permute-done.23 = bf16[2,256,256]{2,1,0:T(8,128)(2,1)S(1)} collective-permute-done((bf16[2,256,256]{2,1,0:T(8,128)(2,1)S(1)}, bf16[2,256,256]{2,1,0:T(8,128)(2,1)S(1)}, u32[]{:S(2)}, u32[]{:S(2)}) %collective-permute-start.23) | collective-permute-done | bytes 262176 | tf_op jit(solution)/shard_map/ppermute | solution.py:253
  235.6 5.2 %collective-permute-done.25 = bf16[2,256,256]{2,1,0:T(8,128)(2,1)S(1)} collective-permute-done((bf16[2,256,256]{2,1,0:T(8,128)(2,1)S(1)}, bf16[2,256,256]{2,1,0:T(8,128)(2,1)S(1)}, u32[]{:S(2)}, u32[]{:S(2)}) %collective-permute-start.25) | collective-permute-done | bytes 262176 | tf_op jit(solution)/shard_map/ppermute | solution.py:253
  240.8 2.0 add_bitcast_fusion
  (67 shorter events, 18.2 us)
Async XLA Ops:
  0.0 83.6 %copy-start.1 = (bf16[1,1,12,64,256]{4,3,2,1,0:T(8,128)(2,1)S(1)}, bf16[1,1,12,64,256]{4,3,2,1,0:T(8,128)(2,1)}, u32[]{:S(2)}) copy-start(bf16[1,1,12,64,256]{4,3,2,1,0:T(8,128)(2,1)} %param.8) | copy-start | bytes 1179652
  0.0 83.6 %copy-start.9 = (s32[1,1,12,27]{3,1,2,0:T(1,128)S(1)}, s32[1,1,12,27]{3,1,2,0:T(1,128)}, u32[]{:S(2)}) copy-start(s32[1,1,12,27]{3,1,2,0:T(1,128)} %param.11) | copy-start | bytes 3892
  0.0 83.6 %copy-start.10 = (s32[1,1,12,27]{3,1,2,0:T(1,128)S(1)}, s32[1,1,12,27]{3,1,2,0:T(1,128)}, u32[]{:S(2)}) copy-start(s32[1,1,12,27]{3,1,2,0:T(1,128)} %param.9) | copy-start | bytes 3892
  0.0 14.6 %collective-permute-start.4 = (bf16[12,64,256]{2,1,0:T(8,128)(2,1)}, bf16[12,64,256]{2,1,0:T(8,128)(2,1)S(1)}, u32[]{:S(2)}, u32[]{:S(2)}) collective-permute-start(bf16[12,64,256]{2,1,0:T(8,128)(2,1)} %bitcast.35), channel_id=1, source_target_pairs={{0,28},{1,29},{2,30},{3,31},{4,0},{5,1},{6,2},{7,3},{8,4},{9,5},{1... | collective-permute-start | bytes 1179656 | tf_op jit(solution)/shard_map/ppermute | solution.py:77
  5.9 12.3 %collective-permute-start.3 = (bf16[12,64,256]{2,1,0:T(8,128)(2,1)}, bf16[12,64,256]{2,1,0:T(8,128)(2,1)S(1)}, u32[]{:S(2)}, u32[]{:S(2)}) collective-permute-start(bf16[12,64,256]{2,1,0:T(8,128)(2,1)} %bitcast.36), channel_id=1, source_target_pairs={{0,4},{1,5},{2,6},{3,7},{4,8},{5,9},{6,10},{7,11},{8,12},{9,13},{1... | collective-permute-start | bytes 1179656 | tf_op jit(solution)/shard_map/ppermute | solution.py:76
  14.6 11.1 %collective-permute-start.9 = (bf16[12,64,256]{2,1,0:T(8,128)(2,1)S(1)}, bf16[12,64,256]{2,1,0:T(8,128)(2,1)S(1)}, u32[]{:S(2)}, u32[]{:S(2)}) collective-permute-start(bf16[12,64,256]{2,1,0:T(8,128)(2,1)S(1)} %collective-permute-done.4.refs_1_), channel_id=1, source_target_pairs={{0,28},{1,29},{2,30},{3,31},{4,0},{5,1},{6,2},{7,3},{8,4},{9,5},{1... | collective-permute-start | bytes 1179656 | tf_op jit(solution)/shard_map/ppermute | solution.py:82
  18.2 11.2 %collective-permute-start.8 = (bf16[12,64,256]{2,1,0:T(8,128)(2,1)S(1)}, bf16[12,64,256]{2,1,0:T(8,128)(2,1)S(1)}, u32[]{:S(2)}, u32[]{:S(2)}) collective-permute-start(bf16[12,64,256]{2,1,0:T(8,128)(2,1)S(1)} %collective-permute-done.3.refs_0_), channel_id=1, source_target_pairs={{0,4},{1,5},{2,6},{3,7},{4,8},{5,9},{6,10},{7,11},{8,12},{9,13},{1... | collective-permute-start | bytes 1179656 | tf_op jit(solution)/shard_map/ppermute | solution.py:81
  25.7 10.4 %collective-permute-start.14 = (bf16[12,64,256]{2,1,0:T(8,128)(2,1)S(1)}, bf16[12,64,256]{2,1,0:T(8,128)(2,1)S(1)}, u32[]{:S(2)}, u32[]{:S(2)}) collective-permute-start(bf16[12,64,256]{2,1,0:T(8,128)(2,1)S(1)} %collective-permute-done.9.refs_1_), channel_id=1, source_target_pairs={{0,28},{1,29},{2,30},{3,31},{4,0},{5,1},{6,2},{7,3},{8,4},{9,5},{1... | collective-permute-start | bytes 1179656 | tf_op jit(solution)/shard_map/ppermute | solution.py:82
  29.4 10.1 %collective-permute-start.13 = (bf16[12,64,256]{2,1,0:T(8,128)(2,1)S(1)}, bf16[12,64,256]{2,1,0:T(8,128)(2,1)S(1)}, u32[]{:S(2)}, u32[]{:S(2)}) collective-permute-start(bf16[12,64,256]{2,1,0:T(8,128)(2,1)S(1)} %collective-permute-done.8.refs_0_), channel_id=1, source_target_pairs={{0,4},{1,5},{2,6},{3,7},{4,8},{5,9},{6,10},{7,11},{8,12},{9,13},{1... | collective-permute-start | bytes 1179656 | tf_op jit(solution)/shard_map/ppermute | solution.py:81
  39.6 42.8 %collective-permute-start.18 = (bf16[12,64,256]{2,1,0:T(8,128)(2,1)S(1)}, bf16[12,64,256]{2,1,0:T(8,128)(2,1)S(1)}, u32[]{:S(2)}, u32[]{:S(2)}) collective-permute-start(bf16[12,64,256]{2,1,0:T(8,128)(2,1)S(1)} %broadcast_select_fusion), channel_id=1, source_target_pairs={{0,4},{1,5},{2,6},{3,7},{4,8},{5,9},{6,10},{7,11},{8,12},{9,13},{1... | collective-permute-start | bytes 1179656 | tf_op jit(solution)/shard_map/ppermute | solution.py:91
  56.7 8.3 %collective-permute-start = (bf16[3,64,256]{2,1,0:T(8,128)(2,1)S(1)}, bf16[3,64,256]{2,1,0:T(8,128)(2,1)S(1)}, u32[]{:S(2)}, u32[]{:S(2)}) collective-permute-start(bf16[3,64,256]{2,1,0:T(8,128)(2,1)S(1)} %get-tuple-element.30), channel_id=1, source_target_pairs={{0,1},{1,2},{2,3},{3,0},{4,5},{5,6},{6,7},{7,4},{8,9},{9,10},{10,1... | collective-permute-start | bytes 294920 | tf_op jit(solution)/shard_map/ppermute | solution.py:66
  58.2 9.4 %collective-permute-start.1 = (bf16[3,64,256]{2,1,0:T(8,128)(2,1)S(1)}, bf16[3,64,256]{2,1,0:T(8,128)(2,1)S(1)}, u32[]{:S(2)}, u32[]{:S(2)}) collective-permute-start(bf16[3,64,256]{2,1,0:T(8,128)(2,1)S(1)} %get-tuple-element.31), channel_id=1, source_target_pairs={{0,3},{1,0},{2,1},{3,2},{4,7},{5,4},{6,5},{7,6},{8,11},{9,8},{10,9... | collective-permute-start | bytes 294920 | tf_op jit(solution)/shard_map/ppermute | solution.py:66
  58.8 10.7 %collective-permute-start.2 = (bf16[3,64,256]{2,1,0:T(8,128)(2,1)S(1)}, bf16[3,64,256]{2,1,0:T(8,128)(2,1)S(1)}, u32[]{:S(2)}, u32[]{:S(2)}) collective-permute-start(bf16[3,64,256]{2,1,0:T(8,128)(2,1)S(1)} %get-tuple-element.32), channel_id=1, source_target_pairs={{0,2},{1,3},{2,0},{3,1},{4,6},{5,7},{6,4},{7,5},{8,10},{9,11},{10,... | collective-permute-start | bytes 294920 | tf_op jit(solution)/shard_map/ppermute | solution.py:66
  63.2 9.5 %collective-permute-start.5 = (bf16[6,64,256]{2,1,0:T(8,128)(2,1)S(1)}, bf16[6,64,256]{2,1,0:T(8,128)(2,1)S(1)}, u32[]{:S(2)}, u32[]{:S(2)}) collective-permute-start(bf16[6,64,256]{2,1,0:T(8,128)(2,1)S(1)} %get-tuple-element.34), channel_id=1, source_target_pairs={{0,1},{1,2},{2,3},{3,0},{4,5},{5,6},{6,7},{7,4},{8,9},{9,10},{10,1... | collective-permute-start | bytes 589832 | tf_op jit(solution)/shard_map/ppermute | solution.py:66
  65.6 8.5 %collective-permute-start.6 = (bf16[6,64,256]{2,1,0:T(8,128)(2,1)S(1)}, bf16[6,64,256]{2,1,0:T(8,128)(2,1)S(1)}, u32[]{:S(2)}, u32[]{:S(2)}) collective-permute-start(bf16[6,64,256]{2,1,0:T(8,128)(2,1)S(1)} %get-tuple-element.35), channel_id=1, source_target_pairs={{0,3},{1,0},{2,1},{3,2},{4,7},{5,4},{6,5},{7,6},{8,11},{9,8},{10,9... | collective-permute-start | bytes 589832 | tf_op jit(solution)/shard_map/ppermute | solution.py:66
  68.3 9.7 %collective-permute-start.7 = (bf16[6,64,256]{2,1,0:T(8,128)(2,1)S(1)}, bf16[6,64,256]{2,1,0:T(8,128)(2,1)S(1)}, u32[]{:S(2)}, u32[]{:S(2)}) collective-permute-start(bf16[6,64,256]{2,1,0:T(8,128)(2,1)S(1)} %get-tuple-element.36), channel_id=1, source_target_pairs={{0,2},{1,3},{2,0},{3,1},{4,6},{5,7},{6,4},{7,5},{8,10},{9,11},{10,... | collective-permute-start | bytes 589832 | tf_op jit(solution)/shard_map/ppermute | solution.py:66
  69.5 12.9 %copy-start.7 = (bf16[3,64,256]{2,1,0:T(8,128)(2,1)}, bf16[3,64,256]{2,1,0:T(8,128)(2,1)S(1)}, u32[]{:S(2)}) copy-start(bf16[3,64,256]{2,1,0:T(8,128)(2,1)S(1)} %collective-permute-done.2.refs_2_) | copy-start | bytes 294916
  69.5 12.4 %collective-permute-start.10 = (bf16[6,64,256]{2,1,0:T(8,128)(2,1)S(1)}, bf16[6,64,256]{2,1,0:T(8,128)(2,1)S(1)}, u32[]{:S(2)}, u32[]{:S(2)}) collective-permute-start(bf16[6,64,256]{2,1,0:T(8,128)(2,1)S(1)} %get-tuple-element.38), channel_id=1, source_target_pairs={{0,1},{1,2},{2,3},{3,0},{4,5},{5,6},{6,7},{7,4},{8,9},{9,10},{10,1... | collective-permute-start | bytes 589832 | tf_op jit(solution)/shard_map/ppermute | solution.py:66
  72.8 22.3 %copy-start.2 = (bf16[6,64,256]{2,1,0:T(8,128)(2,1)}, bf16[6,64,256]{2,1,0:T(8,128)(2,1)S(1)}, u32[]{:S(2)}) copy-start(bf16[6,64,256]{2,1,0:T(8,128)(2,1)S(1)} %get-tuple-element.45.refs_15_) | copy-start | bytes 589828
  72.8 12.7 %collective-permute-start.11 = (bf16[6,64,256]{2,1,0:T(8,128)(2,1)}, bf16[6,64,256]{2,1,0:T(8,128)(2,1)S(1)}, u32[]{:S(2)}, u32[]{:S(2)}) collective-permute-start(bf16[6,64,256]{2,1,0:T(8,128)(2,1)} %get-tuple-element.39), channel_id=1, source_target_pairs={{0,3},{1,0},{2,1},{3,2},{4,7},{5,4},{6,5},{7,6},{8,11},{9,8},{10,9... | collective-permute-start | bytes 589832 | tf_op jit(solution)/shard_map/ppermute | solution.py:66
  74.2 13.5 %collective-permute-start.12 = (bf16[6,64,256]{2,1,0:T(8,128)(2,1)}, bf16[6,64,256]{2,1,0:T(8,128)(2,1)S(1)}, u32[]{:S(2)}, u32[]{:S(2)}) collective-permute-start(bf16[6,64,256]{2,1,0:T(8,128)(2,1)} %get-tuple-element.40), channel_id=1, source_target_pairs={{0,2},{1,3},{2,0},{3,1},{4,6},{5,7},{6,4},{7,5},{8,10},{9,11},{10,... | collective-permute-start | bytes 589832 | tf_op jit(solution)/shard_map/ppermute | solution.py:66
  78.0 10.9 %collective-permute-start.15 = (bf16[6,64,256]{2,1,0:T(8,128)(2,1)}, bf16[6,64,256]{2,1,0:T(8,128)(2,1)S(1)}, u32[]{:S(2)}, u32[]{:S(2)}) collective-permute-start(bf16[6,64,256]{2,1,0:T(8,128)(2,1)} %get-tuple-element.42), channel_id=1, source_target_pairs={{0,1},{1,2},{2,3},{3,0},{4,5},{5,6},{6,7},{7,4},{8,9},{9,10},{10,1... | collective-permute-start | bytes 589832 | tf_op jit(solution)/shard_map/ppermute | solution.py:66
  81.9 9.6 %collective-permute-start.16 = (bf16[6,64,256]{2,1,0:T(8,128)(2,1)}, bf16[6,64,256]{2,1,0:T(8,128)(2,1)S(1)}, u32[]{:S(2)}, u32[]{:S(2)}) collective-permute-start(bf16[6,64,256]{2,1,0:T(8,128)(2,1)} %get-tuple-element.43), channel_id=1, source_target_pairs={{0,3},{1,0},{2,1},{3,2},{4,7},{5,4},{6,5},{7,6},{8,11},{9,8},{10,9... | collective-permute-start | bytes 589832 | tf_op jit(solution)/shard_map/ppermute | solution.py:66
  82.4 9.1 %collective-permute-start.17 = (bf16[6,64,256]{2,1,0:T(8,128)(2,1)}, bf16[6,64,256]{2,1,0:T(8,128)(2,1)S(1)}, u32[]{:S(2)}, u32[]{:S(2)}) collective-permute-start(bf16[6,64,256]{2,1,0:T(8,128)(2,1)} %get-tuple-element.44), channel_id=1, source_target_pairs={{0,2},{1,3},{2,0},{3,1},{4,6},{5,7},{6,4},{7,5},{8,10},{9,11},{10,... | collective-permute-start | bytes 589832 | tf_op jit(solution)/shard_map/ppermute | solution.py:66
  85.4 6.7 %collective-permute-start.19 = (bf16[3,64,256]{2,1,0:T(8,128)(2,1)S(1)}, bf16[3,64,256]{2,1,0:T(8,128)(2,1)S(1)}, u32[]{:S(2)}, u32[]{:S(2)}) collective-permute-start(bf16[3,64,256]{2,1,0:T(8,128)(2,1)S(1)} %get-tuple-element.46), channel_id=1, source_target_pairs={{0,1},{1,2},{2,3},{3,0},{4,5},{5,6},{6,7},{7,4},{8,9},{9,10},{10,1... | collective-permute-start | bytes 294920 | tf_op jit(solution)/shard_map/ppermute | solution.py:66
  87.7 5.3 %collective-permute-start.20 = (bf16[3,64,256]{2,1,0:T(8,128)(2,1)S(1)}, bf16[3,64,256]{2,1,0:T(8,128)(2,1)S(1)}, u32[]{:S(2)}, u32[]{:S(2)}) collective-permute-start(bf16[3,64,256]{2,1,0:T(8,128)(2,1)S(1)} %get-tuple-element.47), channel_id=1, source_target_pairs={{0,3},{1,0},{2,1},{3,2},{4,7},{5,4},{6,5},{7,6},{8,11},{9,8},{10,9... | collective-permute-start | bytes 294920 | tf_op jit(solution)/shard_map/ppermute | solution.py:66
  88.9 6.1 %collective-permute-start.21 = (bf16[3,64,256]{2,1,0:T(8,128)(2,1)S(1)}, bf16[3,64,256]{2,1,0:T(8,128)(2,1)S(1)}, u32[]{:S(2)}, u32[]{:S(2)}) collective-permute-start(bf16[3,64,256]{2,1,0:T(8,128)(2,1)S(1)} %get-tuple-element.48), channel_id=1, source_target_pairs={{0,2},{1,3},{2,0},{3,1},{4,6},{5,7},{6,4},{7,5},{8,10},{9,11},{10,... | collective-permute-start | bytes 294920 | tf_op jit(solution)/shard_map/ppermute | solution.py:66
  117.0 96.8 %all-to-all-start.1 = ((bf16[32,256,256]{2,1,0:T(8,128)(2,1)}), bf16[32,256,256]{2,1,0:T(8,128)(2,1)}, u32[]{:S(2)}, u32[]{:S(2)}) async-start(bf16[32,256,256]{2,1,0:T(8,128)(2,1)} %device_tiles.1), calls=%async_computation.1 | async-start | bytes 8388608 | tf_op jit(solution)/shard_map/all_to_all | solution.py:271
  220.4 2.9 %collective-permute-start.22 = (bf16[8,256,256]{2,1,0:T(8,128)(2,1)}, bf16[8,256,256]{2,1,0:T(8,128)(2,1)S(1)}, u32[]{:S(2)}, u32[]{:S(2)}) collective-permute-start(bf16[8,256,256]{2,1,0:T(8,128)(2,1)} %get-tuple-element.51), channel_id=1, source_target_pairs={{0,32},{32,0},{64,96},{96,64},{128,160},{160,128},{192,224},{224,1... | collective-permute-start | bytes 3145736 | tf_op jit(solution)/shard_map/ppermute | solution.py:245
  224.8 10.8 %collective-permute-start.23 = (bf16[2,256,256]{2,1,0:T(8,128)(2,1)S(1)}, bf16[2,256,256]{2,1,0:T(8,128)(2,1)S(1)}, u32[]{:S(2)}, u32[]{:S(2)}) collective-permute-start(bf16[2,256,256]{2,1,0:T(8,128)(2,1)S(1)} %get-tuple-element.55), channel_id=1, source_target_pairs={{0,128},{32,160},{64,192},{96,224},{128,0},{160,32},{192,64},{224,... | collective-permute-start | bytes 786440 | tf_op jit(solution)/shard_map/ppermute | solution.py:253
  228.0 12.7 %collective-permute-start.25 = (bf16[2,256,256]{2,1,0:T(8,128)(2,1)S(1)}, bf16[2,256,256]{2,1,0:T(8,128)(2,1)S(1)}, u32[]{:S(2)}, u32[]{:S(2)}) collective-permute-start(bf16[2,256,256]{2,1,0:T(8,128)(2,1)S(1)} %get-tuple-element.56), channel_id=1, source_target_pairs={{0,192},{32,224},{64,0},{96,32},{128,64},{160,96},{192,128},{224,1... | collective-permute-start | bytes 786440 | tf_op jit(solution)/shard_map/ppermute | solution.py:253
  229.1 11.6 %collective-permute-start.24 = (bf16[2,256,256]{2,1,0:T(8,128)(2,1)S(1)}, bf16[2,256,256]{2,1,0:T(8,128)(2,1)S(1)}, u32[]{:S(2)}, u32[]{:S(2)}) collective-permute-start(bf16[2,256,256]{2,1,0:T(8,128)(2,1)S(1)} %get-tuple-element.57), channel_id=1, source_target_pairs={{0,64},{32,96},{64,128},{96,160},{128,192},{160,224},{192,0},{224,... | collective-permute-start | bytes 786440 | tf_op jit(solution)/shard_map/ppermute | solution.py:253
  (6 other events, 5.0 us)

commit v6 on v4

--- a/solution.py
+++ b/solution.py
@@ -59,7 +59,7 @@
 
     pieces, spots = [], []
 
-    def forward(ups, blocks):
+    def forward(asks, ups, blocks):
         picked = pick(asks, n_x, ups, blocks)
         for step, block in zip(STEPS, picked):
             if step:
@@ -75,6 +75,7 @@
     up = lax.ppermute(panels, "dev", along_z(1))
     down = lax.ppermute(panels, "dev", along_z(-1))
     asks = lax.all_to_all(asked, "dev", split_axis=0, concat_axis=0, tiled=True)
+    forward(asked, (0,), (panels,))
     for k in range(1, half):
         if k + 1 < half:
             new_up = lax.ppermute(up, "dev", along_z(1))
@@ -88,12 +89,9 @@
                 for s, t in along_z(-1 if g % 2 else 1)
             ]
             far = lax.ppermute(jnp.where(odd, down, up), ("grp", "dev"), pairs)
-        if k == 1:
-            forward((0, k, -k), (panels, up, down))
-        else:
-            forward((k, -k), (up, down))
+        forward(asks, (k, -k), (up, down))
         up, down = new_up, new_down
-    forward((half,), (far,))
+    forward(asks, (half,), (far,))
 
     entry = jnp.arange(n_z * n_x * NCAP, dtype=jnp.int32)
     s, c = entry // NCAP, entry % NCAP
@@ -173,7 +171,7 @@
             pltpu.VMEM((LT + 1, R * BLOCK, W), jnp.float32),
             pltpu.SemaphoreType.DMA((R,)),
         ],
-        compiler_params=pltpu.CompilerParams(vmem_limit_bytes=50 << 20),
+        compiler_params=pltpu.CompilerParams(vmem_limit_bytes=51 << 20),
         cost_estimate=pl.CostEstimate(
             flops=8_000_000_000, bytes_accessed=12_000_000, transcendentals=0
         ),
@@ -181,46 +179,41 @@
     )(cols, slots, places, where, blocks, pt, *pieces)
 
 
-def table_kernel(labels_ref, got_ref, here_ref, there_ref, sum_ref):
-    n_here, n_there = here_ref.shape[0], there_ref.shape[0]
-
-    @pl.loop(0, n_here + n_there)
+def table_kernel(first, labels_ref, got_ref, out_ref, sum_ref):
+    n = sum_ref.shape[0]
+
+    @pl.loop(0, n)
     def _(t):
         sum_ref[t] = jnp.zeros(sum_ref.shape[1:], jnp.float32)
 
     @pl.loop(0, got_ref.shape[0])
     def _(s):
-        label = labels_ref[s]
-        at = jnp.where(label < 0, n_here + n_there, label)
-        sum_ref[at] += got_ref[s].astype(jnp.float32)
-
-    @pl.loop(0, n_here)
-    def _(t):
-        here_ref[t] = sum_ref[t]
-
-    @pl.loop(0, n_there)
-    def _(t):
-        there_ref[t] = sum_ref[n_here + t].astype(there_ref.dtype)
-
-
-def table_of(labels, got, n_here, n_there):
+        at = labels_ref[s] - first
+
+        @pl.when((at >= 0) & (at < n))
+        def _():
+            sum_ref[at] += got_ref[s].astype(jnp.float32)
+
+    @pl.loop(0, n)
+    def _(t):
+        out_ref[t] = sum_ref[t].astype(out_ref.dtype)
+
+
+def table_of(labels, got, first, n, dtype):
     rows = 64
     block = lambda n: pl.BlockSpec((n, rows, W), lambda i, *_: (0, i, 0))
     return pl.pallas_call(
-        table_kernel,
-        out_shape=[
-            jax.ShapeDtypeStruct((n_here, W, W), jnp.float32),
-            jax.ShapeDtypeStruct((n_there, W, W), jnp.bfloat16),
-        ],
+        functools.partial(table_kernel, first),
+        out_shape=jax.ShapeDtypeStruct((n, W, W), dtype),
         grid_spec=pltpu.PrefetchScalarGridSpec(
             num_scalar_prefetch=1,
             grid=(W // rows,),
             in_specs=[block(got.shape[0])],
-            out_specs=[block(n_here), block(n_there)],
-            scratch_shapes=[pltpu.VMEM((n_here + n_there + 1, rows, W), jnp.float32)],
+            out_specs=block(n),
+            scratch_shapes=[pltpu.VMEM((n, rows, W), jnp.float32)],
         ),
         compiler_params=pltpu.CompilerParams(dimension_semantics=("arbitrary",)),
-        cost_estimate=pl.CostEstimate(flops=2_000_000, bytes_accessed=7_000_000, transcendentals=0),
+        cost_estimate=pl.CostEstimate(flops=1_000_000, bytes_accessed=6_000_000, transcendentals=0),
         name="table_of",
     )(labels, got)
 
@@ -233,9 +226,12 @@
     dy = (to // cores - y) % n_y
     other = (to % cores - core) % cores
     at = jnp.where(labels < 0, -1, (other * n_y + dy) * CT + place)
-    here, there = table_of(at, got, n_y * CT, n_y * CT)
+    n = n_y * CT
+    there = table_of(at, got, n, n, jnp.bfloat16)
     swap = [(g, g // cores * cores + (g + 1) % cores) for g in range(groups)]
-    here += lax.ppermute(there, "grp", swap).astype(jnp.float32)
+    there = lax.ppermute(there, "grp", swap)
+    here = table_of(at, got, 0, n, jnp.float32)
+    here += there.astype(jnp.float32)
     total = here[:CT]
     for step in (2, 1, 3):
         pairs = [(g, (g + step * cores) % groups) for g in range(groups)]

time: 232 us -> 241 us (1.039)
  Pallas kernels: 26.6 us -> 33.3 us
  local copies, waits for them, and re-layouts: 3.95 us -> 7 us
  waiting for transfers between devices: 132 us -> 129 us
  starting transfers between devices: 48.2 us -> 50.8 us
    pallas_call x1 -> x2, Pallas kernels: 6.27 us -> 12 us  [table_of(): pl.pallas_call(functools.partial(table_kernel, first), out_shape=jax.Shap...]
    ppermute x1, waiting for transfers between devices: 2.87 us -> 0.01 us  [sum_over_groups(): there = lax.ppermute(there, 'grp', swap)]
    ppermute x12 -> x15, waiting for transfers between devices: 7.05 us -> 4.67 us  [forward(): block = lax.ppermute(block, 'dev', along_x(step))]
    unnamed x14 -> x24, local copies, waits for them, and re-layouts: 3.45 us -> 5.75 us
    ppermute x12 -> x15, starting transfers between devices: 23.2 us -> 25.4 us  [forward(): block = lax.ppermute(block, 'dev', along_x(step))]
    pallas_call x4 -> x5, Pallas kernels: 5.16 us -> 6.01 us  [pick(): pl.pallas_call(functools.partial(pick_kernel, n_x, ups), out_shape=[jax.S...]
  transfers between devices with their start and end apart: 24 -> 27, of which waited for: 13 -> 10; matrix products, arithmetic and copies ran while one was open for 1% -> 1% of each run, Pallas kernels for 2% -> 5%
where the time goes in v6:
time: 241 us; the launch traced here: 240 us
  waiting for transfers between devices  129 us (54%)
  starting transfers between devices  50.8 us (21%)
  Pallas kernels  33.3 us (14%)
  blocking collectives  15.1 us (6%)
  local copies, waits for them, and re-layouts  7 us (3%)
  other arithmetic  4.52 us (2%)
    all_to_all x1, waiting for transfers between devices, layer(): lax.all_to_all(sending, 'dev', split_axis=0, concat_axis=0, tiled=True)  88.3 us
    ppermute x15, starting transfers between devices, forward(): block = lax.ppermute(block, 'dev', along_x(step))  25.4 us
    pallas_call x1, Pallas kernels, device_tiles(): pl.pallas_call(functools.partial(tiles_kernel, spots), out_shape=jax.Shap...  15.3 us
    all_to_all x1, blocking collectives, fetch(): asks = lax.all_to_all(asked, 'dev', split_axis=0, concat_axis=0, tiled=True)  15.1 us
    ppermute x2, waiting for transfers between devices, fetch(): new_down = lax.ppermute(down, 'dev', along_z(-1))  12.4 us
    pallas_call x2, Pallas kernels, table_of(): pl.pallas_call(functools.partial(table_kernel, first), out_shape=jax.Shap...  12 us
    ppermute x3, waiting for transfers between devices, sum_over_groups(): total += lax.ppermute(part, 'grp', pairs).astype(jnp.float32)  11.1 us
    ppermute x1, waiting for transfers between devices, fetch(): down = lax.ppermute(panels, 'dev', along_z(-1))  8.69 us
  transfers between devices with their start and end apart: 27, of which 10 were waited for; matrix products, arithmetic and copies ran while one was open for 1% of the time, Pallas kernels for 5%

profile of v6, /device:TPU:4, one launch (start us, length us, event | category | flops | bytes accessed | tf_op | source)
XLA Modules:
  0.0 239.5 jit_solution(12983687845684311020)
XLA Ops:
  0.0 5.9 %collective-permute-start.4 = (bf16[12,64,256]{2,1,0:T(8,128)(2,1)}, bf16[12,64,256]{2,1,0:T(8,128)(2,1)S(1)}, u32[]{:S(2)}, u32[]{:S(2)}) collective-permute-start(bf16[12,64,256]{2,1,0:T(8,128)(2,1)} %bitcast.37), channel_id=1, source_target_pairs={{0,28},{1,29},{2,30},{3,31},{4,0},{5,1},{6,2},{7,3},{8,4},{9,5},{1... | collective-permute-start | bytes 1179656 | tf_op jit(solution)/shard_map/ppermute | solution.py:76
  5.9 8.7 %collective-permute-done.4.refs_1_ = bf16[12,64,256]{2,1,0:T(8,128)(2,1)S(1)} collective-permute-done((bf16[12,64,256]{2,1,0:T(8,128)(2,1)}, bf16[12,64,256]{2,1,0:T(8,128)(2,1)S(1)}, u32[]{:S(2)}, u32[]{:S(2)}) %collective-permute-start.4) | collective-permute-done | bytes 393248 | tf_op jit(solution)/shard_map/ppermute | solution.py:76
  14.5 3.6 %collective-permute-start.9 = (bf16[12,64,256]{2,1,0:T(8,128)(2,1)S(1)}, bf16[12,64,256]{2,1,0:T(8,128)(2,1)S(1)}, u32[]{:S(2)}, u32[]{:S(2)}) collective-permute-start(bf16[12,64,256]{2,1,0:T(8,128)(2,1)S(1)} %collective-permute-done.4.refs_1_), channel_id=1, source_target_pairs={{0,28},{1,29},{2,30},{3,31},{4,0},{5,1},{6,2},{7,3},{8,4},{9,5},{1... | collective-permute-start | bytes 1179656 | tf_op jit(solution)/shard_map/ppermute | solution.py:82
  18.1 7.5 %collective-permute-done.9.refs_1_ = bf16[12,64,256]{2,1,0:T(8,128)(2,1)S(1)} collective-permute-done((bf16[12,64,256]{2,1,0:T(8,128)(2,1)S(1)}, bf16[12,64,256]{2,1,0:T(8,128)(2,1)S(1)}, u32[]{:S(2)}, u32[]{:S(2)}) %collective-permute-start.9) | collective-permute-done | bytes 393248 | tf_op jit(solution)/shard_map/ppermute | solution.py:82
  25.7 3.7 %collective-permute-start.14 = (bf16[12,64,256]{2,1,0:T(8,128)(2,1)S(1)}, bf16[12,64,256]{2,1,0:T(8,128)(2,1)S(1)}, u32[]{:S(2)}, u32[]{:S(2)}) collective-permute-start(bf16[12,64,256]{2,1,0:T(8,128)(2,1)S(1)} %collective-permute-done.9.refs_1_), channel_id=1, source_target_pairs={{0,28},{1,29},{2,30},{3,31},{4,0},{5,1},{6,2},{7,3},{8,4},{9,5},{1... | collective-permute-start | bytes 1179656 | tf_op jit(solution)/shard_map/ppermute | solution.py:82
  31.1 4.9 %collective-permute-done.14.refs_1_ = bf16[12,64,256]{2,1,0:T(8,128)(2,1)S(1)} collective-permute-done((bf16[12,64,256]{2,1,0:T(8,128)(2,1)S(1)}, bf16[12,64,256]{2,1,0:T(8,128)(2,1)S(1)}, u32[]{:S(2)}, u32[]{:S(2)}) %collective-permute-start.14) | collective-permute-done | bytes 393248 | tf_op jit(solution)/shard_map/ppermute | solution.py:82
  36.0 3.4 %collective-permute-done.13.refs_0_ = bf16[12,64,256]{2,1,0:T(8,128)(2,1)S(1)} collective-permute-done((bf16[12,64,256]{2,1,0:T(8,128)(2,1)S(1)}, bf16[12,64,256]{2,1,0:T(8,128)(2,1)S(1)}, u32[]{:S(2)}, u32[]{:S(2)}) %collective-permute-start.13) | collective-permute-done | bytes 393248 | tf_op jit(solution)/shard_map/ppermute | solution.py:81
  41.5 1.3 collective-permute-start
  43.6 1.7 collective-permute-start.2
  45.3 15.1 %all_to_all.16 = s32[32,1,13]{2,1,0:T(1,128)S(1)} all-to-all(s32[32,1,13]{2,1,0:T(1,128)S(1)} %bitcast.46), channel_id=1, replica_groups=mesh['grp'=8,'dev'=32] {'dev'}, dimensions={0} | all-to-all | bytes 3328 | tf_op jit(solution)/shard_map/all_to_all | solution.py:77
  61.3 1.5 collective-permute-start.5
  62.9 1.7 pick.7
  66.4 3.5 %collective-permute-start.7 = (bf16[6,64,256]{2,1,0:T(8,128)(2,1)S(1)}, bf16[6,64,256]{2,1,0:T(8,128)(2,1)S(1)}, u32[]{:S(2)}, u32[]{:S(2)}) collective-permute-start(bf16[6,64,256]{2,1,0:T(8,128)(2,1)S(1)} %get-tuple-element.31), channel_id=1, source_target_pairs={{0,2},{1,3},{2,0},{3,1},{4,6},{5,7},{6,4},{7,5},{8,10},{9,11},{10,... | collective-permute-start | bytes 589832 | tf_op jit(solution)/shard_map/ppermute | solution.py:66
  69.9 1.7 pick.8
  71.7 2.0 collective-permute-start.11
  73.7 2.7 %collective-permute-start.12 = (bf16[6,64,256]{2,1,0:T(8,128)(2,1)}, bf16[6,64,256]{2,1,0:T(8,128)(2,1)S(1)}, u32[]{:S(2)}, u32[]{:S(2)}) collective-permute-start(bf16[6,64,256]{2,1,0:T(8,128)(2,1)} %get-tuple-element.35), channel_id=1, source_target_pairs={{0,2},{1,3},{2,0},{3,1},{4,6},{5,7},{6,4},{7,5},{8,10},{9,11},{10,... | collective-permute-start | bytes 589832 | tf_op jit(solution)/shard_map/ppermute | solution.py:66
  76.4 2.5 %collective-permute-start.15 = (bf16[6,64,256]{2,1,0:T(8,128)(2,1)}, bf16[6,64,256]{2,1,0:T(8,128)(2,1)S(1)}, u32[]{:S(2)}, u32[]{:S(2)}) collective-permute-start(bf16[6,64,256]{2,1,0:T(8,128)(2,1)} %get-tuple-element.37), channel_id=1, source_target_pairs={{0,1},{1,2},{2,3},{3,0},{4,5},{5,6},{6,7},{7,4},{8,9},{9,10},{10,1... | collective-permute-start | bytes 589832 | tf_op jit(solution)/shard_map/ppermute | solution.py:66
  80.5 3.5 %collective-permute-start.17 = (bf16[6,64,256]{2,1,0:T(8,128)(2,1)}, bf16[6,64,256]{2,1,0:T(8,128)(2,1)S(1)}, u32[]{:S(2)}, u32[]{:S(2)}) collective-permute-start(bf16[6,64,256]{2,1,0:T(8,128)(2,1)} %get-tuple-element.39), channel_id=1, source_target_pairs={{0,2},{1,3},{2,0},{3,1},{4,6},{5,7},{6,4},{7,5},{8,10},{9,11},{10,... | collective-permute-start | bytes 589832 | tf_op jit(solution)/shard_map/ppermute | solution.py:66
  85.8 2.1 collective-permute-start.19
  87.9 2.6 %collective-permute-start.21 = (bf16[3,64,256]{2,1,0:T(8,128)(2,1)S(1)}, bf16[3,64,256]{2,1,0:T(8,128)(2,1)S(1)}, u32[]{:S(2)}, u32[]{:S(2)}) collective-permute-start(bf16[3,64,256]{2,1,0:T(8,128)(2,1)S(1)} %get-tuple-element.43), channel_id=1, source_target_pairs={{0,2},{1,3},{2,0},{3,1},{4,6},{5,7},{6,4},{7,5},{8,10},{9,11},{10,... | collective-permute-start | bytes 294920 | tf_op jit(solution)/shard_map/ppermute | solution.py:66
  90.6 1.9 collective-permute-done.20.refs_17_
  92.5 1.6 collective-permute-done.21.refs_18_
  96.8 15.3 %device_tiles.1 = bf16[32,256,256]{2,1,0:T(8,128)(2,1)} custom-call(s32[12,27]{1,0:T(8,128)S(1)} %get-tuple-element.53.cols_ref, s32[12,27]{1,0:T(8,128)S(1)} %get-tuple-element.52.slots_ref, s32[16]{0:T(128)S(1)} %get-tuple-element.50.places_ref, s32[96]{0:T(128)S(1)} %fusion.3.where_ref, bf16[12,64,1728]{2,1,0:T(8,128)(2,1)} %bitcast.50, ...), custom_call_target="tpu_custom_call" | custom-call | flops 8000000000 | bytes 12000000 | tf_op jit(solution)/shard_map/device_tiles/pallas_call | solution.py:163
  112.1 7.0 %all-to-all-start.1 = ((bf16[32,256,256]{2,1,0:T(8,128)(2,1)}), bf16[32,256,256]{2,1,0:T(8,128)(2,1)}, u32[]{:S(2)}, u32[]{:S(2)}) async-start(bf16[32,256,256]{2,1,0:T(8,128)(2,1)} %device_tiles.1), calls=%async_computation.1 | async-start | bytes 8388608 | tf_op jit(solution)/shard_map/all_to_all | solution.py:257
  119.8 88.3 %all-to-all-done.1.got_ref = bf16[32,256,256]{2,1,0:T(8,128)(2,1)} async-done(((bf16[32,256,256]{2,1,0:T(8,128)(2,1)}), bf16[32,256,256]{2,1,0:T(8,128)(2,1)}, u32[]{:S(2)}, u32[]{:S(2)}) %all-to-all-start.1) | async-done | bytes 4194336 | tf_op jit(solution)/shard_map/all_to_all | solution.py:257
  208.1 5.9 %table_of.3 = bf16[8,256,256]{2,1,0:T(8,128)(2,1)} custom-call(s32[32]{0:T(128)} %fusion.7.labels_ref, bf16[32,256,256]{2,1,0:T(8,128)(2,1)} %all-to-all-done.1.got_ref), custom_call_target="tpu_custom_call" | custom-call | flops 1000000 | bytes 6000000 | tf_op jit(solution)/shard_map/table_of/pallas_call | solution.py:205
  214.0 6.1 %table_of.2 = f32[8,256,256]{2,1,0:T(8,128)} custom-call(s32[32]{0:T(128)} %fusion.7.labels_ref, bf16[32,256,256]{2,1,0:T(8,128)(2,1)} %all-to-all-done.1.got_ref), custom_call_target="tpu_custom_call" | custom-call | flops 1000000 | bytes 6000000 | tf_op jit(solution)/shard_map/table_of/pallas_call | solution.py:205
  220.1 2.1 fusion.16
  222.3 3.2 %collective-permute-start.23 = (bf16[2,256,256]{2,1,0:T(8,128)(2,1)S(1)}, bf16[2,256,256]{2,1,0:T(8,128)(2,1)S(1)}, u32[]{:S(2)}, u32[]{:S(2)}) collective-permute-start(bf16[2,256,256]{2,1,0:T(8,128)(2,1)S(1)} %get-tuple-element.47), channel_id=1, source_target_pairs={{0,128},{32,160},{64,192},{96,224},{128,0},{160,32},{192,64},{224,... | collective-permute-start | bytes 786440 | tf_op jit(solution)/shard_map/ppermute | solution.py:239
  225.5 1.1 collective-permute-start.25
  227.6 5.5 %collective-permute-done.23 = bf16[2,256,256]{2,1,0:T(8,128)(2,1)S(1)} collective-permute-done((bf16[2,256,256]{2,1,0:T(8,128)(2,1)S(1)}, bf16[2,256,256]{2,1,0:T(8,128)(2,1)S(1)}, u32[]{:S(2)}, u32[]{:S(2)}) %collective-permute-start.23) | collective-permute-done | bytes 262176 | tf_op jit(solution)/shard_map/ppermute | solution.py:239
  233.1 5.5 %collective-permute-done.25 = bf16[2,256,256]{2,1,0:T(8,128)(2,1)S(1)} collective-permute-done((bf16[2,256,256]{2,1,0:T(8,128)(2,1)S(1)}, bf16[2,256,256]{2,1,0:T(8,128)(2,1)S(1)}, u32[]{:S(2)}, u32[]{:S(2)}) %collective-permute-start.25) | collective-permute-done | bytes 262176 | tf_op jit(solution)/shard_map/ppermute | solution.py:239
  (69 shorter events, 16.1 us)
Async XLA Ops:
  0.0 14.5 %collective-permute-start.4 = (bf16[12,64,256]{2,1,0:T(8,128)(2,1)}, bf16[12,64,256]{2,1,0:T(8,128)(2,1)S(1)}, u32[]{:S(2)}, u32[]{:S(2)}) collective-permute-start(bf16[12,64,256]{2,1,0:T(8,128)(2,1)} %bitcast.37), channel_id=1, source_target_pairs={{0,28},{1,29},{2,30},{3,31},{4,0},{5,1},{6,2},{7,3},{8,4},{9,5},{1... | collective-permute-start | bytes 1179656 | tf_op jit(solution)/shard_map/ppermute | solution.py:76
  5.9 12.3 %collective-permute-start.3 = (bf16[12,64,256]{2,1,0:T(8,128)(2,1)}, bf16[12,64,256]{2,1,0:T(8,128)(2,1)S(1)}, u32[]{:S(2)}, u32[]{:S(2)}) collective-permute-start(bf16[12,64,256]{2,1,0:T(8,128)(2,1)} %bitcast.38), channel_id=1, source_target_pairs={{0,4},{1,5},{2,6},{3,7},{4,8},{5,9},{6,10},{7,11},{8,12},{9,13},{1... | collective-permute-start | bytes 1179656 | tf_op jit(solution)/shard_map/ppermute | solution.py:75
  14.5 11.1 %collective-permute-start.9 = (bf16[12,64,256]{2,1,0:T(8,128)(2,1)S(1)}, bf16[12,64,256]{2,1,0:T(8,128)(2,1)S(1)}, u32[]{:S(2)}, u32[]{:S(2)}) collective-permute-start(bf16[12,64,256]{2,1,0:T(8,128)(2,1)S(1)} %collective-permute-done.4.refs_1_), channel_id=1, source_target_pairs={{0,28},{1,29},{2,30},{3,31},{4,0},{5,1},{6,2},{7,3},{8,4},{9,5},{1... | collective-permute-start | bytes 1179656 | tf_op jit(solution)/shard_map/ppermute | solution.py:82
  18.1 11.2 %collective-permute-start.8 = (bf16[12,64,256]{2,1,0:T(8,128)(2,1)S(1)}, bf16[12,64,256]{2,1,0:T(8,128)(2,1)S(1)}, u32[]{:S(2)}, u32[]{:S(2)}) collective-permute-start(bf16[12,64,256]{2,1,0:T(8,128)(2,1)S(1)} %collective-permute-done.3.refs_0_), channel_id=1, source_target_pairs={{0,4},{1,5},{2,6},{3,7},{4,8},{5,9},{6,10},{7,11},{8,12},{9,13},{1... | collective-permute-start | bytes 1179656 | tf_op jit(solution)/shard_map/ppermute | solution.py:81
  25.7 10.4 %collective-permute-start.14 = (bf16[12,64,256]{2,1,0:T(8,128)(2,1)S(1)}, bf16[12,64,256]{2,1,0:T(8,128)(2,1)S(1)}, u32[]{:S(2)}, u32[]{:S(2)}) collective-permute-start(bf16[12,64,256]{2,1,0:T(8,128)(2,1)S(1)} %collective-permute-done.9.refs_1_), channel_id=1, source_target_pairs={{0,28},{1,29},{2,30},{3,31},{4,0},{5,1},{6,2},{7,3},{8,4},{9,5},{1... | collective-permute-start | bytes 1179656 | tf_op jit(solution)/shard_map/ppermute | solution.py:82
  29.3 10.1 %collective-permute-start.13 = (bf16[12,64,256]{2,1,0:T(8,128)(2,1)S(1)}, bf16[12,64,256]{2,1,0:T(8,128)(2,1)S(1)}, u32[]{:S(2)}, u32[]{:S(2)}) collective-permute-start(bf16[12,64,256]{2,1,0:T(8,128)(2,1)S(1)} %collective-permute-done.8.refs_0_), channel_id=1, source_target_pairs={{0,4},{1,5},{2,6},{3,7},{4,8},{5,9},{6,10},{7,11},{8,12},{9,13},{1... | collective-permute-start | bytes 1179656 | tf_op jit(solution)/shard_map/ppermute | solution.py:81
  29.4 54.7 %copy-start.9 = (s32[1,1,12,27]{3,1,2,0:T(1,128)S(1)}, s32[1,1,12,27]{3,1,2,0:T(1,128)}, u32[]{:S(2)}) copy-start(s32[1,1,12,27]{3,1,2,0:T(1,128)} %param.11) | copy-start | bytes 3892
  29.4 54.7 %copy-start.10 = (s32[1,1,12,27]{3,1,2,0:T(1,128)S(1)}, s32[1,1,12,27]{3,1,2,0:T(1,128)}, u32[]{:S(2)}) copy-start(s32[1,1,12,27]{3,1,2,0:T(1,128)} %param.9) | copy-start | bytes 3892
  31.1 52.9 %copy-start.1 = (bf16[1,1,12,64,256]{4,3,2,1,0:T(8,128)(2,1)S(1)}, bf16[1,1,12,64,256]{4,3,2,1,0:T(8,128)(2,1)}, u32[]{:S(2)}) copy-start(bf16[1,1,12,64,256]{4,3,2,1,0:T(8,128)(2,1)} %param.8) | copy-start | bytes 1179652
  39.5 41.0 %collective-permute-start.18 = (bf16[12,64,256]{2,1,0:T(8,128)(2,1)S(1)}, bf16[12,64,256]{2,1,0:T(8,128)(2,1)S(1)}, u32[]{:S(2)}, u32[]{:S(2)}) collective-permute-start(bf16[12,64,256]{2,1,0:T(8,128)(2,1)S(1)} %broadcast_select_fusion), channel_id=1, source_target_pairs={{0,4},{1,5},{2,6},{3,7},{4,8},{5,9},{6,10},{7,11},{8,12},{9,13},{1... | collective-permute-start | bytes 1179656 | tf_op jit(solution)/shard_map/ppermute | solution.py:91
  41.5 23.0 %collective-permute-start = (bf16[3,64,256]{2,1,0:T(8,128)(2,1)S(1)}, bf16[3,64,256]{2,1,0:T(8,128)(2,1)S(1)}, u32[]{:S(2)}, u32[]{:S(2)}) collective-permute-start(bf16[3,64,256]{2,1,0:T(8,128)(2,1)S(1)} %get-tuple-element.25), channel_id=1, source_target_pairs={{0,1},{1,2},{2,3},{3,0},{4,5},{5,6},{6,7},{7,4},{8,9},{9,10},{10,1... | collective-permute-start | bytes 294920 | tf_op jit(solution)/shard_map/ppermute | solution.py:66
  42.8 22.9 %collective-permute-start.1 = (bf16[3,64,256]{2,1,0:T(8,128)(2,1)S(1)}, bf16[3,64,256]{2,1,0:T(8,128)(2,1)S(1)}, u32[]{:S(2)}, u32[]{:S(2)}) collective-permute-start(bf16[3,64,256]{2,1,0:T(8,128)(2,1)S(1)} %get-tuple-element.26), channel_id=1, source_target_pairs={{0,3},{1,0},{2,1},{3,2},{4,7},{5,4},{6,5},{7,6},{8,11},{9,8},{10,9... | collective-permute-start | bytes 294920 | tf_op jit(solution)/shard_map/ppermute | solution.py:66
  43.6 26.3 %collective-permute-start.2 = (bf16[3,64,256]{2,1,0:T(8,128)(2,1)S(1)}, bf16[3,64,256]{2,1,0:T(8,128)(2,1)S(1)}, u32[]{:S(2)}, u32[]{:S(2)}) collective-permute-start(bf16[3,64,256]{2,1,0:T(8,128)(2,1)S(1)} %get-tuple-element.27), channel_id=1, source_target_pairs={{0,2},{1,3},{2,0},{3,1},{4,6},{5,7},{6,4},{7,5},{8,10},{9,11},{10,... | collective-permute-start | bytes 294920 | tf_op jit(solution)/shard_map/ppermute | solution.py:66
  61.3 10.3 %collective-permute-start.5 = (bf16[6,64,256]{2,1,0:T(8,128)(2,1)S(1)}, bf16[6,64,256]{2,1,0:T(8,128)(2,1)S(1)}, u32[]{:S(2)}, u32[]{:S(2)}) collective-permute-start(bf16[6,64,256]{2,1,0:T(8,128)(2,1)S(1)} %get-tuple-element.29), channel_id=1, source_target_pairs={{0,1},{1,2},{2,3},{3,0},{4,5},{5,6},{6,7},{7,4},{8,9},{9,10},{10,1... | collective-permute-start | bytes 589832 | tf_op jit(solution)/shard_map/ppermute | solution.py:66
  65.2 8.5 %collective-permute-start.6 = (bf16[6,64,256]{2,1,0:T(8,128)(2,1)S(1)}, bf16[6,64,256]{2,1,0:T(8,128)(2,1)S(1)}, u32[]{:S(2)}, u32[]{:S(2)}) collective-permute-start(bf16[6,64,256]{2,1,0:T(8,128)(2,1)S(1)} %get-tuple-element.30), channel_id=1, source_target_pairs={{0,3},{1,0},{2,1},{3,2},{4,7},{5,4},{6,5},{7,6},{8,11},{9,8},{10,9... | collective-permute-start | bytes 589832 | tf_op jit(solution)/shard_map/ppermute | solution.py:66
  66.4 10.0 %collective-permute-start.7 = (bf16[6,64,256]{2,1,0:T(8,128)(2,1)S(1)}, bf16[6,64,256]{2,1,0:T(8,128)(2,1)S(1)}, u32[]{:S(2)}, u32[]{:S(2)}) collective-permute-start(bf16[6,64,256]{2,1,0:T(8,128)(2,1)S(1)} %get-tuple-element.31), channel_id=1, source_target_pairs={{0,2},{1,3},{2,0},{3,1},{4,6},{5,7},{6,4},{7,5},{8,10},{9,11},{10,... | collective-permute-start | bytes 589832 | tf_op jit(solution)/shard_map/ppermute | solution.py:66
  69.9 10.6 %copy-start.7 = (bf16[3,64,256]{2,1,0:T(8,128)(2,1)}, bf16[3,64,256]{2,1,0:T(8,128)(2,1)S(1)}, u32[]{:S(2)}) copy-start(bf16[3,64,256]{2,1,0:T(8,128)(2,1)S(1)} %collective-permute-done.2.refs_2_) | copy-start | bytes 294916
  69.9 10.1 %collective-permute-start.10 = (bf16[6,64,256]{2,1,0:T(8,128)(2,1)S(1)}, bf16[6,64,256]{2,1,0:T(8,128)(2,1)S(1)}, u32[]{:S(2)}, u32[]{:S(2)}) collective-permute-start(bf16[6,64,256]{2,1,0:T(8,128)(2,1)S(1)} %get-tuple-element.33), channel_id=1, source_target_pairs={{0,1},{1,2},{2,3},{3,0},{4,5},{5,6},{6,7},{7,4},{8,9},{9,10},{10,1... | collective-permute-start | bytes 589832 | tf_op jit(solution)/shard_map/ppermute | solution.py:66
  71.7 22.5 %copy-start.2 = (bf16[6,64,256]{2,1,0:T(8,128)(2,1)}, bf16[6,64,256]{2,1,0:T(8,128)(2,1)S(1)}, u32[]{:S(2)}) copy-start(bf16[6,64,256]{2,1,0:T(8,128)(2,1)S(1)} %get-tuple-element.40.refs_15_) | copy-start | bytes 589828
  71.7 14.1 %collective-permute-start.11 = (bf16[6,64,256]{2,1,0:T(8,128)(2,1)}, bf16[6,64,256]{2,1,0:T(8,128)(2,1)S(1)}, u32[]{:S(2)}, u32[]{:S(2)}) collective-permute-start(bf16[6,64,256]{2,1,0:T(8,128)(2,1)} %get-tuple-element.34), channel_id=1, source_target_pairs={{0,3},{1,0},{2,1},{3,2},{4,7},{5,4},{6,5},{7,6},{8,11},{9,8},{10,9... | collective-permute-start | bytes 589832 | tf_op jit(solution)/shard_map/ppermute | solution.py:66
  73.7 14.2 %collective-permute-start.12 = (bf16[6,64,256]{2,1,0:T(8,128)(2,1)}, bf16[6,64,256]{2,1,0:T(8,128)(2,1)S(1)}, u32[]{:S(2)}, u32[]{:S(2)}) collective-permute-start(bf16[6,64,256]{2,1,0:T(8,128)(2,1)} %get-tuple-element.35), channel_id=1, source_target_pairs={{0,2},{1,3},{2,0},{3,1},{4,6},{5,7},{6,4},{7,5},{8,10},{9,11},{10,... | collective-permute-start | bytes 589832 | tf_op jit(solution)/shard_map/ppermute | solution.py:66
  76.4 11.6 %collective-permute-start.15 = (bf16[6,64,256]{2,1,0:T(8,128)(2,1)}, bf16[6,64,256]{2,1,0:T(8,128)(2,1)S(1)}, u32[]{:S(2)}, u32[]{:S(2)}) collective-permute-start(bf16[6,64,256]{2,1,0:T(8,128)(2,1)} %get-tuple-element.37), channel_id=1, source_target_pairs={{0,1},{1,2},{2,3},{3,0},{4,5},{5,6},{6,7},{7,4},{8,9},{9,10},{10,1... | collective-permute-start | bytes 589832 | tf_op jit(solution)/shard_map/ppermute | solution.py:66
  80.0 10.6 %collective-permute-start.16 = (bf16[6,64,256]{2,1,0:T(8,128)(2,1)}, bf16[6,64,256]{2,1,0:T(8,128)(2,1)S(1)}, u32[]{:S(2)}, u32[]{:S(2)}) collective-permute-start(bf16[6,64,256]{2,1,0:T(8,128)(2,1)} %get-tuple-element.38), channel_id=1, source_target_pairs={{0,3},{1,0},{2,1},{3,2},{4,7},{5,4},{6,5},{7,6},{8,11},{9,8},{10,9... | collective-permute-start | bytes 589832 | tf_op jit(solution)/shard_map/ppermute | solution.py:66
  80.5 10.1 %collective-permute-start.17 = (bf16[6,64,256]{2,1,0:T(8,128)(2,1)}, bf16[6,64,256]{2,1,0:T(8,128)(2,1)S(1)}, u32[]{:S(2)}, u32[]{:S(2)}) collective-permute-start(bf16[6,64,256]{2,1,0:T(8,128)(2,1)} %get-tuple-element.39), channel_id=1, source_target_pairs={{0,2},{1,3},{2,0},{3,1},{4,6},{5,7},{6,4},{7,5},{8,10},{9,11},{10,... | collective-permute-start | bytes 589832 | tf_op jit(solution)/shard_map/ppermute | solution.py:66
  85.8 4.8 %collective-permute-start.19 = (bf16[3,64,256]{2,1,0:T(8,128)(2,1)S(1)}, bf16[3,64,256]{2,1,0:T(8,128)(2,1)S(1)}, u32[]{:S(2)}, u32[]{:S(2)}) collective-permute-start(bf16[3,64,256]{2,1,0:T(8,128)(2,1)S(1)} %get-tuple-element.41), channel_id=1, source_target_pairs={{0,1},{1,2},{2,3},{3,0},{4,5},{5,6},{6,7},{7,4},{8,9},{9,10},{10,1... | collective-permute-start | bytes 294920 | tf_op jit(solution)/shard_map/ppermute | solution.py:66
  87.9 4.6 %collective-permute-start.20 = (bf16[3,64,256]{2,1,0:T(8,128)(2,1)S(1)}, bf16[3,64,256]{2,1,0:T(8,128)(2,1)S(1)}, u32[]{:S(2)}, u32[]{:S(2)}) collective-permute-start(bf16[3,64,256]{2,1,0:T(8,128)(2,1)S(1)} %get-tuple-element.42), channel_id=1, source_target_pairs={{0,3},{1,0},{2,1},{3,2},{4,7},{5,4},{6,5},{7,6},{8,11},{9,8},{10,9... | collective-permute-start | bytes 294920 | tf_op jit(solution)/shard_map/ppermute | solution.py:66
  87.9 6.2 %collective-permute-start.21 = (bf16[3,64,256]{2,1,0:T(8,128)(2,1)S(1)}, bf16[3,64,256]{2,1,0:T(8,128)(2,1)S(1)}, u32[]{:S(2)}, u32[]{:S(2)}) collective-permute-start(bf16[3,64,256]{2,1,0:T(8,128)(2,1)S(1)} %get-tuple-element.43), channel_id=1, source_target_pairs={{0,2},{1,3},{2,0},{3,1},{4,6},{5,7},{6,4},{7,5},{8,10},{9,11},{10,... | collective-permute-start | bytes 294920 | tf_op jit(solution)/shard_map/ppermute | solution.py:66
  112.1 96.0 %all-to-all-start.1 = ((bf16[32,256,256]{2,1,0:T(8,128)(2,1)}), bf16[32,256,256]{2,1,0:T(8,128)(2,1)}, u32[]{:S(2)}, u32[]{:S(2)}) async-start(bf16[32,256,256]{2,1,0:T(8,128)(2,1)} %device_tiles.1), calls=%async_computation.1 | async-start | bytes 8388608 | tf_op jit(solution)/shard_map/all_to_all | solution.py:257
  214.0 6.1 %collective-permute-start.22 = (bf16[8,256,256]{2,1,0:T(8,128)(2,1)}, bf16[8,256,256]{2,1,0:T(8,128)(2,1)}, u32[]{:S(2)}, u32[]{:S(2)}) collective-permute-start(bf16[8,256,256]{2,1,0:T(8,128)(2,1)} %table_of.3), channel_id=1, source_target_pairs={{0,32},{32,0},{64,96},{96,64},{128,160},{160,128},{192,224},{224,1... | collective-permute-start | bytes 3145736 | tf_op jit(solution)/shard_map/ppermute | solution.py:232
  222.3 10.8 %collective-permute-start.23 = (bf16[2,256,256]{2,1,0:T(8,128)(2,1)S(1)}, bf16[2,256,256]{2,1,0:T(8,128)(2,1)S(1)}, u32[]{:S(2)}, u32[]{:S(2)}) collective-permute-start(bf16[2,256,256]{2,1,0:T(8,128)(2,1)S(1)} %get-tuple-element.47), channel_id=1, source_target_pairs={{0,128},{32,160},{64,192},{96,224},{128,0},{160,32},{192,64},{224,... | collective-permute-start | bytes 786440 | tf_op jit(solution)/shard_map/ppermute | solution.py:239
  225.5 13.1 %collective-permute-start.25 = (bf16[2,256,256]{2,1,0:T(8,128)(2,1)S(1)}, bf16[2,256,256]{2,1,0:T(8,128)(2,1)S(1)}, u32[]{:S(2)}, u32[]{:S(2)}) collective-permute-start(bf16[2,256,256]{2,1,0:T(8,128)(2,1)S(1)} %get-tuple-element.48), channel_id=1, source_target_pairs={{0,192},{32,224},{64,0},{96,32},{128,64},{160,96},{192,128},{224,1... | collective-permute-start | bytes 786440 | tf_op jit(solution)/shard_map/ppermute | solution.py:239
  226.6 12.0 %collective-permute-start.24 = (bf16[2,256,256]{2,1,0:T(8,128)(2,1)S(1)}, bf16[2,256,256]{2,1,0:T(8,128)(2,1)S(1)}, u32[]{:S(2)}, u32[]{:S(2)}) collective-permute-start(bf16[2,256,256]{2,1,0:T(8,128)(2,1)S(1)} %get-tuple-element.49), channel_id=1, source_target_pairs={{0,64},{32,96},{64,128},{96,160},{128,192},{160,224},{192,0},{224,... | collective-permute-start | bytes 786440 | tf_op jit(solution)/shard_map/ppermute | solution.py:239
  (6 other events, 5.0 us)

commit v7 on v4

--- a/solution.py
+++ b/solution.py
@@ -59,7 +59,7 @@
 
     pieces, spots = [], []
 
-    def forward(ups, blocks):
+    def forward(asks, ups, blocks):
         picked = pick(asks, n_x, ups, blocks)
         for step, block in zip(STEPS, picked):
             if step:
@@ -89,11 +89,11 @@
             ]
             far = lax.ppermute(jnp.where(odd, down, up), ("grp", "dev"), pairs)
         if k == 1:
-            forward((0, k, -k), (panels, up, down))
+            forward(asks, (0, k, -k), (panels, up, down))
         else:
-            forward((k, -k), (up, down))
+            forward(asks, (k, -k), (up, down))
         up, down = new_up, new_down
-    forward((half,), (far,))
+    forward(asks, (half,), (far,))
 
     entry = jnp.arange(n_z * n_x * NCAP, dtype=jnp.int32)
     s, c = entry // NCAP, entry % NCAP
@@ -173,7 +173,7 @@
             pltpu.VMEM((LT + 1, R * BLOCK, W), jnp.float32),
             pltpu.SemaphoreType.DMA((R,)),
         ],
-        compiler_params=pltpu.CompilerParams(vmem_limit_bytes=50 << 20),
+        compiler_params=pltpu.CompilerParams(vmem_limit_bytes=51 << 20),
         cost_estimate=pl.CostEstimate(
             flops=8_000_000_000, bytes_accessed=12_000_000, transcendentals=0
         ),
@@ -181,45 +181,63 @@
     )(cols, slots, places, where, blocks, pt, *pieces)
 
 
-def table_kernel(labels_ref, got_ref, here_ref, there_ref, sum_ref):
+def table_kernel(labels_ref, got_hbm, here_ref, there_ref, got_ref, sum_ref, sems):
     n_here, n_there = here_ref.shape[0], there_ref.shape[0]
 
-    @pl.loop(0, n_here + n_there)
+    def load(s):
+        return pltpu.make_async_copy(got_hbm.at[s], got_ref.at[s], sems.at[s])
+
+    @pl.loop(0, got_ref.shape[0])
+    def _(s):
+        @pl.when(labels_ref[s] >= 0)
+        def _():
+            load(s).start()
+
+    @pl.loop(0, n_here)
+    def _(t):
+        here_ref[t] = jnp.zeros(here_ref.shape[1:], jnp.float32)
+
+    @pl.loop(0, n_there)
     def _(t):
         sum_ref[t] = jnp.zeros(sum_ref.shape[1:], jnp.float32)
 
     @pl.loop(0, got_ref.shape[0])
     def _(s):
         label = labels_ref[s]
-        at = jnp.where(label < 0, n_here + n_there, label)
-        sum_ref[at] += got_ref[s].astype(jnp.float32)
-
-    @pl.loop(0, n_here)
-    def _(t):
-        here_ref[t] = sum_ref[t]
+
+        @pl.when(label >= 0)
+        def _():
+            load(s).wait()
+
+        @pl.when((label >= 0) & (label < n_here))
+        def _():
+            here_ref[label] += got_ref[s].astype(jnp.float32)
+
+        @pl.when(label >= n_here)
+        def _():
+            sum_ref[label - n_here] += got_ref[s].astype(jnp.float32)
 
     @pl.loop(0, n_there)
     def _(t):
-        there_ref[t] = sum_ref[n_here + t].astype(there_ref.dtype)
+        there_ref[t] = sum_ref[t].astype(there_ref.dtype)
 
 
 def table_of(labels, got, n_here, n_there):
-    rows = 64
-    block = lambda n: pl.BlockSpec((n, rows, W), lambda i, *_: (0, i, 0))
+    vmem = pl.BlockSpec(memory_space=pltpu.VMEM)
     return pl.pallas_call(
         table_kernel,
         out_shape=[
             jax.ShapeDtypeStruct((n_here, W, W), jnp.float32),
             jax.ShapeDtypeStruct((n_there, W, W), jnp.bfloat16),
         ],
-        grid_spec=pltpu.PrefetchScalarGridSpec(
-            num_scalar_prefetch=1,
-            grid=(W // rows,),
-            in_specs=[block(got.shape[0])],
-            out_specs=[block(n_here), block(n_there)],
-            scratch_shapes=[pltpu.VMEM((n_here + n_there + 1, rows, W), jnp.float32)],
-        ),
-        compiler_params=pltpu.CompilerParams(dimension_semantics=("arbitrary",)),
+        in_specs=[pl.BlockSpec(memory_space=pltpu.SMEM), pl.BlockSpec(memory_space=pltpu.HBM)],
+        out_specs=[vmem] * 2,
+        scratch_shapes=[
+            pltpu.VMEM(got.shape, got.dtype),
+            pltpu.VMEM((n_there, W, W), jnp.float32),
+            pltpu.SemaphoreType.DMA((got.shape[0],)),
+        ],
+        compiler_params=pltpu.CompilerParams(vmem_limit_bytes=24 << 20),
         cost_estimate=pl.CostEstimate(flops=2_000_000, bytes_accessed=7_000_000, transcendentals=0),
         name="table_of",
     )(labels, got)

time: 232 us -> 226 us (0.974)
  Pallas kernels: 26.6 us -> 23.2 us
    ppermute x12, waiting for transfers between devices: 7.05 us -> 10.6 us  [forward(): block = lax.ppermute(block, 'dev', along_x(step))]
    pallas_call x1, Pallas kernels: 6.27 us -> 2.87 us  [table_of(): pl.pallas_call(table_kernel, out_shape=[jax.ShapeDtypeStruct((n_here, W,...]
    all_to_all x1, waiting for transfers between devices: 87.2 us -> 84.6 us  [layer(): lax.all_to_all(sending, 'dev', split_axis=0, concat_axis=0, tiled=True)]
  transfers between devices with their start and end apart: 24 -> 24, of which waited for: 13 -> 12; matrix products, arithmetic and copies ran while one was open for 1% -> 1% of each run, Pallas kernels for 2% -> 2%
where the time goes in v7:
time: 226 us; the launch traced here: 223 us
  waiting for transfers between devices  133 us (59%)
  starting transfers between devices  46 us (20%)
  Pallas kernels  23.2 us (10%)
  blocking collectives  15.1 us (7%)
  local copies, waits for them, and re-layouts  3.02 us (1%)
    all_to_all x1, waiting for transfers between devices, layer(): lax.all_to_all(sending, 'dev', split_axis=0, concat_axis=0, tiled=True)  84.6 us
    ppermute x12, starting transfers between devices, forward(): block = lax.ppermute(block, 'dev', along_x(step))  21 us
    pallas_call x1, Pallas kernels, device_tiles(): pl.pallas_call(functools.partial(tiles_kernel, spots), out_shape=jax.Shap...  15.2 us
    all_to_all x1, blocking collectives, fetch(): asks = lax.all_to_all(asked, 'dev', split_axis=0, concat_axis=0, tiled=True)  15.1 us
    ppermute x2, waiting for transfers between devices, fetch(): new_down = lax.ppermute(down, 'dev', along_z(-1))  12.4 us
    ppermute x3, waiting for transfers between devices, sum_over_groups(): total += lax.ppermute(part, 'grp', pairs).astype(jnp.float32)  10.8 us
    ppermute x12, waiting for transfers between devices, forward(): block = lax.ppermute(block, 'dev', along_x(step))  10.6 us
    ppermute x1, waiting for transfers between devices, fetch(): down = lax.ppermute(panels, 'dev', along_z(-1))  8.69 us
  transfers between devices with their start and end apart: 24, of which 12 were waited for; matrix products, arithmetic and copies ran while one was open for 1% of the time, Pallas kernels for 2%

profile of v7, /device:TPU:4, one launch (start us, length us, event | category | flops | bytes accessed | tf_op | source)
XLA Modules:
  0.0 222.8 jit_solution(15966721281295629521)
XLA Ops:
  0.0 5.9 %collective-permute-start.1 = (bf16[12,64,256]{2,1,0:T(8,128)(2,1)}, bf16[12,64,256]{2,1,0:T(8,128)(2,1)S(1)}, u32[]{:S(2)}, u32[]{:S(2)}) collective-permute-start(bf16[12,64,256]{2,1,0:T(8,128)(2,1)} %bitcast.35), channel_id=1, source_target_pairs={{0,28},{1,29},{2,30},{3,31},{4,0},{5,1},{6,2},{7,3},{8,4},{9,5},{1... | collective-permute-start | bytes 1179656 | tf_op jit(solution)/shard_map/ppermute | solution.py:76
  5.9 8.7 %collective-permute-done.1.refs_2_ = bf16[12,64,256]{2,1,0:T(8,128)(2,1)S(1)} collective-permute-done((bf16[12,64,256]{2,1,0:T(8,128)(2,1)}, bf16[12,64,256]{2,1,0:T(8,128)(2,1)S(1)}, u32[]{:S(2)}, u32[]{:S(2)}) %collective-permute-start.1) | collective-permute-done | bytes 393248 | tf_op jit(solution)/shard_map/ppermute | solution.py:76
  14.5 3.6 %collective-permute-start.6 = (bf16[12,64,256]{2,1,0:T(8,128)(2,1)S(1)}, bf16[12,64,256]{2,1,0:T(8,128)(2,1)S(1)}, u32[]{:S(2)}, u32[]{:S(2)}) collective-permute-start(bf16[12,64,256]{2,1,0:T(8,128)(2,1)S(1)} %collective-permute-done.1.refs_2_), channel_id=1, source_target_pairs={{0,28},{1,29},{2,30},{3,31},{4,0},{5,1},{6,2},{7,3},{8,4},{9,5},{1... | collective-permute-start | bytes 1179656 | tf_op jit(solution)/shard_map/ppermute | solution.py:81
  18.1 7.5 %collective-permute-done.6.refs_1_ = bf16[12,64,256]{2,1,0:T(8,128)(2,1)S(1)} collective-permute-done((bf16[12,64,256]{2,1,0:T(8,128)(2,1)S(1)}, bf16[12,64,256]{2,1,0:T(8,128)(2,1)S(1)}, u32[]{:S(2)}, u32[]{:S(2)}) %collective-permute-start.6) | collective-permute-done | bytes 393248 | tf_op jit(solution)/shard_map/ppermute | solution.py:81
  25.7 3.7 %collective-permute-start.11 = (bf16[12,64,256]{2,1,0:T(8,128)(2,1)S(1)}, bf16[12,64,256]{2,1,0:T(8,128)(2,1)S(1)}, u32[]{:S(2)}, u32[]{:S(2)}) collective-permute-start(bf16[12,64,256]{2,1,0:T(8,128)(2,1)S(1)} %collective-permute-done.6.refs_1_), channel_id=1, source_target_pairs={{0,28},{1,29},{2,30},{3,31},{4,0},{5,1},{6,2},{7,3},{8,4},{9,5},{1... | collective-permute-start | bytes 1179656 | tf_op jit(solution)/shard_map/ppermute | solution.py:81
  31.1 4.9 %collective-permute-done.11.refs_1_ = bf16[12,64,256]{2,1,0:T(8,128)(2,1)S(1)} collective-permute-done((bf16[12,64,256]{2,1,0:T(8,128)(2,1)S(1)}, bf16[12,64,256]{2,1,0:T(8,128)(2,1)S(1)}, u32[]{:S(2)}, u32[]{:S(2)}) %collective-permute-start.11) | collective-permute-done | bytes 393248 | tf_op jit(solution)/shard_map/ppermute | solution.py:81
  36.0 3.4 %collective-permute-done.10.refs_0_ = bf16[12,64,256]{2,1,0:T(8,128)(2,1)S(1)} collective-permute-done((bf16[12,64,256]{2,1,0:T(8,128)(2,1)S(1)}, bf16[12,64,256]{2,1,0:T(8,128)(2,1)S(1)}, u32[]{:S(2)}, u32[]{:S(2)}) %collective-permute-start.10) | collective-permute-done | bytes 393248 | tf_op jit(solution)/shard_map/ppermute | solution.py:80
  39.6 15.1 %all_to_all.16 = s32[32,1,13]{2,1,0:T(1,128)S(1)} all-to-all(s32[32,1,13]{2,1,0:T(1,128)S(1)} %bitcast.46), channel_id=1, replica_groups=mesh['grp'=8,'dev'=32] {'dev'}, dimensions={0} | all-to-all | bytes 3328 | tf_op jit(solution)/shard_map/all_to_all | solution.py:77
  54.7 1.0 copy-done
  56.7 1.5 collective-permute-start.2
  58.8 3.5 %collective-permute-start.4 = (bf16[9,64,256]{2,1,0:T(8,128)(2,1)S(1)}, bf16[9,64,256]{2,1,0:T(8,128)(2,1)S(1)}, u32[]{:S(2)}, u32[]{:S(2)}) collective-permute-start(bf16[9,64,256]{2,1,0:T(8,128)(2,1)S(1)} %get-tuple-element.25), channel_id=1, source_target_pairs={{0,2},{1,3},{2,0},{3,1},{4,6},{5,7},{6,4},{7,5},{8,10},{9,11},{10,... | collective-permute-start | bytes 884744 | tf_op jit(solution)/shard_map/ppermute | solution.py:66
  62.3 1.6 pick.5
  64.0 1.7 pick.6
  65.7 4.7 %collective-permute-done.2.refs_0_ = bf16[9,64,256]{2,1,0:T(8,128)(2,1)S(1)} collective-permute-done((bf16[9,64,256]{2,1,0:T(8,128)(2,1)S(1)}, bf16[9,64,256]{2,1,0:T(8,128)(2,1)S(1)}, u32[]{:S(2)}, u32[]{:S(2)}) %collective-permute-start.2) | collective-permute-done | bytes 294944 | tf_op jit(solution)/shard_map/ppermute | solution.py:66
  70.4 4.0 %collective-permute-start.9 = (bf16[6,64,256]{2,1,0:T(8,128)(2,1)}, bf16[6,64,256]{2,1,0:T(8,128)(2,1)S(1)}, u32[]{:S(2)}, u32[]{:S(2)}) collective-permute-start(bf16[6,64,256]{2,1,0:T(8,128)(2,1)} %get-tuple-element.29), channel_id=1, source_target_pairs={{0,2},{1,3},{2,0},{3,1},{4,6},{5,7},{6,4},{7,5},{8,10},{9,11},{10,... | collective-permute-start | bytes 589832 | tf_op jit(solution)/shard_map/ppermute | solution.py:66
  74.4 2.5 %collective-permute-start.12 = (bf16[6,64,256]{2,1,0:T(8,128)(2,1)}, bf16[6,64,256]{2,1,0:T(8,128)(2,1)S(1)}, u32[]{:S(2)}, u32[]{:S(2)}) collective-permute-start(bf16[6,64,256]{2,1,0:T(8,128)(2,1)} %get-tuple-element.31), channel_id=1, source_target_pairs={{0,1},{1,2},{2,3},{3,0},{4,5},{5,6},{6,7},{7,4},{8,9},{9,10},{10,1... | collective-permute-start | bytes 589832 | tf_op jit(solution)/shard_map/ppermute | solution.py:66
  76.9 1.9 collective-permute-done.7.refs_4_
  78.8 4.2 %collective-permute-start.14 = (bf16[6,64,256]{2,1,0:T(8,128)(2,1)}, bf16[6,64,256]{2,1,0:T(8,128)(2,1)S(1)}, u32[]{:S(2)}, u32[]{:S(2)}) collective-permute-start(bf16[6,64,256]{2,1,0:T(8,128)(2,1)} %get-tuple-element.33), channel_id=1, source_target_pairs={{0,2},{1,3},{2,0},{3,1},{4,6},{5,7},{6,4},{7,5},{8,10},{9,11},{10,... | collective-permute-start | bytes 589832 | tf_op jit(solution)/shard_map/ppermute | solution.py:66
  84.8 2.4 %collective-permute-start.16 = (bf16[3,64,256]{2,1,0:T(8,128)(2,1)S(1)}, bf16[3,64,256]{2,1,0:T(8,128)(2,1)S(1)}, u32[]{:S(2)}, u32[]{:S(2)}) collective-permute-start(bf16[3,64,256]{2,1,0:T(8,128)(2,1)S(1)} %get-tuple-element.35), channel_id=1, source_target_pairs={{0,1},{1,2},{2,3},{3,0},{4,5},{5,6},{6,7},{7,4},{8,9},{9,10},{10,1... | collective-permute-start | bytes 294920 | tf_op jit(solution)/shard_map/ppermute | solution.py:66
  87.2 2.2 collective-permute-start.18
  89.5 2.4 %collective-permute-done.17.refs_13_ = bf16[3,64,256]{2,1,0:T(8,128)(2,1)S(1)} collective-permute-done((bf16[3,64,256]{2,1,0:T(8,128)(2,1)S(1)}, bf16[3,64,256]{2,1,0:T(8,128)(2,1)S(1)}, u32[]{:S(2)}, u32[]{:S(2)}) %collective-permute-start.17) | collective-permute-done | bytes 98336 | tf_op jit(solution)/shard_map/ppermute | solution.py:66
  91.8 1.6 collective-permute-done.18.refs_14_
  93.4 15.2 %device_tiles.1 = bf16[32,256,256]{2,1,0:T(8,128)(2,1)} custom-call(s32[12,27]{1,0:T(8,128)S(1)} %get-tuple-element.49.cols_ref, s32[12,27]{1,0:T(8,128)S(1)} %get-tuple-element.48.slots_ref, s32[16]{0:T(128)S(1)} %get-tuple-element.46.places_ref, s32[96]{0:T(128)S(1)} %fusion.3.where_ref, bf16[12,64,1728]{2,1,0:T(8,128)(2,1)} %bitcast.48, ...), custom_call_target="tpu_custom_call" | custom-call | flops 8000000000 | bytes 12000000 | tf_op jit(solution)/shard_map/device_tiles/pallas_call | solution.py:165
  108.7 6.5 %all-to-all-start.1 = ((bf16[32,256,256]{2,1,0:T(8,128)(2,1)}), bf16[32,256,256]{2,1,0:T(8,128)(2,1)}, u32[]{:S(2)}, u32[]{:S(2)}) async-start(bf16[32,256,256]{2,1,0:T(8,128)(2,1)} %device_tiles.1), calls=%async_computation.1 | async-start | bytes 8388608 | tf_op jit(solution)/shard_map/all_to_all | solution.py:279
  115.3 84.6 %all-to-all-done.1.got_hbm = bf16[32,256,256]{2,1,0:T(8,128)(2,1)} async-done(((bf16[32,256,256]{2,1,0:T(8,128)(2,1)}), bf16[32,256,256]{2,1,0:T(8,128)(2,1)}, u32[]{:S(2)}, u32[]{:S(2)}) %all-to-all-start.1) | async-done | bytes 4194336 | tf_op jit(solution)/shard_map/all_to_all | solution.py:279
  199.9 2.9 %table_of.1 = (f32[8,256,256]{2,1,0:T(8,128)S(1)}, bf16[8,256,256]{2,1,0:T(8,128)(2,1)S(1)}) custom-call(s32[32]{0:T(128)S(1)} %fusion.7.labels_ref, bf16[32,256,256]{2,1,0:T(8,128)(2,1)} %all-to-all-done.1.got_hbm), custom_call_target="tpu_custom_call" | custom-call | flops 2000000 | bytes 7000000 | tf_op jit(solution)/shard_map/table_of/pallas_call | solution.py:227
  202.9 2.6 %collective-permute-done.19 = bf16[8,256,256]{2,1,0:T(8,128)(2,1)S(1)} collective-permute-done((bf16[8,256,256]{2,1,0:T(8,128)(2,1)S(1)}, bf16[8,256,256]{2,1,0:T(8,128)(2,1)S(1)}, u32[]{:S(2)}, u32[]{:S(2)}) %collective-permute-start.19) | collective-permute-done | bytes 1048608 | tf_op jit(solution)/shard_map/ppermute | solution.py:256
  205.9 3.1 %collective-permute-start.20 = (bf16[2,256,256]{2,1,0:T(8,128)(2,1)S(1)}, bf16[2,256,256]{2,1,0:T(8,128)(2,1)S(1)}, u32[]{:S(2)}, u32[]{:S(2)}) collective-permute-start(bf16[2,256,256]{2,1,0:T(8,128)(2,1)S(1)} %get-tuple-element.43), channel_id=1, source_target_pairs={{0,128},{32,160},{64,192},{96,224},{128,0},{160,32},{192,64},{224,... | collective-permute-start | bytes 786440 | tf_op jit(solution)/shard_map/ppermute | solution.py:261
  209.1 1.2 collective-permute-start.22
  211.1 5.6 %collective-permute-done.20 = bf16[2,256,256]{2,1,0:T(8,128)(2,1)S(1)} collective-permute-done((bf16[2,256,256]{2,1,0:T(8,128)(2,1)S(1)}, bf16[2,256,256]{2,1,0:T(8,128)(2,1)S(1)}, u32[]{:S(2)}, u32[]{:S(2)}) %collective-permute-start.20) | collective-permute-done | bytes 262176 | tf_op jit(solution)/shard_map/ppermute | solution.py:261
  216.7 5.2 %collective-permute-done.22 = bf16[2,256,256]{2,1,0:T(8,128)(2,1)S(1)} collective-permute-done((bf16[2,256,256]{2,1,0:T(8,128)(2,1)S(1)}, bf16[2,256,256]{2,1,0:T(8,128)(2,1)S(1)}, u32[]{:S(2)}, u32[]{:S(2)}) %collective-permute-start.22) | collective-permute-done | bytes 262176 | tf_op jit(solution)/shard_map/ppermute | solution.py:261
  221.9 0.9 fusion.2
  (49 shorter events, 6.8 us)
Async XLA Ops:
  0.0 14.5 %collective-permute-start.1 = (bf16[12,64,256]{2,1,0:T(8,128)(2,1)}, bf16[12,64,256]{2,1,0:T(8,128)(2,1)S(1)}, u32[]{:S(2)}, u32[]{:S(2)}) collective-permute-start(bf16[12,64,256]{2,1,0:T(8,128)(2,1)} %bitcast.35), channel_id=1, source_target_pairs={{0,28},{1,29},{2,30},{3,31},{4,0},{5,1},{6,2},{7,3},{8,4},{9,5},{1... | collective-permute-start | bytes 1179656 | tf_op jit(solution)/shard_map/ppermute | solution.py:76
  5.9 12.3 %collective-permute-start = (bf16[12,64,256]{2,1,0:T(8,128)(2,1)}, bf16[12,64,256]{2,1,0:T(8,128)(2,1)S(1)}, u32[]{:S(2)}, u32[]{:S(2)}) collective-permute-start(bf16[12,64,256]{2,1,0:T(8,128)(2,1)} %bitcast.36), channel_id=1, source_target_pairs={{0,4},{1,5},{2,6},{3,7},{4,8},{5,9},{6,10},{7,11},{8,12},{9,13},{1... | collective-permute-start | bytes 1179656 | tf_op jit(solution)/shard_map/ppermute | solution.py:75
  14.5 11.1 %collective-permute-start.6 = (bf16[12,64,256]{2,1,0:T(8,128)(2,1)S(1)}, bf16[12,64,256]{2,1,0:T(8,128)(2,1)S(1)}, u32[]{:S(2)}, u32[]{:S(2)}) collective-permute-start(bf16[12,64,256]{2,1,0:T(8,128)(2,1)S(1)} %collective-permute-done.1.refs_2_), channel_id=1, source_target_pairs={{0,28},{1,29},{2,30},{3,31},{4,0},{5,1},{6,2},{7,3},{8,4},{9,5},{1... | collective-permute-start | bytes 1179656 | tf_op jit(solution)/shard_map/ppermute | solution.py:81
  18.1 11.2 %collective-permute-start.5 = (bf16[12,64,256]{2,1,0:T(8,128)(2,1)S(1)}, bf16[12,64,256]{2,1,0:T(8,128)(2,1)S(1)}, u32[]{:S(2)}, u32[]{:S(2)}) collective-permute-start(bf16[12,64,256]{2,1,0:T(8,128)(2,1)S(1)} %collective-permute-done.refs_1_), channel_id=1, source_target_pairs={{0,4},{1,5},{2,6},{3,7},{4,8},{5,9},{6,10},{7,11},{8,12},{9,13},{1... | collective-permute-start | bytes 1179656 | tf_op jit(solution)/shard_map/ppermute | solution.py:80
  25.7 10.4 %collective-permute-start.11 = (bf16[12,64,256]{2,1,0:T(8,128)(2,1)S(1)}, bf16[12,64,256]{2,1,0:T(8,128)(2,1)S(1)}, u32[]{:S(2)}, u32[]{:S(2)}) collective-permute-start(bf16[12,64,256]{2,1,0:T(8,128)(2,1)S(1)} %collective-permute-done.6.refs_1_), channel_id=1, source_target_pairs={{0,28},{1,29},{2,30},{3,31},{4,0},{5,1},{6,2},{7,3},{8,4},{9,5},{1... | collective-permute-start | bytes 1179656 | tf_op jit(solution)/shard_map/ppermute | solution.py:81
  29.3 10.1 %collective-permute-start.10 = (bf16[12,64,256]{2,1,0:T(8,128)(2,1)S(1)}, bf16[12,64,256]{2,1,0:T(8,128)(2,1)S(1)}, u32[]{:S(2)}, u32[]{:S(2)}) collective-permute-start(bf16[12,64,256]{2,1,0:T(8,128)(2,1)S(1)} %collective-permute-done.5.refs_0_), channel_id=1, source_target_pairs={{0,4},{1,5},{2,6},{3,7},{4,8},{5,9},{6,10},{7,11},{8,12},{9,13},{1... | collective-permute-start | bytes 1179656 | tf_op jit(solution)/shard_map/ppermute | solution.py:80
  29.4 53.6 %copy-start.3 = (s32[1,1,12,27]{3,1,2,0:T(1,128)S(1)}, s32[1,1,12,27]{3,1,2,0:T(1,128)}, u32[]{:S(2)}) copy-start(s32[1,1,12,27]{3,1,2,0:T(1,128)} %param.11) | copy-start | bytes 3892
  29.4 53.6 %copy-start.4 = (s32[1,1,12,27]{3,1,2,0:T(1,128)S(1)}, s32[1,1,12,27]{3,1,2,0:T(1,128)}, u32[]{:S(2)}) copy-start(s32[1,1,12,27]{3,1,2,0:T(1,128)} %param.9) | copy-start | bytes 3892
  31.0 52.0 %copy-start.1 = (bf16[1,1,12,64,256]{4,3,2,1,0:T(8,128)(2,1)S(1)}, bf16[1,1,12,64,256]{4,3,2,1,0:T(8,128)(2,1)}, u32[]{:S(2)}) copy-start(bf16[1,1,12,64,256]{4,3,2,1,0:T(8,128)(2,1)} %param.8) | copy-start | bytes 1179652
  39.5 39.3 %collective-permute-start.15 = (bf16[12,64,256]{2,1,0:T(8,128)(2,1)S(1)}, bf16[12,64,256]{2,1,0:T(8,128)(2,1)S(1)}, u32[]{:S(2)}, u32[]{:S(2)}) collective-permute-start(bf16[12,64,256]{2,1,0:T(8,128)(2,1)S(1)} %broadcast_select_fusion), channel_id=1, source_target_pairs={{0,4},{1,5},{2,6},{3,7},{4,8},{5,9},{6,10},{7,11},{8,12},{9,13},{1... | collective-permute-start | bytes 1179656 | tf_op jit(solution)/shard_map/ppermute | solution.py:90
  54.7 1.0 copy-start
  56.7 22.1 %copy-start.2 = (bf16[9,64,256]{2,1,0:T(8,128)(2,1)}, bf16[9,64,256]{2,1,0:T(8,128)(2,1)S(1)}, u32[]{:S(2)}) copy-start(bf16[9,64,256]{2,1,0:T(8,128)(2,1)S(1)} %get-tuple-element.26.refs_3_) | copy-start | bytes 884740
  56.7 13.7 %collective-permute-start.2 = (bf16[9,64,256]{2,1,0:T(8,128)(2,1)S(1)}, bf16[9,64,256]{2,1,0:T(8,128)(2,1)S(1)}, u32[]{:S(2)}, u32[]{:S(2)}) collective-permute-start(bf16[9,64,256]{2,1,0:T(8,128)(2,1)S(1)} %get-tuple-element.23), channel_id=1, source_target_pairs={{0,1},{1,2},{2,3},{3,0},{4,5},{5,6},{6,7},{7,4},{8,9},{9,10},{10,1... | collective-permute-start | bytes 884744 | tf_op jit(solution)/shard_map/ppermute | solution.py:66
  58.2 12.1 %collective-permute-start.3 = (bf16[9,64,256]{2,1,0:T(8,128)(2,1)S(1)}, bf16[9,64,256]{2,1,0:T(8,128)(2,1)S(1)}, u32[]{:S(2)}, u32[]{:S(2)}) collective-permute-start(bf16[9,64,256]{2,1,0:T(8,128)(2,1)S(1)} %get-tuple-element.24), channel_id=1, source_target_pairs={{0,3},{1,0},{2,1},{3,2},{4,7},{5,4},{6,5},{7,6},{8,11},{9,8},{10,9... | collective-permute-start | bytes 884744 | tf_op jit(solution)/shard_map/ppermute | solution.py:66
  58.8 15.6 %collective-permute-start.4 = (bf16[9,64,256]{2,1,0:T(8,128)(2,1)S(1)}, bf16[9,64,256]{2,1,0:T(8,128)(2,1)S(1)}, u32[]{:S(2)}, u32[]{:S(2)}) collective-permute-start(bf16[9,64,256]{2,1,0:T(8,128)(2,1)S(1)} %get-tuple-element.25), channel_id=1, source_target_pairs={{0,2},{1,3},{2,0},{3,1},{4,6},{5,7},{6,4},{7,5},{8,10},{9,11},{10,... | collective-permute-start | bytes 884744 | tf_op jit(solution)/shard_map/ppermute | solution.py:66
  64.0 14.8 %collective-permute-start.7 = (bf16[6,64,256]{2,1,0:T(8,128)(2,1)S(1)}, bf16[6,64,256]{2,1,0:T(8,128)(2,1)S(1)}, u32[]{:S(2)}, u32[]{:S(2)}) collective-permute-start(bf16[6,64,256]{2,1,0:T(8,128)(2,1)S(1)} %get-tuple-element.27), channel_id=1, source_target_pairs={{0,1},{1,2},{2,3},{3,0},{4,5},{5,6},{6,7},{7,4},{8,9},{9,10},{10,1... | collective-permute-start | bytes 589832 | tf_op jit(solution)/shard_map/ppermute | solution.py:66
  70.3 14.4 %collective-permute-start.8 = (bf16[6,64,256]{2,1,0:T(8,128)(2,1)}, bf16[6,64,256]{2,1,0:T(8,128)(2,1)S(1)}, u32[]{:S(2)}, u32[]{:S(2)}) collective-permute-start(bf16[6,64,256]{2,1,0:T(8,128)(2,1)} %get-tuple-element.28), channel_id=1, source_target_pairs={{0,3},{1,0},{2,1},{3,2},{4,7},{5,4},{6,5},{7,6},{8,11},{9,8},{10,9... | collective-permute-start | bytes 589832 | tf_op jit(solution)/shard_map/ppermute | solution.py:66
  70.4 16.9 %collective-permute-start.9 = (bf16[6,64,256]{2,1,0:T(8,128)(2,1)}, bf16[6,64,256]{2,1,0:T(8,128)(2,1)S(1)}, u32[]{:S(2)}, u32[]{:S(2)}) collective-permute-start(bf16[6,64,256]{2,1,0:T(8,128)(2,1)} %get-tuple-element.29), channel_id=1, source_target_pairs={{0,2},{1,3},{2,0},{3,1},{4,6},{5,7},{6,4},{7,5},{8,10},{9,11},{10,... | collective-permute-start | bytes 589832 | tf_op jit(solution)/shard_map/ppermute | solution.py:66
  74.4 12.9 %collective-permute-start.12 = (bf16[6,64,256]{2,1,0:T(8,128)(2,1)}, bf16[6,64,256]{2,1,0:T(8,128)(2,1)S(1)}, u32[]{:S(2)}, u32[]{:S(2)}) collective-permute-start(bf16[6,64,256]{2,1,0:T(8,128)(2,1)} %get-tuple-element.31), channel_id=1, source_target_pairs={{0,1},{1,2},{2,3},{3,0},{4,5},{5,6},{6,7},{7,4},{8,9},{9,10},{10,1... | collective-permute-start | bytes 589832 | tf_op jit(solution)/shard_map/ppermute | solution.py:66
  78.8 10.6 %collective-permute-start.13 = (bf16[6,64,256]{2,1,0:T(8,128)(2,1)}, bf16[6,64,256]{2,1,0:T(8,128)(2,1)S(1)}, u32[]{:S(2)}, u32[]{:S(2)}) collective-permute-start(bf16[6,64,256]{2,1,0:T(8,128)(2,1)} %get-tuple-element.32), channel_id=1, source_target_pairs={{0,3},{1,0},{2,1},{3,2},{4,7},{5,4},{6,5},{7,6},{8,11},{9,8},{10,9... | collective-permute-start | bytes 589832 | tf_op jit(solution)/shard_map/ppermute | solution.py:66
  78.8 10.6 %collective-permute-start.14 = (bf16[6,64,256]{2,1,0:T(8,128)(2,1)}, bf16[6,64,256]{2,1,0:T(8,128)(2,1)S(1)}, u32[]{:S(2)}, u32[]{:S(2)}) collective-permute-start(bf16[6,64,256]{2,1,0:T(8,128)(2,1)} %get-tuple-element.33), channel_id=1, source_target_pairs={{0,2},{1,3},{2,0},{3,1},{4,6},{5,7},{6,4},{7,5},{8,10},{9,11},{10,... | collective-permute-start | bytes 589832 | tf_op jit(solution)/shard_map/ppermute | solution.py:66
  84.8 4.7 %collective-permute-start.16 = (bf16[3,64,256]{2,1,0:T(8,128)(2,1)S(1)}, bf16[3,64,256]{2,1,0:T(8,128)(2,1)S(1)}, u32[]{:S(2)}, u32[]{:S(2)}) collective-permute-start(bf16[3,64,256]{2,1,0:T(8,128)(2,1)S(1)} %get-tuple-element.35), channel_id=1, source_target_pairs={{0,1},{1,2},{2,3},{3,0},{4,5},{5,6},{6,7},{7,4},{8,9},{9,10},{10,1... | collective-permute-start | bytes 294920 | tf_op jit(solution)/shard_map/ppermute | solution.py:66
  87.2 4.6 %collective-permute-start.17 = (bf16[3,64,256]{2,1,0:T(8,128)(2,1)S(1)}, bf16[3,64,256]{2,1,0:T(8,128)(2,1)S(1)}, u32[]{:S(2)}, u32[]{:S(2)}) collective-permute-start(bf16[3,64,256]{2,1,0:T(8,128)(2,1)S(1)} %get-tuple-element.36), channel_id=1, source_target_pairs={{0,3},{1,0},{2,1},{3,2},{4,7},{5,4},{6,5},{7,6},{8,11},{9,8},{10,9... | collective-permute-start | bytes 294920 | tf_op jit(solution)/shard_map/ppermute | solution.py:66
  87.2 6.2 %collective-permute-start.18 = (bf16[3,64,256]{2,1,0:T(8,128)(2,1)S(1)}, bf16[3,64,256]{2,1,0:T(8,128)(2,1)S(1)}, u32[]{:S(2)}, u32[]{:S(2)}) collective-permute-start(bf16[3,64,256]{2,1,0:T(8,128)(2,1)S(1)} %get-tuple-element.37), channel_id=1, source_target_pairs={{0,2},{1,3},{2,0},{3,1},{4,6},{5,7},{6,4},{7,5},{8,10},{9,11},{10,... | collective-permute-start | bytes 294920 | tf_op jit(solution)/shard_map/ppermute | solution.py:66
  108.7 91.3 %all-to-all-start.1 = ((bf16[32,256,256]{2,1,0:T(8,128)(2,1)}), bf16[32,256,256]{2,1,0:T(8,128)(2,1)}, u32[]{:S(2)}, u32[]{:S(2)}) async-start(bf16[32,256,256]{2,1,0:T(8,128)(2,1)} %device_tiles.1), calls=%async_computation.1 | async-start | bytes 8388608 | tf_op jit(solution)/shard_map/all_to_all | solution.py:279
  202.8 2.7 %collective-permute-start.19 = (bf16[8,256,256]{2,1,0:T(8,128)(2,1)S(1)}, bf16[8,256,256]{2,1,0:T(8,128)(2,1)S(1)}, u32[]{:S(2)}, u32[]{:S(2)}) collective-permute-start(bf16[8,256,256]{2,1,0:T(8,128)(2,1)S(1)} %get-tuple-element.40), channel_id=1, source_target_pairs={{0,32},{32,0},{64,96},{96,64},{128,160},{160,128},{192,224},{224,1... | collective-permute-start | bytes 3145736 | tf_op jit(solution)/shard_map/ppermute | solution.py:256
  205.9 10.8 %collective-permute-start.20 = (bf16[2,256,256]{2,1,0:T(8,128)(2,1)S(1)}, bf16[2,256,256]{2,1,0:T(8,128)(2,1)S(1)}, u32[]{:S(2)}, u32[]{:S(2)}) collective-permute-start(bf16[2,256,256]{2,1,0:T(8,128)(2,1)S(1)} %get-tuple-element.43), channel_id=1, source_target_pairs={{0,128},{32,160},{64,192},{96,224},{128,0},{160,32},{192,64},{224,... | collective-permute-start | bytes 786440 | tf_op jit(solution)/shard_map/ppermute | solution.py:261
  209.1 12.8 %collective-permute-start.22 = (bf16[2,256,256]{2,1,0:T(8,128)(2,1)S(1)}, bf16[2,256,256]{2,1,0:T(8,128)(2,1)S(1)}, u32[]{:S(2)}, u32[]{:S(2)}) collective-permute-start(bf16[2,256,256]{2,1,0:T(8,128)(2,1)S(1)} %get-tuple-element.44), channel_id=1, source_target_pairs={{0,192},{32,224},{64,0},{96,32},{128,64},{160,96},{192,128},{224,1... | collective-permute-start | bytes 786440 | tf_op jit(solution)/shard_map/ppermute | solution.py:261
  210.2 11.7 %collective-permute-start.21 = (bf16[2,256,256]{2,1,0:T(8,128)(2,1)S(1)}, bf16[2,256,256]{2,1,0:T(8,128)(2,1)S(1)}, u32[]{:S(2)}, u32[]{:S(2)}) collective-permute-start(bf16[2,256,256]{2,1,0:T(8,128)(2,1)S(1)} %get-tuple-element.45), channel_id=1, source_target_pairs={{0,64},{32,96},{64,128},{96,160},{128,192},{160,224},{192,0},{224,... | collective-permute-start | bytes 786440 | tf_op jit(solution)/shard_map/ppermute | solution.py:261

commit v8 on v7

--- a/solution.py
+++ b/solution.py
@@ -16,7 +16,7 @@
 NCAP = 3
 LT = 16
 PAIR = 2 * BLOCK
-STEPS = (1, -1, 2, 0)
+STEPS = (2, 1, -1, 0)
 
 
 def pick_kernel(n_x, ups, asks_ref, *refs):
@@ -75,6 +75,7 @@
     up = lax.ppermute(panels, "dev", along_z(1))
     down = lax.ppermute(panels, "dev", along_z(-1))
     asks = lax.all_to_all(asked, "dev", split_axis=0, concat_axis=0, tiled=True)
+    forward(asked, (0,), (panels,))
     for k in range(1, half):
         if k + 1 < half:
             new_up = lax.ppermute(up, "dev", along_z(1))
@@ -88,10 +89,7 @@
                 for s, t in along_z(-1 if g % 2 else 1)
             ]
             far = lax.ppermute(jnp.where(odd, down, up), ("grp", "dev"), pairs)
-        if k == 1:
-            forward(asks, (0, k, -k), (panels, up, down))
-        else:
-            forward(asks, (k, -k), (up, down))
+        forward(asks, (k, -k), (up, down))
         up, down = new_up, new_down
     forward(asks, (half,), (far,))
 

time: 226 us -> 233 us (1.031)
  local copies, waits for them, and re-layouts: 3.02 us -> 6.98 us
  waiting for transfers between devices: 133 us -> 136 us
    all_to_all x1, waiting for transfers between devices: 84.6 us -> 91.4 us  [layer(): lax.all_to_all(sending, 'dev', split_axis=0, concat_axis=0, tiled=True)]
    ppermute x12 -> x15, waiting for transfers between devices: 10.6 us -> 6.53 us  [forward(): block = lax.ppermute(block, 'dev', along_x(step))]
    unnamed x12 -> x24, local copies, waits for them, and re-layouts: 1.77 us -> 5.73 us
    ppermute x12 -> x15, starting transfers between devices: 21 us -> 22.2 us  [forward(): block = lax.ppermute(block, 'dev', along_x(step))]
    pallas_call x4 -> x5, Pallas kernels: 5.14 us -> 5.95 us  [pick(): pl.pallas_call(functools.partial(pick_kernel, n_x, ups), out_shape=[jax.S...]
  transfers between devices with their start and end apart: 24 -> 27, of which waited for: 12 -> 12; matrix products, arithmetic and copies ran while one was open for 1% -> 1% of each run, Pallas kernels for 2% -> 3%
where the time goes in v8:
time: 233 us; the launch traced here: 232 us
  waiting for transfers between devices  136 us (58%)
  starting transfers between devices  46.2 us (20%)
  Pallas kernels  24.1 us (10%)
  blocking collectives  16.2 us (7%)
  local copies, waits for them, and re-layouts  6.98 us (3%)
    all_to_all x1, waiting for transfers between devices, layer(): lax.all_to_all(sending, 'dev', split_axis=0, concat_axis=0, tiled=True)  91.4 us
    ppermute x15, starting transfers between devices, forward(): block = lax.ppermute(block, 'dev', along_x(step))  22.2 us
    all_to_all x1, blocking collectives, fetch(): asks = lax.all_to_all(asked, 'dev', split_axis=0, concat_axis=0, tiled=True)  16.2 us
    pallas_call x1, Pallas kernels, device_tiles(): pl.pallas_call(functools.partial(tiles_kernel, spots), out_shape=jax.Shap...  15.2 us
    ppermute x2, waiting for transfers between devices, fetch(): new_down = lax.ppermute(down, 'dev', along_z(-1))  12.4 us
    ppermute x3, waiting for transfers between devices, sum_over_groups(): total += lax.ppermute(part, 'grp', pairs).astype(jnp.float32)  10.8 us
    ppermute x1, waiting for transfers between devices, fetch(): down = lax.ppermute(panels, 'dev', along_z(-1))  8.69 us
    ppermute x2, starting transfers between devices, fetch(): new_down = lax.ppermute(down, 'dev', along_z(-1))  7.28 us
  transfers between devices with their start and end apart: 27, of which 12 were waited for; matrix products, arithmetic and copies ran while one was open for 1% of the time, Pallas kernels for 3%

profile of v8, /device:TPU:4, one launch (start us, length us, event | category | flops | bytes accessed | tf_op | source)
XLA Modules:
  0.0 231.8 jit_solution(12422203552524328031)
XLA Ops:
  0.0 5.9 %collective-permute-start.4 = (bf16[12,64,256]{2,1,0:T(8,128)(2,1)}, bf16[12,64,256]{2,1,0:T(8,128)(2,1)S(1)}, u32[]{:S(2)}, u32[]{:S(2)}) collective-permute-start(bf16[12,64,256]{2,1,0:T(8,128)(2,1)} %bitcast.37), channel_id=1, source_target_pairs={{0,28},{1,29},{2,30},{3,31},{4,0},{5,1},{6,2},{7,3},{8,4},{9,5},{1... | collective-permute-start | bytes 1179656 | tf_op jit(solution)/shard_map/ppermute | solution.py:76
  5.9 8.7 %collective-permute-done.4.refs_1_ = bf16[12,64,256]{2,1,0:T(8,128)(2,1)S(1)} collective-permute-done((bf16[12,64,256]{2,1,0:T(8,128)(2,1)}, bf16[12,64,256]{2,1,0:T(8,128)(2,1)S(1)}, u32[]{:S(2)}, u32[]{:S(2)}) %collective-permute-start.4) | collective-permute-done | bytes 393248 | tf_op jit(solution)/shard_map/ppermute | solution.py:76
  14.5 3.6 %collective-permute-start.9 = (bf16[12,64,256]{2,1,0:T(8,128)(2,1)S(1)}, bf16[12,64,256]{2,1,0:T(8,128)(2,1)S(1)}, u32[]{:S(2)}, u32[]{:S(2)}) collective-permute-start(bf16[12,64,256]{2,1,0:T(8,128)(2,1)S(1)} %collective-permute-done.4.refs_1_), channel_id=1, source_target_pairs={{0,28},{1,29},{2,30},{3,31},{4,0},{5,1},{6,2},{7,3},{8,4},{9,5},{1... | collective-permute-start | bytes 1179656 | tf_op jit(solution)/shard_map/ppermute | solution.py:82
  18.1 7.5 %collective-permute-done.9.refs_1_ = bf16[12,64,256]{2,1,0:T(8,128)(2,1)S(1)} collective-permute-done((bf16[12,64,256]{2,1,0:T(8,128)(2,1)S(1)}, bf16[12,64,256]{2,1,0:T(8,128)(2,1)S(1)}, u32[]{:S(2)}, u32[]{:S(2)}) %collective-permute-start.9) | collective-permute-done | bytes 393248 | tf_op jit(solution)/shard_map/ppermute | solution.py:82
  25.7 3.7 %collective-permute-start.14 = (bf16[12,64,256]{2,1,0:T(8,128)(2,1)S(1)}, bf16[12,64,256]{2,1,0:T(8,128)(2,1)S(1)}, u32[]{:S(2)}, u32[]{:S(2)}) collective-permute-start(bf16[12,64,256]{2,1,0:T(8,128)(2,1)S(1)} %collective-permute-done.9.refs_1_), channel_id=1, source_target_pairs={{0,28},{1,29},{2,30},{3,31},{4,0},{5,1},{6,2},{7,3},{8,4},{9,5},{1... | collective-permute-start | bytes 1179656 | tf_op jit(solution)/shard_map/ppermute | solution.py:82
  31.1 4.9 %collective-permute-done.14.refs_1_ = bf16[12,64,256]{2,1,0:T(8,128)(2,1)S(1)} collective-permute-done((bf16[12,64,256]{2,1,0:T(8,128)(2,1)S(1)}, bf16[12,64,256]{2,1,0:T(8,128)(2,1)S(1)}, u32[]{:S(2)}, u32[]{:S(2)}) %collective-permute-start.14) | collective-permute-done | bytes 393248 | tf_op jit(solution)/shard_map/ppermute | solution.py:82
  36.0 3.4 %collective-permute-done.13.refs_0_ = bf16[12,64,256]{2,1,0:T(8,128)(2,1)S(1)} collective-permute-done((bf16[12,64,256]{2,1,0:T(8,128)(2,1)S(1)}, bf16[12,64,256]{2,1,0:T(8,128)(2,1)S(1)}, u32[]{:S(2)}, u32[]{:S(2)}) %collective-permute-start.13) | collective-permute-done | bytes 393248 | tf_op jit(solution)/shard_map/ppermute | solution.py:81
  39.7 1.0 copy-done
  42.1 2.1 collective-permute-start.1
  44.3 16.2 %all_to_all.16 = s32[32,1,13]{2,1,0:T(1,128)S(1)} all-to-all(s32[32,1,13]{2,1,0:T(1,128)S(1)} %bitcast.46), channel_id=1, replica_groups=mesh['grp'=8,'dev'=32] {'dev'}, dimensions={0} | all-to-all | bytes 3328 | tf_op jit(solution)/shard_map/all_to_all | solution.py:77
  61.4 2.4 %collective-permute-start.5 = (bf16[6,64,256]{2,1,0:T(8,128)(2,1)S(1)}, bf16[6,64,256]{2,1,0:T(8,128)(2,1)S(1)}, u32[]{:S(2)}, u32[]{:S(2)}) collective-permute-start(bf16[6,64,256]{2,1,0:T(8,128)(2,1)S(1)} %get-tuple-element.31), channel_id=1, source_target_pairs={{0,2},{1,3},{2,0},{3,1},{4,6},{5,7},{6,4},{7,5},{8,10},{9,11},{10,... | collective-permute-start | bytes 589832 | tf_op jit(solution)/shard_map/ppermute | solution.py:66
  63.8 1.6 pick.7
  66.1 1.2 collective-permute-start.6
  68.8 2.4 %collective-permute-start.10 = (bf16[6,64,256]{2,1,0:T(8,128)(2,1)S(1)}, bf16[6,64,256]{2,1,0:T(8,128)(2,1)S(1)}, u32[]{:S(2)}, u32[]{:S(2)}) collective-permute-start(bf16[6,64,256]{2,1,0:T(8,128)(2,1)S(1)} %get-tuple-element.35), channel_id=1, source_target_pairs={{0,2},{1,3},{2,0},{3,1},{4,6},{5,7},{6,4},{7,5},{8,10},{9,11},{10,... | collective-permute-start | bytes 589832 | tf_op jit(solution)/shard_map/ppermute | solution.py:66
  71.2 1.7 pick.8
  73.1 1.9 collective-permute-done.6.refs_5_
  75.6 4.6 %collective-permute-start.15 = (bf16[6,64,256]{2,1,0:T(8,128)(2,1)}, bf16[6,64,256]{2,1,0:T(8,128)(2,1)S(1)}, u32[]{:S(2)}, u32[]{:S(2)}) collective-permute-start(bf16[6,64,256]{2,1,0:T(8,128)(2,1)} %get-tuple-element.39), channel_id=1, source_target_pairs={{0,2},{1,3},{2,0},{3,1},{4,6},{5,7},{6,4},{7,5},{8,10},{9,11},{10,... | collective-permute-start | bytes 589832 | tf_op jit(solution)/shard_map/ppermute | solution.py:66
  80.1 1.6 collective-permute-start.16
  81.8 1.5 collective-permute-start.17
  85.1 1.6 collective-permute-start.19
  86.7 2.5 %collective-permute-start.20 = (bf16[3,64,256]{2,1,0:T(8,128)(2,1)S(1)}, bf16[3,64,256]{2,1,0:T(8,128)(2,1)S(1)}, u32[]{:S(2)}, u32[]{:S(2)}) collective-permute-start(bf16[3,64,256]{2,1,0:T(8,128)(2,1)S(1)} %get-tuple-element.44), channel_id=1, source_target_pairs={{0,1},{1,2},{2,3},{3,0},{4,5},{5,6},{6,7},{7,4},{8,9},{9,10},{10,1... | collective-permute-start | bytes 294920 | tf_op jit(solution)/shard_map/ppermute | solution.py:66
  89.3 2.2 collective-permute-done.19.refs_16_
  92.4 1.5 collective-permute-done.21.refs_18_
  96.5 15.2 %device_tiles.1 = bf16[32,256,256]{2,1,0:T(8,128)(2,1)} custom-call(s32[12,27]{1,0:T(8,128)S(1)} %get-tuple-element.57.cols_ref, s32[12,27]{1,0:T(8,128)S(1)} %get-tuple-element.56.slots_ref, s32[16]{0:T(128)S(1)} %get-tuple-element.54.places_ref, s32[96]{0:T(128)S(1)} %fusion.3.where_ref, bf16[12,64,1728]{2,1,0:T(8,128)(2,1)} %bitcast.50, ...), custom_call_target="tpu_custom_call" | custom-call | flops 8000000000 | bytes 12000000 | tf_op jit(solution)/shard_map/device_tiles/pallas_call | solution.py:163
  111.8 5.6 %all-to-all-start.1 = ((bf16[32,256,256]{2,1,0:T(8,128)(2,1)}), bf16[32,256,256]{2,1,0:T(8,128)(2,1)}, u32[]{:S(2)}, u32[]{:S(2)}) async-start(bf16[32,256,256]{2,1,0:T(8,128)(2,1)} %device_tiles.1), calls=%async_computation.1 | async-start | bytes 8388608 | tf_op jit(solution)/shard_map/all_to_all | solution.py:277
  117.5 91.4 %all-to-all-done.1.got_hbm = bf16[32,256,256]{2,1,0:T(8,128)(2,1)} async-done(((bf16[32,256,256]{2,1,0:T(8,128)(2,1)}), bf16[32,256,256]{2,1,0:T(8,128)(2,1)}, u32[]{:S(2)}, u32[]{:S(2)}) %all-to-all-start.1) | async-done | bytes 4194336 | tf_op jit(solution)/shard_map/all_to_all | solution.py:277
  208.9 2.9 %table_of.1 = (f32[8,256,256]{2,1,0:T(8,128)S(1)}, bf16[8,256,256]{2,1,0:T(8,128)(2,1)S(1)}) custom-call(s32[32]{0:T(128)S(1)} %fusion.7.labels_ref, bf16[32,256,256]{2,1,0:T(8,128)(2,1)} %all-to-all-done.1.got_hbm), custom_call_target="tpu_custom_call" | custom-call | flops 2000000 | bytes 7000000 | tf_op jit(solution)/shard_map/table_of/pallas_call | solution.py:225
  211.9 2.6 %collective-permute-done.22 = bf16[8,256,256]{2,1,0:T(8,128)(2,1)S(1)} collective-permute-done((bf16[8,256,256]{2,1,0:T(8,128)(2,1)S(1)}, bf16[8,256,256]{2,1,0:T(8,128)(2,1)S(1)}, u32[]{:S(2)}, u32[]{:S(2)}) %collective-permute-start.22) | collective-permute-done | bytes 1048608 | tf_op jit(solution)/shard_map/ppermute | solution.py:254
  215.0 3.1 %collective-permute-start.23 = (bf16[2,256,256]{2,1,0:T(8,128)(2,1)S(1)}, bf16[2,256,256]{2,1,0:T(8,128)(2,1)S(1)}, u32[]{:S(2)}, u32[]{:S(2)}) collective-permute-start(bf16[2,256,256]{2,1,0:T(8,128)(2,1)S(1)} %get-tuple-element.51), channel_id=1, source_target_pairs={{0,128},{32,160},{64,192},{96,224},{128,0},{160,32},{192,64},{224,... | collective-permute-start | bytes 786440 | tf_op jit(solution)/shard_map/ppermute | solution.py:259
  218.1 1.2 collective-permute-start.25
  220.1 5.6 %collective-permute-done.23 = bf16[2,256,256]{2,1,0:T(8,128)(2,1)S(1)} collective-permute-done((bf16[2,256,256]{2,1,0:T(8,128)(2,1)S(1)}, bf16[2,256,256]{2,1,0:T(8,128)(2,1)S(1)}, u32[]{:S(2)}, u32[]{:S(2)}) %collective-permute-start.23) | collective-permute-done | bytes 262176 | tf_op jit(solution)/shard_map/ppermute | solution.py:259
  225.7 5.2 %collective-permute-done.25 = bf16[2,256,256]{2,1,0:T(8,128)(2,1)S(1)} collective-permute-done((bf16[2,256,256]{2,1,0:T(8,128)(2,1)S(1)}, bf16[2,256,256]{2,1,0:T(8,128)(2,1)S(1)}, u32[]{:S(2)}, u32[]{:S(2)}) %collective-permute-start.25) | collective-permute-done | bytes 262176 | tf_op jit(solution)/shard_map/ppermute | solution.py:259
  (68 shorter events, 15.1 us)
Async XLA Ops:
  0.0 14.5 %collective-permute-start.4 = (bf16[12,64,256]{2,1,0:T(8,128)(2,1)}, bf16[12,64,256]{2,1,0:T(8,128)(2,1)S(1)}, u32[]{:S(2)}, u32[]{:S(2)}) collective-permute-start(bf16[12,64,256]{2,1,0:T(8,128)(2,1)} %bitcast.37), channel_id=1, source_target_pairs={{0,28},{1,29},{2,30},{3,31},{4,0},{5,1},{6,2},{7,3},{8,4},{9,5},{1... | collective-permute-start | bytes 1179656 | tf_op jit(solution)/shard_map/ppermute | solution.py:76
  5.9 12.3 %collective-permute-start.3 = (bf16[12,64,256]{2,1,0:T(8,128)(2,1)}, bf16[12,64,256]{2,1,0:T(8,128)(2,1)S(1)}, u32[]{:S(2)}, u32[]{:S(2)}) collective-permute-start(bf16[12,64,256]{2,1,0:T(8,128)(2,1)} %bitcast.38), channel_id=1, source_target_pairs={{0,4},{1,5},{2,6},{3,7},{4,8},{5,9},{6,10},{7,11},{8,12},{9,13},{1... | collective-permute-start | bytes 1179656 | tf_op jit(solution)/shard_map/ppermute | solution.py:75
  14.5 11.1 %collective-permute-start.9 = (bf16[12,64,256]{2,1,0:T(8,128)(2,1)S(1)}, bf16[12,64,256]{2,1,0:T(8,128)(2,1)S(1)}, u32[]{:S(2)}, u32[]{:S(2)}) collective-permute-start(bf16[12,64,256]{2,1,0:T(8,128)(2,1)S(1)} %collective-permute-done.4.refs_1_), channel_id=1, source_target_pairs={{0,28},{1,29},{2,30},{3,31},{4,0},{5,1},{6,2},{7,3},{8,4},{9,5},{1... | collective-permute-start | bytes 1179656 | tf_op jit(solution)/shard_map/ppermute | solution.py:82
  18.1 11.2 %collective-permute-start.8 = (bf16[12,64,256]{2,1,0:T(8,128)(2,1)S(1)}, bf16[12,64,256]{2,1,0:T(8,128)(2,1)S(1)}, u32[]{:S(2)}, u32[]{:S(2)}) collective-permute-start(bf16[12,64,256]{2,1,0:T(8,128)(2,1)S(1)} %collective-permute-done.3.refs_0_), channel_id=1, source_target_pairs={{0,4},{1,5},{2,6},{3,7},{4,8},{5,9},{6,10},{7,11},{8,12},{9,13},{1... | collective-permute-start | bytes 1179656 | tf_op jit(solution)/shard_map/ppermute | solution.py:81
  25.7 10.4 %collective-permute-start.14 = (bf16[12,64,256]{2,1,0:T(8,128)(2,1)S(1)}, bf16[12,64,256]{2,1,0:T(8,128)(2,1)S(1)}, u32[]{:S(2)}, u32[]{:S(2)}) collective-permute-start(bf16[12,64,256]{2,1,0:T(8,128)(2,1)S(1)} %collective-permute-done.9.refs_1_), channel_id=1, source_target_pairs={{0,28},{1,29},{2,30},{3,31},{4,0},{5,1},{6,2},{7,3},{8,4},{9,5},{1... | collective-permute-start | bytes 1179656 | tf_op jit(solution)/shard_map/ppermute | solution.py:82
  29.3 10.1 %collective-permute-start.13 = (bf16[12,64,256]{2,1,0:T(8,128)(2,1)S(1)}, bf16[12,64,256]{2,1,0:T(8,128)(2,1)S(1)}, u32[]{:S(2)}, u32[]{:S(2)}) collective-permute-start(bf16[12,64,256]{2,1,0:T(8,128)(2,1)S(1)} %collective-permute-done.8.refs_0_), channel_id=1, source_target_pairs={{0,4},{1,5},{2,6},{3,7},{4,8},{5,9},{6,10},{7,11},{8,12},{9,13},{1... | collective-permute-start | bytes 1179656 | tf_op jit(solution)/shard_map/ppermute | solution.py:81
  29.4 54.0 %copy-start.9 = (s32[1,1,12,27]{3,1,2,0:T(1,128)S(1)}, s32[1,1,12,27]{3,1,2,0:T(1,128)}, u32[]{:S(2)}) copy-start(s32[1,1,12,27]{3,1,2,0:T(1,128)} %param.11) | copy-start | bytes 3892
  29.4 54.0 %copy-start.10 = (s32[1,1,12,27]{3,1,2,0:T(1,128)S(1)}, s32[1,1,12,27]{3,1,2,0:T(1,128)}, u32[]{:S(2)}) copy-start(s32[1,1,12,27]{3,1,2,0:T(1,128)} %param.9) | copy-start | bytes 3892
  31.1 52.2 %copy-start.1 = (bf16[1,1,12,64,256]{4,3,2,1,0:T(8,128)(2,1)S(1)}, bf16[1,1,12,64,256]{4,3,2,1,0:T(8,128)(2,1)}, u32[]{:S(2)}) copy-start(bf16[1,1,12,64,256]{4,3,2,1,0:T(8,128)(2,1)} %param.8) | copy-start | bytes 1179652
  39.5 42.3 %collective-permute-start.18 = (bf16[12,64,256]{2,1,0:T(8,128)(2,1)S(1)}, bf16[12,64,256]{2,1,0:T(8,128)(2,1)S(1)}, u32[]{:S(2)}, u32[]{:S(2)}) collective-permute-start(bf16[12,64,256]{2,1,0:T(8,128)(2,1)S(1)} %broadcast_select_fusion), channel_id=1, source_target_pairs={{0,4},{1,5},{2,6},{3,7},{4,8},{5,9},{6,10},{7,11},{8,12},{9,13},{1... | collective-permute-start | bytes 1179656 | tf_op jit(solution)/shard_map/ppermute | solution.py:91
  41.5 23.9 %collective-permute-start = (bf16[3,64,256]{2,1,0:T(8,128)(2,1)S(1)}, bf16[3,64,256]{2,1,0:T(8,128)(2,1)S(1)}, u32[]{:S(2)}, u32[]{:S(2)}) collective-permute-start(bf16[3,64,256]{2,1,0:T(8,128)(2,1)S(1)} %get-tuple-element.27), channel_id=1, source_target_pairs={{0,2},{1,3},{2,0},{3,1},{4,6},{5,7},{6,4},{7,5},{8,10},{9,11},{10,... | collective-permute-start | bytes 294920 | tf_op jit(solution)/shard_map/ppermute | solution.py:66
  42.1 25.2 %collective-permute-start.1 = (bf16[3,64,256]{2,1,0:T(8,128)(2,1)S(1)}, bf16[3,64,256]{2,1,0:T(8,128)(2,1)S(1)}, u32[]{:S(2)}, u32[]{:S(2)}) collective-permute-start(bf16[3,64,256]{2,1,0:T(8,128)(2,1)S(1)} %get-tuple-element.28), channel_id=1, source_target_pairs={{0,1},{1,2},{2,3},{3,0},{4,5},{5,6},{6,7},{7,4},{8,9},{9,10},{10,1... | collective-permute-start | bytes 294920 | tf_op jit(solution)/shard_map/ppermute | solution.py:66
  44.2 24.5 %collective-permute-start.2 = (bf16[3,64,256]{2,1,0:T(8,128)(2,1)S(1)}, bf16[3,64,256]{2,1,0:T(8,128)(2,1)S(1)}, u32[]{:S(2)}, u32[]{:S(2)}) collective-permute-start(bf16[3,64,256]{2,1,0:T(8,128)(2,1)S(1)} %get-tuple-element.29), channel_id=1, source_target_pairs={{0,3},{1,0},{2,1},{3,2},{4,7},{5,4},{6,5},{7,6},{8,11},{9,8},{10,9... | collective-permute-start | bytes 294920 | tf_op jit(solution)/shard_map/ppermute | solution.py:66
  61.4 11.5 %collective-permute-start.5 = (bf16[6,64,256]{2,1,0:T(8,128)(2,1)S(1)}, bf16[6,64,256]{2,1,0:T(8,128)(2,1)S(1)}, u32[]{:S(2)}, u32[]{:S(2)}) collective-permute-start(bf16[6,64,256]{2,1,0:T(8,128)(2,1)S(1)} %get-tuple-element.31), channel_id=1, source_target_pairs={{0,2},{1,3},{2,0},{3,1},{4,6},{5,7},{6,4},{7,5},{8,10},{9,11},{10,... | collective-permute-start | bytes 589832 | tf_op jit(solution)/shard_map/ppermute | solution.py:66
  66.1 9.0 %collective-permute-start.6 = (bf16[6,64,256]{2,1,0:T(8,128)(2,1)S(1)}, bf16[6,64,256]{2,1,0:T(8,128)(2,1)S(1)}, u32[]{:S(2)}, u32[]{:S(2)}) collective-permute-start(bf16[6,64,256]{2,1,0:T(8,128)(2,1)S(1)} %get-tuple-element.32), channel_id=1, source_target_pairs={{0,1},{1,2},{2,3},{3,0},{4,5},{5,6},{6,7},{7,4},{8,9},{9,10},{10,1... | collective-permute-start | bytes 589832 | tf_op jit(solution)/shard_map/ppermute | solution.py:66
  67.9 7.6 %collective-permute-start.7 = (bf16[6,64,256]{2,1,0:T(8,128)(2,1)S(1)}, bf16[6,64,256]{2,1,0:T(8,128)(2,1)S(1)}, u32[]{:S(2)}, u32[]{:S(2)}) collective-permute-start(bf16[6,64,256]{2,1,0:T(8,128)(2,1)S(1)} %get-tuple-element.33), channel_id=1, source_target_pairs={{0,3},{1,0},{2,1},{3,2},{4,7},{5,4},{6,5},{7,6},{8,11},{9,8},{10,9... | collective-permute-start | bytes 589832 | tf_op jit(solution)/shard_map/ppermute | solution.py:66
  68.8 13.0 %copy-start.7 = (bf16[3,64,256]{2,1,0:T(8,128)(2,1)}, bf16[3,64,256]{2,1,0:T(8,128)(2,1)S(1)}, u32[]{:S(2)}) copy-start(bf16[3,64,256]{2,1,0:T(8,128)(2,1)S(1)} %collective-permute-done.2.refs_2_) | copy-start | bytes 294916
  68.8 11.4 %collective-permute-start.10 = (bf16[6,64,256]{2,1,0:T(8,128)(2,1)S(1)}, bf16[6,64,256]{2,1,0:T(8,128)(2,1)S(1)}, u32[]{:S(2)}, u32[]{:S(2)}) collective-permute-start(bf16[6,64,256]{2,1,0:T(8,128)(2,1)S(1)} %get-tuple-element.35), channel_id=1, source_target_pairs={{0,2},{1,3},{2,0},{3,1},{4,6},{5,7},{6,4},{7,5},{8,10},{9,11},{10,... | collective-permute-start | bytes 589832 | tf_op jit(solution)/shard_map/ppermute | solution.py:66
  72.9 21.0 %copy-start.2 = (bf16[6,64,256]{2,1,0:T(8,128)(2,1)}, bf16[6,64,256]{2,1,0:T(8,128)(2,1)S(1)}, u32[]{:S(2)}) copy-start(bf16[6,64,256]{2,1,0:T(8,128)(2,1)S(1)} %get-tuple-element.42.refs_15_) | copy-start | bytes 589828
  72.9 12.2 %collective-permute-start.11 = (bf16[6,64,256]{2,1,0:T(8,128)(2,1)}, bf16[6,64,256]{2,1,0:T(8,128)(2,1)S(1)}, u32[]{:S(2)}, u32[]{:S(2)}) collective-permute-start(bf16[6,64,256]{2,1,0:T(8,128)(2,1)} %get-tuple-element.36), channel_id=1, source_target_pairs={{0,1},{1,2},{2,3},{3,0},{4,5},{5,6},{6,7},{7,4},{8,9},{9,10},{10,1... | collective-permute-start | bytes 589832 | tf_op jit(solution)/shard_map/ppermute | solution.py:66
  75.1 11.6 %collective-permute-start.12 = (bf16[6,64,256]{2,1,0:T(8,128)(2,1)}, bf16[6,64,256]{2,1,0:T(8,128)(2,1)S(1)}, u32[]{:S(2)}, u32[]{:S(2)}) collective-permute-start(bf16[6,64,256]{2,1,0:T(8,128)(2,1)} %get-tuple-element.37), channel_id=1, source_target_pairs={{0,3},{1,0},{2,1},{3,2},{4,7},{5,4},{6,5},{7,6},{8,11},{9,8},{10,9... | collective-permute-start | bytes 589832 | tf_op jit(solution)/shard_map/ppermute | solution.py:66
  75.6 13.7 %collective-permute-start.15 = (bf16[6,64,256]{2,1,0:T(8,128)(2,1)}, bf16[6,64,256]{2,1,0:T(8,128)(2,1)S(1)}, u32[]{:S(2)}, u32[]{:S(2)}) collective-permute-start(bf16[6,64,256]{2,1,0:T(8,128)(2,1)} %get-tuple-element.39), channel_id=1, source_target_pairs={{0,2},{1,3},{2,0},{3,1},{4,6},{5,7},{6,4},{7,5},{8,10},{9,11},{10,... | collective-permute-start | bytes 589832 | tf_op jit(solution)/shard_map/ppermute | solution.py:66
  80.1 9.1 %collective-permute-start.16 = (bf16[6,64,256]{2,1,0:T(8,128)(2,1)}, bf16[6,64,256]{2,1,0:T(8,128)(2,1)S(1)}, u32[]{:S(2)}, u32[]{:S(2)}) collective-permute-start(bf16[6,64,256]{2,1,0:T(8,128)(2,1)} %get-tuple-element.40), channel_id=1, source_target_pairs={{0,1},{1,2},{2,3},{3,0},{4,5},{5,6},{6,7},{7,4},{8,9},{9,10},{10,1... | collective-permute-start | bytes 589832 | tf_op jit(solution)/shard_map/ppermute | solution.py:66
  81.8 7.5 %collective-permute-start.17 = (bf16[6,64,256]{2,1,0:T(8,128)(2,1)}, bf16[6,64,256]{2,1,0:T(8,128)(2,1)S(1)}, u32[]{:S(2)}, u32[]{:S(2)}) collective-permute-start(bf16[6,64,256]{2,1,0:T(8,128)(2,1)} %get-tuple-element.41), channel_id=1, source_target_pairs={{0,3},{1,0},{2,1},{3,2},{4,7},{5,4},{6,5},{7,6},{8,11},{9,8},{10,9... | collective-permute-start | bytes 589832 | tf_op jit(solution)/shard_map/ppermute | solution.py:66
  85.1 6.3 %collective-permute-start.19 = (bf16[3,64,256]{2,1,0:T(8,128)(2,1)S(1)}, bf16[3,64,256]{2,1,0:T(8,128)(2,1)S(1)}, u32[]{:S(2)}, u32[]{:S(2)}) collective-permute-start(bf16[3,64,256]{2,1,0:T(8,128)(2,1)S(1)} %get-tuple-element.43), channel_id=1, source_target_pairs={{0,2},{1,3},{2,0},{3,1},{4,6},{5,7},{6,4},{7,5},{8,10},{9,11},{10,... | collective-permute-start | bytes 294920 | tf_op jit(solution)/shard_map/ppermute | solution.py:66
  86.7 5.7 %collective-permute-start.20 = (bf16[3,64,256]{2,1,0:T(8,128)(2,1)S(1)}, bf16[3,64,256]{2,1,0:T(8,128)(2,1)S(1)}, u32[]{:S(2)}, u32[]{:S(2)}) collective-permute-start(bf16[3,64,256]{2,1,0:T(8,128)(2,1)S(1)} %get-tuple-element.44), channel_id=1, source_target_pairs={{0,1},{1,2},{2,3},{3,0},{4,5},{5,6},{6,7},{7,4},{8,9},{9,10},{10,1... | collective-permute-start | bytes 294920 | tf_op jit(solution)/shard_map/ppermute | solution.py:66
  89.2 4.6 %collective-permute-start.21 = (bf16[3,64,256]{2,1,0:T(8,128)(2,1)S(1)}, bf16[3,64,256]{2,1,0:T(8,128)(2,1)S(1)}, u32[]{:S(2)}, u32[]{:S(2)}) collective-permute-start(bf16[3,64,256]{2,1,0:T(8,128)(2,1)S(1)} %get-tuple-element.45), channel_id=1, source_target_pairs={{0,3},{1,0},{2,1},{3,2},{4,7},{5,4},{6,5},{7,6},{8,11},{9,8},{10,9... | collective-permute-start | bytes 294920 | tf_op jit(solution)/shard_map/ppermute | solution.py:66
  111.8 97.2 %all-to-all-start.1 = ((bf16[32,256,256]{2,1,0:T(8,128)(2,1)}), bf16[32,256,256]{2,1,0:T(8,128)(2,1)}, u32[]{:S(2)}, u32[]{:S(2)}) async-start(bf16[32,256,256]{2,1,0:T(8,128)(2,1)} %device_tiles.1), calls=%async_computation.1 | async-start | bytes 8388608 | tf_op jit(solution)/shard_map/all_to_all | solution.py:277
  211.8 2.7 %collective-permute-start.22 = (bf16[8,256,256]{2,1,0:T(8,128)(2,1)S(1)}, bf16[8,256,256]{2,1,0:T(8,128)(2,1)S(1)}, u32[]{:S(2)}, u32[]{:S(2)}) collective-permute-start(bf16[8,256,256]{2,1,0:T(8,128)(2,1)S(1)} %get-tuple-element.48), channel_id=1, source_target_pairs={{0,32},{32,0},{64,96},{96,64},{128,160},{160,128},{192,224},{224,1... | collective-permute-start | bytes 3145736 | tf_op jit(solution)/shard_map/ppermute | solution.py:254
  215.0 10.8 %collective-permute-start.23 = (bf16[2,256,256]{2,1,0:T(8,128)(2,1)S(1)}, bf16[2,256,256]{2,1,0:T(8,128)(2,1)S(1)}, u32[]{:S(2)}, u32[]{:S(2)}) collective-permute-start(bf16[2,256,256]{2,1,0:T(8,128)(2,1)S(1)} %get-tuple-element.51), channel_id=1, source_target_pairs={{0,128},{32,160},{64,192},{96,224},{128,0},{160,32},{192,64},{224,... | collective-permute-start | bytes 786440 | tf_op jit(solution)/shard_map/ppermute | solution.py:259
  218.1 12.8 %collective-permute-start.25 = (bf16[2,256,256]{2,1,0:T(8,128)(2,1)S(1)}, bf16[2,256,256]{2,1,0:T(8,128)(2,1)S(1)}, u32[]{:S(2)}, u32[]{:S(2)}) collective-permute-start(bf16[2,256,256]{2,1,0:T(8,128)(2,1)S(1)} %get-tuple-element.52), channel_id=1, source_target_pairs={{0,192},{32,224},{64,0},{96,32},{128,64},{160,96},{192,128},{224,1... | collective-permute-start | bytes 786440 | tf_op jit(solution)/shard_map/ppermute | solution.py:259
  219.2 11.7 %collective-permute-start.24 = (bf16[2,256,256]{2,1,0:T(8,128)(2,1)S(1)}, bf16[2,256,256]{2,1,0:T(8,128)(2,1)S(1)}, u32[]{:S(2)}, u32[]{:S(2)}) collective-permute-start(bf16[2,256,256]{2,1,0:T(8,128)(2,1)S(1)} %get-tuple-element.53), channel_id=1, source_target_pairs={{0,64},{32,96},{64,128},{96,160},{128,192},{160,224},{192,0},{224,... | collective-permute-start | bytes 786440 | tf_op jit(solution)/shard_map/ppermute | solution.py:259
  (6 other events, 5.0 us)
